TPU v7x, 256 devices: a whole 4x4x8 slice. The times are simulated.
256 devices in a mesh: lat: 8 (over y, x_hi), lon: 32 (over z, x_lo, core).
Axes of the slice: x: 4 (x_hi: 2, x_lo: 2; x = x_hi * 2 + x_lo), y: 4, z: 8, core: 2. Of those that a mesh axis runs over, the one named last changes fastest.
Arguments:
- hi_res: bfloat16 [384, 768, 256], P('lat', 'lon'), may hold values from -6 to 6
- low_res: bfloat16 [128, 256, 256], P('lat', 'lon'), may hold values from -6 to 6
- kernel_high: bfloat16 [3, 3, 256, 256], replicated, may hold values from -0.125 to 0.125
- kernel_low: bfloat16 [3, 3, 256, 256], replicated, may hold values from -0.125 to 0.125
- kernel_join: bfloat16 [3, 3, 256, 256], replicated, may hold values from -0.125 to 0.125
- target: bfloat16 [384, 768, 256], P('lat', 'lon'), may hold values from -6 to 6
- land_count: int32 [8, 32], P('lat', 'lon'), may hold values from 144 to 1152
Outputs:
- grad_high: float32 [2304, 256], P('lon', 'lat')
- grad_low: float32 [2304, 256], P('lon', 'lat')
- grad_join: float32 [2304, 256], P('lon', 'lat')
All inputs are finite; a program needn't handle non-finite values.
Results may differ from a plain program's by a relative error of at most 0.003.
Values may be sent and summed in bfloat16 or wider, within the bound.
No kernel may reach another device: no remote copies, remote signals or barrier semaphores. Data moves between devices by JAX's collectives and lax.ppermute only.
A program may use at most 64 MiB of HBM per device.

v0:
```python
import jax
import jax.numpy as jnp
from jax import lax
from jax.sharding import PartitionSpec as P

ONE_THIRD = 1.0 / 3.0
TWO_THIRDS = 2.0 / 3.0


def padded_2(cells, sides, width):
    for axis, dim in sides:
        count = lax.axis_size(axis)
        head = lax.slice_in_dim(cells, 0, width, axis=dim)
        tail = lax.slice_in_dim(cells, cells.shape[dim] - width, cells.shape[dim], axis=dim)
        cells = jnp.concatenate(
            [
                lax.ppermute(tail, axis, [(i, (i + 1) % count) for i in range(count)]),
                cells,
                lax.ppermute(head, axis, [((i + 1) % count, i) for i in range(count)]),
            ],
            axis=dim,
        )
    return cells


def conv_valid(padded, kernel):
    row_count = padded.shape[0] - 2
    col_count = padded.shape[1] - 2
    channels = padded.shape[2]
    running = jnp.zeros((row_count * col_count, kernel.shape[3]), jnp.float32)
    for offset_row in range(3):
        for offset_col in range(3):
            window = padded[
                offset_row : offset_row + row_count, offset_col : offset_col + col_count
            ].reshape(row_count * col_count, channels)
            running = running + jnp.dot(
                window, kernel[offset_row, offset_col], preferred_element_type=jnp.float32
            )
    return running.reshape(row_count, col_count, kernel.shape[3])


def conv_back(padded, kernel):
    row_count = padded.shape[0] - 2
    col_count = padded.shape[1] - 2
    channels = padded.shape[2]
    running = jnp.zeros((row_count * col_count, kernel.shape[2]), jnp.float32)
    for offset_row in range(3):
        for offset_col in range(3):
            window = padded[
                2 - offset_row : 2 - offset_row + row_count,
                2 - offset_col : 2 - offset_col + col_count,
            ].reshape(row_count * col_count, channels)
            running = running + lax.dot_general(
                window,
                kernel[offset_row, offset_col],
                (((1,), (1,)), ((), ())),
                preferred_element_type=jnp.float32,
            )
    return running.reshape(row_count, col_count, kernel.shape[2])


def kernel_grad(padded, gradient):
    row_count, col_count, out_count = gradient.shape
    flat_grad = gradient.reshape(row_count * col_count, out_count)
    pieces = []
    for offset_row in range(3):
        for offset_col in range(3):
            window = padded[
                offset_row : offset_row + row_count, offset_col : offset_col + col_count
            ].reshape(row_count * col_count, padded.shape[2])
            pieces.append(
                lax.dot_general(
                    window, flat_grad, (((0,), (0,)), ((), ())), preferred_element_type=jnp.float32
                )
            )
    return jnp.concatenate(pieces, axis=0)


def up_rows(values):
    before = values[:-2]
    centre = values[1:-1]
    latter = values[2:]
    leading = ONE_THIRD * before + TWO_THIRDS * centre
    trailing = TWO_THIRDS * centre + ONE_THIRD * latter
    return jnp.stack([leading, centre, trailing], axis=1).reshape(
        3 * centre.shape[0], values.shape[1], values.shape[2]
    )


def up_cols(values):
    before = values[:, :-2]
    centre = values[:, 1:-1]
    latter = values[:, 2:]
    leading = ONE_THIRD * before + TWO_THIRDS * centre
    trailing = TWO_THIRDS * centre + ONE_THIRD * latter
    return jnp.stack([leading, centre, trailing], axis=2).reshape(
        values.shape[0], 3 * centre.shape[1], values.shape[2]
    )


def down_rows(values):
    cell_count = (values.shape[0] - 2) // 3
    triple = values[1:-1].reshape(cell_count, 3, values.shape[1], values.shape[2])
    middle = TWO_THIRDS * triple[:, 0] + triple[:, 1] + TWO_THIRDS * triple[:, 2]
    return middle + ONE_THIRD * (
        values[0 : 3 * cell_count : 3] + values[4 : 3 * cell_count + 4 : 3]
    )


def down_cols(values):
    cell_count = (values.shape[1] - 2) // 3
    triple = values[:, 1:-1].reshape(values.shape[0], cell_count, 3, values.shape[2])
    middle = TWO_THIRDS * triple[:, :, 0] + triple[:, :, 1] + TWO_THIRDS * triple[:, :, 2]
    return middle + ONE_THIRD * (
        values[:, 0 : 3 * cell_count : 3] + values[:, 4 : 3 * cell_count + 4 : 3]
    )


def pole_zero(values, margin):
    position = lax.axis_index("lat")
    last_index = lax.axis_size("lat") - 1
    row_ids = lax.broadcasted_iota(jnp.int32, (values.shape[0], 1, 1), 0)
    outside = (row_ids < margin) & (position == 0) | (row_ids >= values.shape[0] - margin) & (
        position == last_index
    )
    return jnp.where(outside, jnp.zeros_like(values), values)


def body(hi_res, low_res, kernel_high, kernel_low, kernel_join, target, land_count):
    row_count = hi_res.shape[0]
    col_count = hi_res.shape[1]
    low_rows = low_res.shape[0]
    low_cols = low_res.shape[1]
    depth = 1
    high_wide = pole_zero(padded_2(hi_res, (("lat", 0), ("lon", 1)), depth), depth)
    low_wide = pole_zero(padded_2(low_res, (("lat", 0), ("lon", 1)), depth + 1), depth + 1)
    high_act_wide = jnp.maximum(conv_valid(high_wide, kernel_high), 0.0).astype(jnp.bfloat16)
    low_act_wide = pole_zero(jnp.maximum(conv_valid(low_wide, kernel_low), 0.0), depth).astype(
        jnp.bfloat16
    )
    lifted_all = up_cols(up_rows(low_act_wide.astype(jnp.float32)))
    joined_wide = (high_act_wide.astype(jnp.float32) + lifted_all).astype(jnp.bfloat16)
    joined_pad = pole_zero(padded_2(joined_wide, (("lat", 0), ("lon", 1)), 1), 1)
    low_act = low_act_wide[depth : depth + low_rows, depth : depth + low_cols]
    low_pad = low_wide[depth : depth + low_rows + 2, depth : depth + low_cols + 2]
    output = conv_valid(joined_pad, kernel_join)
    scale = 2.0 / (row_count * col_count * row_count * col_count)
    weight_here = land_count[0, 0].astype(jnp.float32) * scale
    out_grad = (weight_here * (output - target.astype(jnp.float32))).astype(jnp.bfloat16)
    grad_wide = pole_zero(padded_2(out_grad, (("lat", 0), ("lon", 1)), 2), 2)
    grad_join = kernel_grad(joined_pad, out_grad)
    joined_grad_wide = pole_zero(conv_back(grad_wide, kernel_join), 1).astype(jnp.bfloat16)
    joined_grad = joined_grad_wide[1 : 1 + row_count, 1 : 1 + col_count]
    high_grad = jnp.where(high_act_wide > 0, joined_grad, jnp.zeros_like(joined_grad))
    grad_high = kernel_grad(high_wide, high_grad)
    lifted_grad = down_cols(down_rows(joined_grad_wide.astype(jnp.float32)))
    low_grad = jnp.where(low_act > 0, lifted_grad, jnp.zeros_like(lifted_grad)).astype(jnp.bfloat16)
    grad_low = kernel_grad(low_pad, low_grad)
    summed = lax.psum((grad_high, grad_low, grad_join), ("lat", "lon"))
    row_part = grad_high.shape[0] // lax.axis_size("lon")
    col_part = grad_high.shape[1] // lax.axis_size("lat")
    row_start = lax.axis_index("lon") * row_part
    col_start = lax.axis_index("lat") * col_part
    results = tuple(
        (
            lax.dynamic_slice(member, (row_start, col_start), (row_part, col_part))
            for member in summed
        )
    )
    return (results[0], results[1], results[2])


def solution(mesh):
    in_specs = (
        P("lat", "lon", None),
        P("lat", "lon", None),
        P(),
        P(),
        P(),
        P("lat", "lon", None),
        P("lat", "lon"),
    )
    out_specs = (P("lon", "lat"), P("lon", "lat"), P("lon", "lat"))
    return jax.shard_map(body, mesh=mesh, in_specs=in_specs, out_specs=out_specs, check_vma=False)
```

profile of v0, /device:TPU:8, one launch (start us, length us, event | category | flops | bytes accessed | tf_op | source)
XLA Modules:
  0.0 416.6 jit_solution(7609639112995314114)
XLA Ops:
  7.2 0.9 copy.46
  8.1 3.1 collective-permute-start.4
  11.2 1.4 collective-permute-start.5
  12.6 1.2 copy.34
  13.8 2.2 collective-permute-start
  16.0 2.3 collective-permute-start.1
  18.5 5.2 %collective-permute-start.7 = (bf16[20,2,256]{2,0,1:T(8,128)(2,1)S(1)}, bf16[20,2,256]{2,0,1:T(8,128)(2,1)S(1)}, u32[]{:S(2)}, u32[]{:S(2)}) collective-permute-start(bf16[20,2,256]{2,0,1:T(8,128)(2,1)S(1)} %get-tuple-element.72), channel_id=1, source_target_pairs={{1,0},{2,1},{3,2},{4,3},{5,4},{6,5},{7,6},{8,7},{9,8},{10,9},{11,1... | collective-permute-start | bytes 61448 | tf_op jit(solution)/shard_map/ppermute | solution.py:19
  23.8 4.3 %collective-permute-start.3 = (bf16[50,1,256]{2,0,1:T(8,128)(2,1)S(1)}, bf16[50,1,256]{2,0,1:T(8,128)(2,1)S(1)}, u32[]{:S(2)}, u32[]{:S(2)}) collective-permute-start(bf16[50,1,256]{2,0,1:T(8,128)(2,1)S(1)} %get-tuple-element.49), channel_id=1, source_target_pairs={{1,0},{2,1},{3,2},{4,3},{5,4},{6,5},{7,6},{8,7},{9,8},{10,9},{11,1... | collective-permute-start | bytes 76808 | tf_op jit(solution)/shard_map/ppermute | solution.py:19
  29.0 0.9 copy-done.11
  32.8 0.5 maximum_select_fusion.1
  33.4 0.5 fusion.169
  35.6 0.9 copy-done.12
  40.0 2.2 collective-permute-start.8
  42.2 2.3 collective-permute-start.9
  44.5 1.8 collective-permute-done.8
  46.3 1.2 collective-permute-done.9
  47.6 4.0 collective-permute-start.11
  52.3 0.7 collective-permute-done.10
  53.2 0.5 maximum_select_fusion.2
  55.9 0.9 copy-done
  59.7 0.7 copy-done.13
  61.0 3.4 collective-permute-start.12
  64.4 1.1 collective-permute-start.13
  68.6 1.2 collective-permute-done.13
  69.9 3.8 collective-permute-start.15
  74.2 1.4 collective-permute-done.14
  76.0 3.4 fusion.167
  79.4 2.3 reshape.286
  81.7 2.1 reshape.285
  83.8 2.1 reshape.284
  86.0 2.0 reshape.283
  88.0 2.1 reshape.282
  90.0 2.1 reshape.281
  92.1 2.1 reshape.280
  94.2 2.0 reshape.279
  96.2 1.0 reshape.278
  97.3 1.5 fusion.68
  99.2 0.7 copy-done.7
  100.3 0.7 copy-done.6
  101.4 0.7 copy-done.5
  102.5 0.7 copy-done.4
  103.6 0.7 copy-done.3
  104.7 0.7 copy-done.2
  105.8 0.7 copy-done.1
  107.5 0.6 slice.453
  108.0 0.8 slice.454
  109.3 0.8 copy.73
  110.3 0.9 fusion.34
  113.2 1.4 fusion.30
  114.7 1.1 fusion.29
  115.8 1.1 fusion.28
  116.9 1.1 fusion.27
  118.0 1.1 fusion.26
  119.1 1.1 fusion.25
  120.2 1.1 fusion.24
  121.3 1.1 fusion.23
  122.4 1.1 fusion.22
  123.5 281.4 %all-reduce.3.cloned.1.call-done = (f32[2304,256]{1,0:T(8,128)}, f32[2304,256]{1,0:T(8,128)}, f32[2304,256]{1,0:T(8,128)}) async-done(((f32[2304,256]{1,0:T(8,128)}, f32[2304,256]{1,0:T(8,128)}, f32[2304,256]{1,0:T(8,128)}), (f32[2304,256]{1,0:T(8,128)}, f32[2304,256]{1,0:T(8,128)}, f32[2304,256]{1,0:T(8,128)})) %all-reduce.3.cloned.1.call-update) | async-done | bytes 7077904 | tf_op jit(solution)/shard_map/psum | solution.py:159
  405.0 0.8 dynamic_slice.9
  405.8 0.7 copy.89
  406.5 0.8 dynamic_slice.10
  407.3 0.8 dynamic_slice.11
  408.2 0.7 copy.91
  408.9 0.7 copy.90
  (158 shorter events, 25.2 us)
Async XLA Ops:
  7.2 397.8 %all-reduce.3.cloned.1.call-start = ((), (), s32[]{:S(2)}) async-start(), calls=%async_computation | async-start | bytes 14155776 | tf_op jit(solution)/shard_map/psum | solution.py:159
  8.1 10.3 %collective-permute-start.4 = (bf16[2,8,256]{2,0,1:T(2,128)(2,1)S(1)}, bf16[2,8,256]{2,0,1:T(2,128)(2,1)S(1)}, u32[]{:S(2)}, u32[]{:S(2)}) collective-permute-start(bf16[2,8,256]{2,0,1:T(2,128)(2,1)S(1)} %get-tuple-element.73), channel_id=1, source_target_pairs={{0,32},{32,64},{64,96},{96,128},{128,160},{160,192},{192,224},{224... | collective-permute-start | bytes 24584 | tf_op jit(solution)/shard_map/ppermute | solution.py:17
  11.2 7.2 %collective-permute-start.5 = (bf16[2,8,256]{2,0,1:T(2,128)(2,1)S(1)}, bf16[2,8,256]{2,0,1:T(2,128)(2,1)S(1)}, u32[]{:S(2)}, u32[]{:S(2)}) collective-permute-start(bf16[2,8,256]{2,0,1:T(2,128)(2,1)S(1)} %get-tuple-element.74), channel_id=1, source_target_pairs={{32,0},{64,32},{96,64},{128,96},{160,128},{192,160},{224,192},{0,2... | collective-permute-start | bytes 24584 | tf_op jit(solution)/shard_map/ppermute | solution.py:19
  13.8 9.9 %collective-permute-start = (bf16[1,24,256]{2,0,1:T(2,128)(2,1)S(1)}, bf16[1,24,256]{2,0,1:T(2,128)(2,1)S(1)}, u32[]{:S(2)}, u32[]{:S(2)}) collective-permute-start(bf16[1,24,256]{2,0,1:T(2,128)(2,1)S(1)} %get-tuple-element.54), channel_id=1, source_target_pairs={{0,32},{32,64},{64,96},{96,128},{128,160},{160,192},{192,224},{224... | collective-permute-start | bytes 36872 | tf_op jit(solution)/shard_map/ppermute | solution.py:17
  16.0 7.7 %collective-permute-start.1 = (bf16[1,24,256]{2,0,1:T(2,128)(2,1)S(1)}, bf16[1,24,256]{2,0,1:T(2,128)(2,1)S(1)}, u32[]{:S(2)}, u32[]{:S(2)}) collective-permute-start(bf16[1,24,256]{2,0,1:T(2,128)(2,1)S(1)} %get-tuple-element.55), channel_id=1, source_target_pairs={{32,0},{64,32},{96,64},{128,96},{160,128},{192,160},{224,192},{0,2... | collective-permute-start | bytes 36872 | tf_op jit(solution)/shard_map/ppermute | solution.py:19
  18.4 9.7 %collective-permute-start.6 = (bf16[20,2,256]{2,0,1:T(8,128)(2,1)S(1)}, bf16[20,2,256]{2,0,1:T(8,128)(2,1)S(1)}, u32[]{:S(2)}, u32[]{:S(2)}) collective-permute-start(bf16[20,2,256]{2,0,1:T(8,128)(2,1)S(1)} %get-tuple-element.71), channel_id=1, source_target_pairs={{0,1},{1,2},{2,3},{3,4},{4,5},{5,6},{6,7},{7,8},{8,9},{9,10},{10,1... | collective-permute-start | bytes 61448 | tf_op jit(solution)/shard_map/ppermute | solution.py:17
  18.5 9.6 %collective-permute-start.7 = (bf16[20,2,256]{2,0,1:T(8,128)(2,1)S(1)}, bf16[20,2,256]{2,0,1:T(8,128)(2,1)S(1)}, u32[]{:S(2)}, u32[]{:S(2)}) collective-permute-start(bf16[20,2,256]{2,0,1:T(8,128)(2,1)S(1)} %get-tuple-element.72), channel_id=1, source_target_pairs={{1,0},{2,1},{3,2},{4,3},{5,4},{6,5},{7,6},{8,7},{9,8},{10,9},{11,1... | collective-permute-start | bytes 61448 | tf_op jit(solution)/shard_map/ppermute | solution.py:19
  23.7 9.1 %collective-permute-start.2 = (bf16[50,1,256]{2,0,1:T(8,128)(2,1)S(1)}, bf16[50,1,256]{2,0,1:T(8,128)(2,1)S(1)}, u32[]{:S(2)}, u32[]{:S(2)}) collective-permute-start(bf16[50,1,256]{2,0,1:T(8,128)(2,1)S(1)} %get-tuple-element.48), channel_id=1, source_target_pairs={{0,1},{1,2},{2,3},{3,4},{4,5},{5,6},{6,7},{7,8},{8,9},{9,10},{10,1... | collective-permute-start | bytes 76808 | tf_op jit(solution)/shard_map/ppermute | solution.py:17
  23.8 9.0 %collective-permute-start.3 = (bf16[50,1,256]{2,0,1:T(8,128)(2,1)S(1)}, bf16[50,1,256]{2,0,1:T(8,128)(2,1)S(1)}, u32[]{:S(2)}, u32[]{:S(2)}) collective-permute-start(bf16[50,1,256]{2,0,1:T(8,128)(2,1)S(1)} %get-tuple-element.49), channel_id=1, source_target_pairs={{1,0},{2,1},{3,2},{4,3},{5,4},{6,5},{7,6},{8,7},{9,8},{10,9},{11,1... | collective-permute-start | bytes 76808 | tf_op jit(solution)/shard_map/ppermute | solution.py:19
  28.6 1.3 copy-start.11
  35.2 1.3 copy-start.12
  40.0 6.3 %collective-permute-start.8 = (bf16[1,24,256]{2,0,1:T(2,128)(2,1)S(1)}, bf16[1,24,256]{2,0,1:T(2,128)(2,1)S(1)}, u32[]{:S(2)}, u32[]{:S(2)}) collective-permute-start(bf16[1,24,256]{2,0,1:T(2,128)(2,1)S(1)} %get-tuple-element.52), channel_id=1, source_target_pairs={{0,32},{32,64},{64,96},{96,128},{128,160},{160,192},{192,224},{224... | collective-permute-start | bytes 36872 | tf_op jit(solution)/shard_map/ppermute | solution.py:17
  42.2 5.3 %collective-permute-start.9 = (bf16[1,24,256]{2,0,1:T(2,128)(2,1)S(1)}, bf16[1,24,256]{2,0,1:T(2,128)(2,1)S(1)}, u32[]{:S(2)}, u32[]{:S(2)}) collective-permute-start(bf16[1,24,256]{2,0,1:T(2,128)(2,1)S(1)} %get-tuple-element.53), channel_id=1, source_target_pairs={{32,0},{64,32},{96,64},{128,96},{160,128},{192,160},{224,192},{0,2... | collective-permute-start | bytes 36872 | tf_op jit(solution)/shard_map/ppermute | solution.py:19
  47.5 5.5 %collective-permute-start.10 = (bf16[50,1,256]{2,0,1:T(8,128)(2,1)S(1)}, bf16[50,1,256]{2,0,1:T(8,128)(2,1)S(1)}, u32[]{:S(2)}, u32[]{:S(2)}) collective-permute-start(bf16[50,1,256]{2,0,1:T(8,128)(2,1)S(1)} %get-tuple-element.46), channel_id=1, source_target_pairs={{0,1},{1,2},{2,3},{3,4},{4,5},{5,6},{6,7},{7,8},{8,9},{9,10},{10,1... | collective-permute-start | bytes 76808 | tf_op jit(solution)/shard_map/ppermute | solution.py:17
  47.6 5.6 %collective-permute-start.11 = (bf16[50,1,256]{2,0,1:T(8,128)(2,1)S(1)}, bf16[50,1,256]{2,0,1:T(8,128)(2,1)S(1)}, u32[]{:S(2)}, u32[]{:S(2)}) collective-permute-start(bf16[50,1,256]{2,0,1:T(8,128)(2,1)S(1)} %get-tuple-element.47), channel_id=1, source_target_pairs={{1,0},{2,1},{3,2},{4,3},{5,4},{6,5},{7,6},{8,7},{9,8},{10,9},{11,1... | collective-permute-start | bytes 76808 | tf_op jit(solution)/shard_map/ppermute | solution.py:19
  55.5 1.3 copy-start
  59.4 1.1 copy-start.13
  61.0 7.5 %collective-permute-start.12 = (bf16[2,24,256]{2,1,0:T(8,128)(2,1)S(1)}, bf16[2,24,256]{2,1,0:T(8,128)(2,1)S(1)}, u32[]{:S(2)}, u32[]{:S(2)}) collective-permute-start(bf16[2,24,256]{2,1,0:T(8,128)(2,1)S(1)} %get-tuple-element.50), channel_id=1, source_target_pairs={{0,32},{32,64},{64,96},{96,128},{128,160},{160,192},{192,224},{224... | collective-permute-start | bytes 73736 | tf_op jit(solution)/shard_map/ppermute | solution.py:17
  64.4 5.3 %collective-permute-start.13 = (bf16[2,24,256]{2,1,0:T(8,128)(2,1)S(1)}, bf16[2,24,256]{2,1,0:T(8,128)(2,1)S(1)}, u32[]{:S(2)}, u32[]{:S(2)}) collective-permute-start(bf16[2,24,256]{2,1,0:T(8,128)(2,1)S(1)} %get-tuple-element.51), channel_id=1, source_target_pairs={{32,0},{64,32},{96,64},{128,96},{160,128},{192,160},{224,192},{0,2... | collective-permute-start | bytes 73736 | tf_op jit(solution)/shard_map/ppermute | solution.py:19
  69.8 5.7 %collective-permute-start.14 = (bf16[52,2,256]{2,1,0:T(2,128)(2,1)S(1)}, bf16[52,2,256]{2,1,0:T(2,128)(2,1)S(1)}, u32[]{:S(2)}, u32[]{:S(2)}) collective-permute-start(bf16[52,2,256]{2,1,0:T(2,128)(2,1)S(1)} %get-tuple-element.44), channel_id=1, source_target_pairs={{0,1},{1,2},{2,3},{3,4},{4,5},{5,6},{6,7},{7,8},{8,9},{9,10},{10,1... | collective-permute-start | bytes 159752 | tf_op jit(solution)/shard_map/ppermute | solution.py:17
  69.9 5.7 %collective-permute-start.15 = (bf16[52,2,256]{2,1,0:T(2,128)(2,1)S(1)}, bf16[52,2,256]{2,1,0:T(2,128)(2,1)S(1)}, u32[]{:S(2)}, u32[]{:S(2)}) collective-permute-start(bf16[52,2,256]{2,1,0:T(2,128)(2,1)S(1)} %get-tuple-element.45), channel_id=1, source_target_pairs={{1,0},{2,1},{3,2},{4,3},{5,4},{6,5},{7,6},{8,7},{9,8},{10,9},{11,1... | collective-permute-start | bytes 159752 | tf_op jit(solution)/shard_map/ppermute | solution.py:19
  74.2 1.4 copy-start.9
  97.3 1.5 copy-start.8
  98.8 1.1 copy-start.7
  99.9 1.1 copy-start.6
  101.0 1.1 copy-start.5
  102.1 1.1 copy-start.4
  103.2 1.1 copy-start.3
  104.3 1.1 copy-start.2
  105.4 1.1 copy-start.1
  113.2 1.5 copy-start.10
Sparse Core Ops, SparseCore 0:
  123.7 281.2 all-reduce.2
where the time goes:
time: 423 us; the launch traced here: 417 us
  waiting for transfers between devices  288 us (68%)
  local copies, waits for them, and re-layouts  44.8 us (11%)
  starting transfers between devices  35.7 us (8%)
  matrix products  27.8 us (7%)
  between operations  16 us (4%)
  other arithmetic  4.45 us (1%)
    psum x1, waiting for transfers between devices, body(): summed = lax.psum((grad_high, grad_low, grad_join), ('lat', 'lon'))  281 us
    ppermute x8, starting transfers between devices, padded_2(): lax.ppermute(head, axis, [((i + 1) % count, i) for i in range(count)])  24.5 us
    reshape x9, local copies, waits for them, and re-layouts, conv_back(): window = padded[2 - offset_row:2 - offset_row + row_count, 2 - offset_col...  17.8 us
    dot_general x27, matrix products, kernel_grad(): lax.dot_general(window, flat_grad, (((0,), (0,)), ((), ())), preferred_el...  15.8 us
    unnamed x33, local copies, waits for them, and re-layouts  12.7 us
    ppermute x8, starting transfers between devices, padded_2(): lax.ppermute(tail, axis, [(i, (i + 1) % count) for i in range(count)])  11.2 us
  transfers between devices with their start and end apart: 17, of which 7 were waited for; matrix products, arithmetic and copies ran while one was open for 2% of the time, Pallas kernels for 0%

commit v1 on v0

v1 whole, which is shorter than its diff:
```python
import jax
import jax.numpy as jnp
import numpy as np
from jax import lax
from jax.experimental import pallas as pl
from jax.experimental.pallas import tpu as pltpu
from jax.sharding import Mesh, PartitionSpec as P

F32 = jnp.float32
BF16 = jnp.bfloat16
C = 256
H, W = 48, 24
LH, LW = 16, 8
WW = 32
LWW = 16
LAT = ("yh", "yl", "xh")
LON = ("zh", "zm", "zl", "xl", "core")
SCALE = 2.0 / (H * W * H * W)
NINTH = 1.0 / 9.0
PK = 304
PAD = 8
VMEM = pl.BlockSpec(memory_space=pltpu.VMEM)
SMEM = pl.BlockSpec(memory_space=pltpu.SMEM)


def up_matrix():
    def line(pixel, cell_of):
        m, r = pixel // 3, pixel % 3
        return {0: {m - 1: 1, m: 2}, 1: {m: 3}, 2: {m: 2, m + 1: 1}}[r].get(cell_of, 0)

    rows = np.array([[line(i - 3, e - 2) for e in range(8)] for i in range(18)])
    cols = np.array([[line(j - 4, f - 3) for f in range(LWW)] for j in range(WW)])
    return np.einsum("ie,jf->ijef", rows, cols).reshape(18 * WW, 8 * LWW)


def down_matrix():
    taps = [1, 2, 3, 2, 1]
    rows = np.zeros((8, 26))
    for m in range(8):
        rows[m, 3 * m : 3 * m + 5] = taps
    cols = np.zeros((LWW, WW))
    for m in range(LW):
        cols[m + 3, 3 * m + 3 : 3 * m + 8] = taps
    return np.einsum("md,fj->mfdj", rows, cols).reshape(8 * LWW, 26 * WW)


def pack_lon(land_ref, hi_ref, tgt_ref, low_ref, west_ref, east_ref):
    land = land_ref[0, 0]
    sub = lax.broadcasted_iota(jnp.int32, (H, 8, C), 1)
    land_a = (land // 32).astype(F32)
    land_b = (land % 32).astype(F32)
    lands = jnp.where(sub == 6, land_a, land_b)
    hi = hi_ref[...].astype(F32)
    tgt = tgt_ref[...].astype(F32)
    west = jnp.where(sub < 4, hi[:, 0:8], jnp.where(sub < 6, pltpu.roll(tgt[:, 0:8], 4, 1), lands))
    east = jnp.where(
        sub < 4,
        pltpu.roll(hi[:, 16:24], 4, 1),
        jnp.where(sub < 6, pltpu.roll(tgt[:, 16:24], 6, 1), lands),
    )
    west_ref[0:H] = west.astype(BF16)
    east_ref[0:H] = east.astype(BF16)
    west_ref[H:] = low_ref[...]
    east_ref[H:] = low_ref[...]


def widen(land_ref, hi_ref, tgt_ref, low_ref, w_ref, e_ref, hiw_ref, tgw_ref, loww_ref, landw_ref, north_ref, south_ref):
    sub = lax.broadcasted_iota(jnp.int32, (H, 8, C), 1)
    low_half = sub < 4
    wpk = w_ref[0:H].astype(F32)
    epk = e_ref[0:H].astype(F32)

    def joined_groups(own, left, right):
        turned = [pltpu.roll(own[:, 8 * g : 8 * g + 8], 4, 1) for g in range(3)]
        parts = [left] + turned + [right]
        return jnp.concatenate(
            [jnp.where(low_half, parts[g], parts[g + 1]) for g in range(4)], axis=1
        ).reshape(H * WW, C)

    hi = joined_groups(hi_ref[...].astype(F32), wpk, pltpu.roll(epk, 4, 1)).astype(BF16)
    hiw_ref[...] = hi
    tgt = joined_groups(tgt_ref[...].astype(F32), pltpu.roll(wpk, 6, 1), epk).astype(BF16)
    tgw_ref[...] = tgt
    sub_low = lax.broadcasted_iota(jnp.int32, (LH, 8, C), 1)
    own_low = pltpu.roll(low_ref[...].astype(F32), 3, 1)
    w_low = pltpu.roll(w_ref[H:].astype(F32), 3, 1)
    e_low = pltpu.roll(e_ref[H:].astype(F32), 3, 1)
    low = jnp.concatenate(
        [jnp.where(sub_low < 3, w_low, own_low), jnp.where(sub_low < 3, own_low, e_low)], axis=1
    ).reshape(LH * LWW, C).astype(BF16)
    loww_ref[...] = low
    land = land_ref[0, 0]
    col = lax.broadcasted_iota(jnp.int32, (WW, C), 0)

    def land_rows(part, own):
        left = wpk[0, part : part + 1, :]
        right = epk[0, part : part + 1, :]
        return jnp.where(col < 4, left, jnp.where(col < 4 + W, own, right))

    lands = jnp.concatenate(
        [land_rows(6, (land // 32).astype(F32)), land_rows(7, (land % 32).astype(F32))], axis=0
    ).astype(BF16)
    landw_ref[...] = lands
    north_ref[0:128] = hi[0:128]
    north_ref[128:192] = tgt[0:64]
    north_ref[192:240] = low[0:48]
    north_ref[240:304] = lands
    south_ref[0:128] = hi[44 * WW :]
    south_ref[128:192] = tgt[46 * WW :]
    south_ref[192:240] = low[13 * LWW :]
    south_ref[240:304] = lands


def main(
    pos_ref, hiw_ref, tgw_ref, loww_ref, landw_ref, n_ref, s_ref, kh_ref, kl_ref, kj_ref, up_ref, down_ref,
    keep_ref, send_ref,
    x3_ref, j3_ref, o3_ref, l3_ref, f_ref, ha_ref, la_ref, jg_ref, og_ref, lg_ref, tg_ref, kt_ref, g_ref,
):
    lat = pos_ref[0]
    core = pos_ref[1]
    first = lat == 0
    last = lat == 7

    def spread(dst, count, step):
        def one(t, _):
            s = pl.multiple_of(t * step, 16)
            v = f_ref[pl.ds(s, step + 2 * PAD), :]
            dst[pl.ds(s, step), 0:C] = v[PAD - 1 : PAD - 1 + step].astype(BF16)
            dst[pl.ds(s, step), C : 2 * C] = v[PAD : PAD + step].astype(BF16)
            dst[pl.ds(s, step), 2 * C : 3 * C] = v[PAD + 1 : PAD + 1 + step].astype(BF16)
            return 0

        lax.fori_loop(0, count // step, one, 0)

    def window(src, start, rows, stride):
        return jnp.concatenate(
            [src[pl.ds(pl.multiple_of(start + d * stride, 16), rows), :] for d in range(3)], axis=1
        )

    def zero_rows(start, rows):
        f_ref[PAD + start : PAD + start + rows, :] = jnp.zeros((rows, C), F32)

    f_ref[0:PAD, :] = jnp.zeros((PAD, C), F32)
    f_ref[PAD + 56 * WW :, :] = jnp.zeros((PAD, C), F32)
    for tap in range(9):
        kt_ref[(8 - tap) * C : (9 - tap) * C, :] = kj_ref[tap * C : (tap + 1) * C, :].T

    f_ref[PAD : PAD + 48, :] = n_ref[192:240, :].astype(F32)
    f_ref[PAD + 48 : PAD + 304, :] = loww_ref[...].astype(F32)
    f_ref[PAD + 304 : PAD + 352, :] = s_ref[192:240, :].astype(F32)
    f_ref[PAD + 352 : PAD + 368, :] = jnp.zeros((16, C), F32)

    @pl.when(first)
    def _():
        zero_rows(0, 48)

    @pl.when(last)
    def _():
        zero_rows(304, 48)

    spread(l3_ref, 352, 176)
    low_act = jnp.maximum(
        jnp.dot(window(l3_ref, 0, 320, LWW), kl_ref[...], preferred_element_type=F32), 0.0
    ).astype(BF16)
    la_ref[...] = low_act

    @pl.when(first)
    def _():
        la_ref[0:32, :] = jnp.zeros((32, C), BF16)

    @pl.when(last)
    def _():
        la_ref[288:320, :] = jnp.zeros((32, C), BF16)

    f_ref[PAD : PAD + 128, :] = n_ref[0:128, :].astype(F32)
    f_ref[PAD + 128 : PAD + 1664, :] = hiw_ref[...].astype(F32)
    f_ref[PAD + 1664 : PAD + 1792, :] = s_ref[0:128, :].astype(F32)
    tg_ref[0:64, :] = n_ref[128:192, :]
    tg_ref[64:1600, :] = tgw_ref[...]
    tg_ref[1600:1664, :] = s_ref[128:192, :]

    @pl.when(first)
    def _():
        zero_rows(0, 128)

    @pl.when(last)
    def _():
        zero_rows(1664, 128)

    spread(x3_ref, 1792, 256)

    def high(b, _):
        s = pl.multiple_of(b * 576, 64)
        act = jnp.maximum(
            jnp.dot(window(x3_ref, s, 576, WW), kh_ref[...], preferred_element_type=F32), 0.0
        ).astype(BF16)
        ha_ref[pl.ds(s, 576), :] = act
        cells = la_ref[pl.ds(pl.multiple_of(b * 96, 32), 128), :]
        lift = jnp.dot(up_ref[...], cells, preferred_element_type=F32) * NINTH
        f_ref[pl.ds(PAD + s, 576), :] = act.astype(F32) + lift
        return 0

    lax.fori_loop(0, 3, high, 0)

    @pl.when(first)
    def _():
        zero_rows(0, 96)

    @pl.when(last)
    def _():
        zero_rows(51 * WW, 96)

    spread(j3_ref, 1728, 288)

    def weight_of(ref, base):
        return (ref[base : base + 32, :].astype(F32) * 32.0 + ref[base + 32 : base + 64, :].astype(F32)) * SCALE

    top = weight_of(n_ref, 240)[None]
    mid = weight_of(landw_ref, 0)[None]
    bot = weight_of(s_ref, 240)[None]

    def join(b, _):
        s = pl.multiple_of(b * 416, 32)
        y = jnp.dot(window(j3_ref, s, 416, WW), kj_ref[...], preferred_element_type=F32)
        diff = (y - tg_ref[pl.ds(s, 416), :].astype(F32)).reshape(13, WW, C)
        row = lax.broadcasted_iota(jnp.int32, (13, WW, C), 0) + b * 13
        weight = jnp.where(row < 2, top, jnp.where(row >= 50, bot, mid))
        f_ref[pl.ds(PAD + s, 416), :] = (weight * diff).reshape(416, C)
        return 0

    lax.fori_loop(0, 4, join, 0)

    @pl.when(first)
    def _():
        zero_rows(0, 64)

    @pl.when(last)
    def _():
        zero_rows(50 * WW, 64)

    spread(o3_ref, 1664, 416)

    def own_columns(rows):
        col = lax.broadcasted_iota(jnp.int32, (rows // WW, WW, C), 1).reshape(rows, C)
        return (col >= 4) & (col < 4 + W)

    def contract(x_ref, g_val, base, stride, rows, slot):
        for d in range(3):
            g_ref[slot, d * 768 : (d + 1) * 768, :] = lax.dot_general(
                x_ref[base + d * stride : base + d * stride + rows, :],
                g_val,
                (((0,), (0,)), ((), ())),
                preferred_element_type=F32,
            )

    def own_grad(t, _):
        s = pl.multiple_of(t * 256, 64)
        v = f_ref[pl.ds(PAD + 64 + s, 256), :]
        og_ref[pl.ds(s, 256), :] = jnp.where(own_columns(256), v, 0.0).astype(BF16)
        return 0

    lax.fori_loop(0, 6, own_grad, 0)
    contract(j3_ref, og_ref[...], 64, WW, 1536, 2)

    def back(b, _):
        s = pl.multiple_of(b * 320, 32)
        y = jnp.dot(window(o3_ref, s, 320, WW), kt_ref[...], preferred_element_type=F32)
        jg_ref[pl.ds(s, 320), :] = y.astype(BF16)
        return 0

    lax.fori_loop(0, 5, back, 0)

    @pl.when(first)
    def _():
        jg_ref[0:32, :] = jnp.zeros((32, C), BF16)

    @pl.when(last)
    def _():
        jg_ref[49 * WW :, :] = jnp.zeros((32, C), BF16)

    def high_grad(t, _):
        s = pl.multiple_of(t * 256, 64)
        v = jg_ref[pl.ds(s + 32, 256), :].astype(F32)
        on = ha_ref[pl.ds(s + 96, 256), :].astype(F32) > 0
        og_ref[pl.ds(s, 256), :] = jnp.where(own_columns(256) & on, v, 0.0).astype(BF16)
        return 0

    lax.fori_loop(0, 6, high_grad, 0)
    contract(x3_ref, og_ref[...], 96, WW, 1536, 0)

    for b in range(2):
        lifted = jnp.dot(down_ref[...], jg_ref[b * 768 : b * 768 + 832, :], preferred_element_type=F32) * NINTH
        on = la_ref[32 + b * 128 : 160 + b * 128, :].astype(F32) > 0
        lg_ref[b * 128 : (b + 1) * 128, :] = jnp.where(on, lifted, 0.0).astype(BF16)
    contract(l3_ref, lg_ref[...], 32, LWW, 256, 1)

    def split(t, _):
        pair = t // 4
        k = t % 4
        dst = pl.multiple_of(t * 224, 32)
        for half, ref in ((core, keep_ref), (1 - core, send_ref)):
            src = pl.multiple_of((k * 8 + pair * 2 + half) * 72, 8)
            block = jnp.concatenate(
                [g_ref[g, pl.ds(src, 72), :] for g in range(3)] + [jnp.zeros((8, C), F32)], axis=0
            )
            ref[pl.ds(dst, 224), :] = block.astype(ref.dtype)
        return 0

    lax.fori_loop(0, 16, split, 0)


def merge(keep_ref, recv_ref, out_ref):
    lane = lax.broadcasted_iota(jnp.int32, (224, 128), 1) < 64

    def one(t, _):
        s = pl.multiple_of(t * 224, 32)
        v = keep_ref[pl.ds(s, 224), :] + recv_ref[pl.ds(s, 224), :].astype(F32)
        a, b = v[:, :128], v[:, 128:]
        out_ref[0, pl.ds(s, 224), :] = jnp.where(lane, a, pltpu.roll(b, 64, 1)).astype(BF16)
        out_ref[1, pl.ds(s, 224), :] = jnp.where(lane, pltpu.roll(a, 64, 1), b).astype(BF16)
        return 0

    lax.fori_loop(0, 16, one, 0)


def regroup(in_ref, out_ref):
    quarter = lax.broadcasted_iota(jnp.int32, (56, 128), 1) // 32
    for k in range(4):
        total = in_ref[0, k * 224 : (k + 1) * 224, :].astype(F32)
        for i in range(1, 8):
            total = total + in_ref[i, k * 224 : (k + 1) * 224, :].astype(F32)
        parts = [total[s * 56 : (s + 1) * 56] for s in range(4)]
        for q in range(4):
            out = jnp.zeros((56, 128), F32)
            for s in range(4):
                shift = ((s - q) * 32) % 128
                turned = pltpu.roll(parts[s], shift, 1) if shift else parts[s]
                out = jnp.where(quarter == s, turned, out)
            out_ref[q * 4 + k] = out.astype(out_ref.dtype)


def finish(in_ref, a_ref, b_ref, c_ref):
    total = in_ref[0].astype(F32)
    for i in range(1, 16):
        total = total + in_ref[i].astype(F32)
    rows = jnp.concatenate(
        [total if s == 0 else pltpu.roll(total, 128 - 32 * s, 1) for s in range(4)], axis=0
    )
    for g, ref in enumerate((a_ref, b_ref, c_ref)):
        ref[...] = rows[g * 72 : (g + 1) * 72, 0:32]


def call(kernel, out, specs, scratch=(), name=None, vmem=None):
    return pl.pallas_call(
        kernel,
        out_shape=tuple(jax.ShapeDtypeStruct(s, d) for s, d in out),
        in_specs=list(specs),
        out_specs=tuple(VMEM for _ in out),
        scratch_shapes=list(scratch),
        name=name,
        compiler_params=pltpu.CompilerParams(vmem_limit_bytes=vmem) if vmem else None,
    )


def ring(count, step):
    return [(i, (i + step) % count) for i in range(count)]


def body(hi, low, kh, kl, kj, tgt, land):
    west, east = call(
        pack_lon, [((H + LH, 8, C), BF16)] * 2, [SMEM] + [VMEM] * 3, name="pack_lon"
    )(land, hi, tgt, low)
    from_e = lax.ppermute(west, LON, ring(32, -1))
    from_w = lax.ppermute(east, LON, ring(32, 1))
    hiw, tgw, loww, landw, north, south = call(
        widen,
        [((H * WW, C), BF16), ((H * WW, C), BF16), ((LH * LWW, C), BF16), ((64, C), BF16), ((PK, C), BF16), ((PK, C), BF16)],
        [SMEM] + [VMEM] * 5,
        name="widen",
    )(land, hi, tgt, low, from_w, from_e)
    from_s = lax.ppermute(north, LAT, ring(8, -1))
    from_n = lax.ppermute(south, LAT, ring(8, 1))
    pos = jnp.stack([lax.axis_index(LAT), lax.axis_index("core")]).astype(jnp.int32)
    keep, send = call(
        main,
        [((3584, C), F32), ((3584, C), BF16)],
        [SMEM] + [VMEM] * 11,
        [
            pltpu.VMEM((1792, 768), BF16),
            pltpu.VMEM((1728, 768), BF16),
            pltpu.VMEM((1664, 768), BF16),
            pltpu.VMEM((352, 768), BF16),
            pltpu.VMEM((1792 + 2 * PAD, C), F32),
            pltpu.VMEM((1728, C), BF16),
            pltpu.VMEM((320, C), BF16),
            pltpu.VMEM((1600, C), BF16),
            pltpu.VMEM((1536, C), BF16),
            pltpu.VMEM((256, C), BF16),
            pltpu.VMEM((1664, C), BF16),
            pltpu.VMEM((2304, C), BF16),
            pltpu.VMEM((3, 2304, C), F32),
        ],
        name="main",
        vmem=60 * 1024 * 1024,
    )(
        pos, hiw, tgw, loww, landw, from_n, from_s,
        kh.reshape(9 * C, C), kl.reshape(9 * C, C), kj.reshape(9 * C, C),
        jnp.asarray(up_matrix(), BF16), jnp.asarray(down_matrix(), BF16),
    )
    recv = lax.ppermute(send, "core", ring(2, 1))
    (parts,) = call(merge, [((2, 3584, 128), BF16)], [VMEM] * 2, name="merge")(keep, recv)
    parts = lax.all_to_all(parts.reshape(8, 896, 128), ("yl", "zl", "xl"), 0, 0, tiled=True)
    (parts,) = call(regroup, [((16, 56, 128), F32)], [VMEM], name="regroup")(parts)
    parts = lax.all_to_all(parts, ("yh", "xh", "zh", "zm"), 0, 0, tiled=True)
    return call(finish, [((72, 32), F32)] * 3, [VMEM], name="finish")(parts)


def solution(mesh):
    fine = Mesh(mesh.devices.reshape((2,) * 8), LAT + LON)
    tile = P(LAT, LON, None)
    return jax.shard_map(
        body,
        mesh=fine,
        in_specs=(tile, tile, P(), P(), P(), tile, P(LAT, LON)),
        out_specs=(P(LON, LAT),) * 3,
        check_vma=False,
    )
```

time: 423 us -> 131 us (0.31); the launches traced: 417 us -> 130 us
  waiting for transfers between devices: 288 us -> 14.7 us
  blocking collectives: 0 us -> 58.9 us
  local copies, waits for them, and re-layouts: 44.8 us -> 7.62 us
  Pallas kernels: 0 us -> 36.7 us
  matrix products: 27.8 us -> 0 us
  starting transfers between devices: 35.7 us -> 10.7 us
  between operations: 16 us -> 1.29 us
    psum x1 -> x0, waiting for transfers between devices: 281 us -> none  [body(): summed = lax.psum((grad_high, grad_low, grad_join), ('lat', 'lon'))]
    all_to_all x0 -> x2, blocking collectives: none -> 58.9 us  [the longest x1 31.2 us: body(): parts = lax.all_to_all(parts, ('yh', 'xh', 'zh', 'zm'), 0, 0, tiled=True)]
    pallas_call x0 -> x6, Pallas kernels: none -> 36.7 us  [the longest x1 21.7 us: body(): call(main, [((3584, C), F32), ((3584, C), BF16)], [SMEM] + [VMEM] * 11, [...]
    dot_general x63 -> x0, matrix products: 27.8 us -> none  [the longest x27 15.8 us: kernel_grad(): lax.dot_general(window, flat_grad, (((0,), (0,)), ((), ())), preferred_el...]
    ppermute x16 -> x5, starting transfers between devices: 35.7 us -> 10.7 us  [the longest x1 6.22 us: body(): from_e = lax.ppermute(west, LON, ring(32, -1))]
    reshape x20 -> x0, local copies, waits for them, and re-layouts: 18.6 us -> none  [the longest x9 17.8 us: conv_back(): window = padded[2 - offset_row:2 - offset_row + row_count, 2 - offset_col...]
    slice x41 -> x0, local copies, waits for them, and re-layouts: 10.6 us -> none  [the longest x29 4.37 us: conv_valid(): padded[offset_row:offset_row + row_count, offset_col:offset_col + col_count]]
    unnamed x33 -> x10, local copies, waits for them, and re-layouts: 12.7 us -> 3.28 us
  transfers between devices with their start and end apart: 17 -> 5, of which waited for: 7 -> 4; matrix products, arithmetic and copies ran while one was open for 2% -> 0% of each run, Pallas kernels for 0% -> 0%
where the time goes in v1:
time: 131 us; the launch traced here: 130 us
  blocking collectives  58.9 us (45%)
  Pallas kernels  36.7 us (28%)
  waiting for transfers between devices  14.7 us (11%)
  starting transfers between devices  10.7 us (8%)
  local copies, waits for them, and re-layouts  7.62 us (6%)
    all_to_all x1, blocking collectives, body(): parts = lax.all_to_all(parts, ('yh', 'xh', 'zh', 'zm'), 0, 0, tiled=True)  31.2 us
    all_to_all x1, blocking collectives, body(): lax.all_to_all(parts.reshape(8, 896, 128), ('yl', 'zl', 'xl'), 0, 0, tile...  27.7 us
    pallas_call x1, Pallas kernels, body(): call(main, [((3584, C), F32), ((3584, C), BF16)], [SMEM] + [VMEM] * 11, [...  21.7 us
    ppermute x1, starting transfers between devices, body(): from_e = lax.ppermute(west, LON, ring(32, -1))  6.22 us
    pallas_call x1, Pallas kernels, body(): call(merge, [((2, 3584, 128), BF16)], [VMEM] * 2, name='merge')(keep, recv)  5.52 us
    ppermute x1, waiting for transfers between devices, body(): from_n = lax.ppermute(south, LAT, ring(8, 1))  4.5 us
    ppermute x1, waiting for transfers between devices, body(): from_w = lax.ppermute(east, LON, ring(32, 1))  4.37 us
    pallas_call x3, local copies, waits for them, and re-layouts, body(): return call(finish, [((72, 32), F32)] * 3, [VMEM], name='finish')(parts)  4.34 us
  transfers between devices with their start and end apart: 5, of which 4 were waited for; matrix products, arithmetic and copies ran while one was open for 0% of the time, Pallas kernels for 0%

profile of v1, /device:TPU:8, one launch (start us, length us, event | category | flops | bytes accessed | tf_op | source)
XLA Modules:
  0.0 130.5 jit_solution(7339390725927273930)
XLA Ops:
  1.3 2.1 %pack_lon.1 = (bf16[64,8,256]{2,1,0:T(8,128)(2,1)}, bf16[64,8,256]{2,1,0:T(8,128)(2,1)}) custom-call(s32[1,1]{1,0:T(1,128)S(6)} %copy.15.land_ref, bf16[48,24,256]{2,1,0:T(8,128)(2,1)} %hi_ref.3, bf16[48,24,256]{2,1,0:T(8,128)(2,1)} %tgt_ref.3, bf16[16,8,256]{2,1,0:T(8,128)(2,1)} %low_ref.3), custom_call_target="tpu_custom_call" | custom-call | tf_op jit(solution)/shard_map/pack_lon/pallas_call | solution.py:370
  3.4 0.0 collective-permute-start
  3.4 6.2 %collective-permute-start.1 = (bf16[64,8,256]{2,1,0:T(8,128)(2,1)}, bf16[64,8,256]{2,1,0:T(8,128)(2,1)S(1)}, u32[]{:S(2)}, u32[]{:S(2)}) collective-permute-start(bf16[64,8,256]{2,1,0:T(8,128)(2,1)} %get-tuple-element.14), channel_id=1, source_target_pairs={{0,31},{1,0},{2,1},{3,2},{4,3},{5,4},{6,5},{7,6},{8,7},{9,8},{10,9... | collective-permute-start | bytes 786440 | tf_op jit(solution)/shard_map/ppermute | solution.py:373
  9.6 4.4 %collective-permute-done.w_ref = bf16[64,8,256]{2,1,0:T(8,128)(2,1)S(1)} collective-permute-done((bf16[64,8,256]{2,1,0:T(8,128)(2,1)}, bf16[64,8,256]{2,1,0:T(8,128)(2,1)S(1)}, u32[]{:S(2)}, u32[]{:S(2)}) %collective-permute-start) | collective-permute-done | bytes 262176 | tf_op jit(solution)/shard_map/ppermute | solution.py:374
  14.0 0.0 copy-start.1
  14.0 0.0 collective-permute-done.1.e_ref
  14.0 0.7 copy-done.1
  14.7 0.0 copy-start.2
  14.7 0.7 copy-done.2
  15.4 2.9 %widen.1 = (bf16[1536,256]{1,0:T(8,128)(2,1)}, bf16[1536,256]{1,0:T(8,128)(2,1)}, bf16[256,256]{1,0:T(8,128)(2,1)}, bf16[64,256]{1,0:T(8,128)(2,1)}, bf16[304,256]{1,0:T(8,128)(2,1)}, /*index=5*/bf16[304,256]{1,0:T(8,128)(2,1)}) custom-call(s32[1,1]{1,0:T(1,128)S(6)} %copy.15.land_ref, bf16[48,24,256]{2,1,0:T(8,128)(2,1)} %hi_ref.3, ...), custom_call_target="tpu_custom_call" | custom-call | tf_op jit(solution)/shard_map/widen/pallas_call | solution.py:375
  18.3 2.7 %collective-permute-start.2 = (bf16[304,256]{1,0:T(8,128)(2,1)}, bf16[304,256]{1,0:T(8,128)(2,1)S(1)}, u32[]{:S(2)}, u32[]{:S(2)}) collective-permute-start(bf16[304,256]{1,0:T(8,128)(2,1)} %get-tuple-element.19), channel_id=1, source_target_pairs={{0,32},{32,64},{64,96},{96,128},{128,160},{160,192},{192,224},{224... | collective-permute-start | bytes 466952 | tf_op jit(solution)/shard_map/ppermute | solution.py:382
  21.0 1.7 %collective-permute-start.3 = (bf16[304,256]{1,0:T(8,128)(2,1)}, bf16[304,256]{1,0:T(8,128)(2,1)S(1)}, u32[]{:S(2)}, u32[]{:S(2)}) collective-permute-start(bf16[304,256]{1,0:T(8,128)(2,1)} %get-tuple-element.20), channel_id=1, source_target_pairs={{0,224},{32,0},{64,32},{96,64},{128,96},{160,128},{192,160},{224,1... | collective-permute-start | bytes 466952 | tf_op jit(solution)/shard_map/ppermute | solution.py:381
  22.7 0.6 pad_add_fusion.pos_ref
  23.3 4.5 %collective-permute-done.2.n_ref = bf16[304,256]{1,0:T(8,128)(2,1)S(1)} collective-permute-done((bf16[304,256]{1,0:T(8,128)(2,1)}, bf16[304,256]{1,0:T(8,128)(2,1)S(1)}, u32[]{:S(2)}, u32[]{:S(2)}) %collective-permute-start.2) | collective-permute-done | bytes 155680 | tf_op jit(solution)/shard_map/ppermute | solution.py:382
  27.8 0.0 copy-start.3
  27.8 1.8 %collective-permute-done.3.s_ref = bf16[304,256]{1,0:T(8,128)(2,1)S(1)} collective-permute-done((bf16[304,256]{1,0:T(8,128)(2,1)}, bf16[304,256]{1,0:T(8,128)(2,1)S(1)}, u32[]{:S(2)}, u32[]{:S(2)}) %collective-permute-start.3) | collective-permute-done | bytes 155680 | tf_op jit(solution)/shard_map/ppermute | solution.py:381
  29.7 0.0 copy-start.4
  29.7 0.0 copy-done.3
  29.7 0.6 copy-done.4
  30.3 21.7 %main.1 = (f32[3584,256]{1,0:T(8,128)}, bf16[3584,256]{1,0:T(8,128)(2,1)}) custom-call(s32[2]{0:T(128)} %pad_add_fusion.pos_ref, bf16[1536,256]{1,0:T(8,128)(2,1)} %get-tuple-element.15.hiw_ref, bf16[1536,256]{1,0:T(8,128)(2,1)} %get-tuple-element.16.tgw_ref, bf16[256,256]{1,0:T(8,128)(2,1)} %get-tuple-element.17.loww_ref, ...), custom_call_target="tpu_custom_call" | custom-call | tf_op jit(solution)/shard_map/main/pallas_call | solution.py:384
  52.0 0.0 collective-permute-start.4
  52.0 4.0 %collective-permute-done.4.recv_ref = bf16[3584,256]{1,0:T(8,128)(2,1)S(1)} collective-permute-done((bf16[3584,256]{1,0:T(8,128)(2,1)}, bf16[3584,256]{1,0:T(8,128)(2,1)S(1)}, u32[]{:S(2)}, u32[]{:S(2)}) %collective-permute-start.4) | collective-permute-done | bytes 1835040 | tf_op jit(solution)/shard_map/ppermute | solution.py:410
  56.0 0.0 copy-start
  56.0 1.2 copy-done
  57.2 5.5 %merge.1 = bf16[2,3584,128]{2,1,0:T(8,128)(2,1)} custom-call(f32[3584,256]{1,0:T(8,128)} %get-tuple-element.21.keep_ref, bf16[3584,256]{1,0:T(8,128)(2,1)} %copy-done), custom_call_target="tpu_custom_call" | custom-call | tf_op jit(solution)/shard_map/merge/pallas_call | solution.py:411
  62.7 27.7 %all_to_all.10.in_ref = bf16[8,896,128]{2,1,0:T(8,128)(2,1)} all-to-all(bf16[8,896,128]{2,1,0:T(8,128)(2,1)} %bitcast.6), channel_id=1, replica_groups=mesh['yh'=2,'yl'=2,'xh'=2,'zh'=2,'zm'=2,'zl'=2,'xl'=2,'core'=2] {'yl','z..., dimensions={0} | all-to-all | bytes 3670016 | tf_op jit(solution)/shard_map/all_to_all | solution.py:412
  90.4 2.7 %regroup.1 = f32[16,56,128]{2,1,0:T(8,128)} custom-call(bf16[8,896,128]{2,1,0:T(8,128)(2,1)} %all_to_all.10.in_ref), custom_call_target="tpu_custom_call" | custom-call | tf_op jit(solution)/shard_map/regroup/pallas_call | solution.py:413
  93.2 31.2 %all_to_all.11.in_ref = f32[16,56,128]{2,1,0:T(8,128)} all-to-all(f32[16,56,128]{2,1,0:T(8,128)} %regroup.1), channel_id=1, replica_groups=mesh['yh'=2,'yl'=2,'xh'=2,'zh'=2,'zm'=2,'zl'=2,'xl'=2,'core'=2] {'yh','x..., dimensions={0} | all-to-all | bytes 917504 | tf_op jit(solution)/shard_map/all_to_all | solution.py:414
  124.4 1.8 %finish.1 = (f32[72,32]{1,0:T(8,128)}, f32[72,32]{1,0:T(8,128)}, f32[72,32]{1,0:T(8,128)}) custom-call(f32[16,56,128]{2,1,0:T(8,128)} %all_to_all.11.in_ref), custom_call_target="tpu_custom_call" | custom-call | tf_op jit(solution)/shard_map/finish/pallas_call | solution.py:415
  126.1 1.4 %copy.12 = f32[72,32]{0,1:T(8,128)} copy(f32[72,32]{1,0:T(8,128)} %get-tuple-element.23) | data formatting | bytes 18432 | tf_op jit(solution)/shard_map/finish/pallas_call | solution.py:415
  127.6 1.4 %copy.13 = f32[72,32]{0,1:T(8,128)} copy(f32[72,32]{1,0:T(8,128)} %get-tuple-element.24) | data formatting | bytes 18432 | tf_op jit(solution)/shard_map/finish/pallas_call | solution.py:415
  129.0 1.4 %copy.14 = f32[72,32]{0,1:T(8,128)} copy(f32[72,32]{1,0:T(8,128)} %get-tuple-element.25) | data formatting | bytes 18432 | tf_op jit(solution)/shard_map/finish/pallas_call | solution.py:415
Async XLA Ops:
  3.4 10.6 %collective-permute-start = (bf16[64,8,256]{2,1,0:T(8,128)(2,1)}, bf16[64,8,256]{2,1,0:T(8,128)(2,1)S(1)}, u32[]{:S(2)}, u32[]{:S(2)}) collective-permute-start(bf16[64,8,256]{2,1,0:T(8,128)(2,1)} %get-tuple-element.13), channel_id=1, source_target_pairs={{0,1},{1,2},{2,3},{3,4},{4,5},{5,6},{6,7},{7,8},{8,9},{9,10},{10,1... | collective-permute-start | bytes 786440 | tf_op jit(solution)/shard_map/ppermute | solution.py:374
  3.4 10.6 %collective-permute-start.1 = (bf16[64,8,256]{2,1,0:T(8,128)(2,1)}, bf16[64,8,256]{2,1,0:T(8,128)(2,1)S(1)}, u32[]{:S(2)}, u32[]{:S(2)}) collective-permute-start(bf16[64,8,256]{2,1,0:T(8,128)(2,1)} %get-tuple-element.14), channel_id=1, source_target_pairs={{0,31},{1,0},{2,1},{3,2},{4,3},{5,4},{6,5},{7,6},{8,7},{9,8},{10,9... | collective-permute-start | bytes 786440 | tf_op jit(solution)/shard_map/ppermute | solution.py:373
  14.0 0.7 copy-start.1
  14.7 0.7 copy-start.2
  18.3 9.5 %collective-permute-start.2 = (bf16[304,256]{1,0:T(8,128)(2,1)}, bf16[304,256]{1,0:T(8,128)(2,1)S(1)}, u32[]{:S(2)}, u32[]{:S(2)}) collective-permute-start(bf16[304,256]{1,0:T(8,128)(2,1)} %get-tuple-element.19), channel_id=1, source_target_pairs={{0,32},{32,64},{64,96},{96,128},{128,160},{160,192},{192,224},{224... | collective-permute-start | bytes 466952 | tf_op jit(solution)/shard_map/ppermute | solution.py:382
  21.0 8.6 %collective-permute-start.3 = (bf16[304,256]{1,0:T(8,128)(2,1)}, bf16[304,256]{1,0:T(8,128)(2,1)S(1)}, u32[]{:S(2)}, u32[]{:S(2)}) collective-permute-start(bf16[304,256]{1,0:T(8,128)(2,1)} %get-tuple-element.20), channel_id=1, source_target_pairs={{0,224},{32,0},{64,32},{96,64},{128,96},{160,128},{192,160},{224,1... | collective-permute-start | bytes 466952 | tf_op jit(solution)/shard_map/ppermute | solution.py:381
  27.8 1.9 %copy-start.3 = (bf16[304,256]{1,0:T(8,128)(2,1)}, bf16[304,256]{1,0:T(8,128)(2,1)S(1)}, u32[]{:S(2)}) copy-start(bf16[304,256]{1,0:T(8,128)(2,1)S(1)} %collective-permute-done.2.n_ref) | copy-start | bytes 466948
  29.7 0.7 copy-start.4
  52.0 4.0 %collective-permute-start.4 = (bf16[3584,256]{1,0:T(8,128)(2,1)}, bf16[3584,256]{1,0:T(8,128)(2,1)S(1)}, u32[]{:S(2)}, u32[]{:S(2)}) collective-permute-start(bf16[3584,256]{1,0:T(8,128)(2,1)} %get-tuple-element.22), channel_id=1, source_target_pairs={{0,1},{1,0},{2,3},{3,2},{4,5},{5,4},{6,7},{7,6},{8,9},{9,8},{10,11... | collective-permute-start | bytes 5505032 | tf_op jit(solution)/shard_map/ppermute | solution.py:410
  56.0 1.2 copy-start

commit v2 on v1

--- a/solution.py
+++ b/solution.py
@@ -19,6 +19,7 @@
 NINTH = 1.0 / 9.0
 PK = 304
 PAD = 8
+MIB = 1024 * 1024
 VMEM = pl.BlockSpec(memory_space=pltpu.VMEM)
 SMEM = pl.BlockSpec(memory_space=pltpu.SMEM)
 
@@ -295,11 +296,11 @@
     contract(l3_ref, lg_ref[...], 32, LWW, 256, 1)
 
     def split(t, _):
-        pair = t // 4
-        k = t % 4
+        xl = t // 8
+        z = t % 8
         dst = pl.multiple_of(t * 224, 32)
         for half, ref in ((core, keep_ref), (1 - core, send_ref)):
-            src = pl.multiple_of((k * 8 + pair * 2 + half) * 72, 8)
+            src = pl.multiple_of((z * 4 + xl * 2 + half) * 72, 8)
             block = jnp.concatenate(
                 [g_ref[g, pl.ds(src, 72), :] for g in range(3)] + [jnp.zeros((8, C), F32)], axis=0
             )
@@ -310,44 +311,47 @@
 
 
 def merge(keep_ref, recv_ref, out_ref):
-    lane = lax.broadcasted_iota(jnp.int32, (224, 128), 1) < 64
+    quarter = lax.broadcasted_iota(jnp.int32, (56, 128), 1) // 32
 
     def one(t, _):
+        xl = t // 8
+        z = t % 8
         s = pl.multiple_of(t * 224, 32)
         v = keep_ref[pl.ds(s, 224), :] + recv_ref[pl.ds(s, 224), :].astype(F32)
-        a, b = v[:, :128], v[:, 128:]
-        out_ref[0, pl.ds(s, 224), :] = jnp.where(lane, a, pltpu.roll(b, 64, 1)).astype(BF16)
-        out_ref[1, pl.ds(s, 224), :] = jnp.where(lane, pltpu.roll(a, 64, 1), b).astype(BF16)
+        for h in range(2):
+            parts = [v[g * 56 : (g + 1) * 56, h * 128 : (h + 1) * 128] for g in range(4)]
+            for q in range(4):
+                out = None
+                for g in range(4):
+                    shift = ((g - q) * 32) % 128
+                    turned = pltpu.roll(parts[g], shift, 1) if shift else parts[g]
+                    out = turned if out is None else jnp.where(quarter == g, turned, out)
+                out_ref[(h * 4 + q) * 2 + xl, z] = out.astype(BF16)
         return 0
 
     lax.fori_loop(0, 16, one, 0)
 
 
-def regroup(in_ref, out_ref):
-    quarter = lax.broadcasted_iota(jnp.int32, (56, 128), 1) // 32
-    for k in range(4):
-        total = in_ref[0, k * 224 : (k + 1) * 224, :].astype(F32)
-        for i in range(1, 8):
-            total = total + in_ref[i, k * 224 : (k + 1) * 224, :].astype(F32)
-        parts = [total[s * 56 : (s + 1) * 56] for s in range(4)]
-        for q in range(4):
-            out = jnp.zeros((56, 128), F32)
-            for s in range(4):
-                shift = ((s - q) * 32) % 128
-                turned = pltpu.roll(parts[s], shift, 1) if shift else parts[s]
-                out = jnp.where(quarter == s, turned, out)
-            out_ref[q * 4 + k] = out.astype(out_ref.dtype)
+def total(in_ref, out_ref):
+    def one(z, _):
+        acc = in_ref[0, z].astype(F32)
+        for i in range(1, 16):
+            acc = acc + in_ref[i, z].astype(F32)
+        out_ref[z] = acc.astype(out_ref.dtype)
+        return 0
+
+    lax.fori_loop(0, 8, one, 0)
 
 
 def finish(in_ref, a_ref, b_ref, c_ref):
-    total = in_ref[0].astype(F32)
-    for i in range(1, 16):
-        total = total + in_ref[i].astype(F32)
+    acc = in_ref[0].astype(F32)
+    for i in range(1, 8):
+        acc = acc + in_ref[i].astype(F32)
     rows = jnp.concatenate(
-        [total if s == 0 else pltpu.roll(total, 128 - 32 * s, 1) for s in range(4)], axis=0
+        [acc if s == 0 else pltpu.roll(acc, 128 - 32 * s, 1) for s in range(4)], axis=0
     )
     for g, ref in enumerate((a_ref, b_ref, c_ref)):
-        ref[...] = rows[g * 72 : (g + 1) * 72, 0:32]
+        ref[...] = rows[g * 72 : (g + 1) * 72].T[0:32]
 
 
 def call(kernel, out, specs, scratch=(), name=None, vmem=None):
@@ -368,7 +372,7 @@
 
 def body(hi, low, kh, kl, kj, tgt, land):
     west, east = call(
-        pack_lon, [((H + LH, 8, C), BF16)] * 2, [SMEM] + [VMEM] * 3, name="pack_lon"
+        pack_lon, [((H + LH, 8, C), BF16)] * 2, [SMEM] + [VMEM] * 3, name="pack_lon", vmem=8 * MIB
     )(land, hi, tgt, low)
     from_e = lax.ppermute(west, LON, ring(32, -1))
     from_w = lax.ppermute(east, LON, ring(32, 1))
@@ -377,6 +381,7 @@
         [((H * WW, C), BF16), ((H * WW, C), BF16), ((LH * LWW, C), BF16), ((64, C), BF16), ((PK, C), BF16), ((PK, C), BF16)],
         [SMEM] + [VMEM] * 5,
         name="widen",
+        vmem=14 * MIB,
     )(land, hi, tgt, low, from_w, from_e)
     from_s = lax.ppermute(north, LAT, ring(8, -1))
     from_n = lax.ppermute(south, LAT, ring(8, 1))
@@ -401,18 +406,19 @@
             pltpu.VMEM((3, 2304, C), F32),
         ],
         name="main",
-        vmem=60 * 1024 * 1024,
+        vmem=38 * MIB,
     )(
         pos, hiw, tgw, loww, landw, from_n, from_s,
         kh.reshape(9 * C, C), kl.reshape(9 * C, C), kj.reshape(9 * C, C),
         jnp.asarray(up_matrix(), BF16), jnp.asarray(down_matrix(), BF16),
     )
     recv = lax.ppermute(send, "core", ring(2, 1))
-    (parts,) = call(merge, [((2, 3584, 128), BF16)], [VMEM] * 2, name="merge")(keep, recv)
-    parts = lax.all_to_all(parts.reshape(8, 896, 128), ("yl", "zl", "xl"), 0, 0, tiled=True)
-    (parts,) = call(regroup, [((16, 56, 128), F32)], [VMEM], name="regroup")(parts)
-    parts = lax.all_to_all(parts, ("yh", "xh", "zh", "zm"), 0, 0, tiled=True)
-    return call(finish, [((72, 32), F32)] * 3, [VMEM], name="finish")(parts)
+    (parts,) = call(merge, [((16, 8, 56, 128), BF16)], [VMEM] * 2, name="merge", vmem=12 * MIB)(keep, recv)
+    parts = lax.all_to_all(parts, ("yh", "yl", "xh", "xl"), 0, 0, tiled=True)
+    (parts,) = call(total, [((8, 56, 128), F32)], [VMEM], name="total", vmem=6 * MIB)(parts)
+    parts = lax.all_to_all(parts, ("zh", "zm", "zl"), 0, 0, tiled=True)
+    grads = call(finish, [((32, 72), F32)] * 3, [VMEM], name="finish", vmem=2 * MIB)(parts)
+    return tuple(g.T for g in grads)
 
 
 def solution(mesh):

time: 131 us -> 112 us (0.85)
  Pallas kernels: 36.7 us -> 22.3 us
  blocking collectives: 58.9 us -> 47.1 us
  local copies, waits for them, and re-layouts: 7.62 us -> 13 us
    all_to_all x2, blocking collectives: 58.9 us -> 47.1 us  [the longest x1 30.6 us: body(): parts = lax.all_to_all(parts, ('yh', 'yl', 'xh', 'xl'), 0, 0, tiled=True)]
    unnamed x10 -> x34, local copies, waits for them, and re-layouts: 3.28 us -> 13 us
    pallas_call x3, Pallas kernels: 10 us -> 3.74 us  [the longest x1 2.66 us: body(): call(merge, [((16, 8, 56, 128), BF16)], [VMEM] * 2, name='merge', vmem=12...]
    pallas_call x3 -> x0, local copies, waits for them, and re-layouts: 4.34 us -> none  [body(): return call(finish, [((72, 32), F32)] * 3, [VMEM], name='finish')(parts)]
    pallas_call x1, Pallas kernels: 21.7 us -> 17.5 us  [body(): call(main, [((3584, C), F32), ((3584, C), BF16)], [SMEM] + [VMEM] * 11, [...]
    pallas_call x1, Pallas kernels: 2.92 us -> 0.9 us  [body(): call(widen, [((H * WW, C), BF16), ((H * WW, C), BF16), ((LH * LWW, C), BF...]
    pallas_call x1, Pallas kernels: 2.13 us -> 0.16 us  [body(): call(pack_lon, [((H + LH, 8, C), BF16)] * 2, [SMEM] + [VMEM] * 3, name='p...]
where the time goes in v2:
time: 112 us; the launch traced here: 110 us
  blocking collectives  47.1 us (42%)
  Pallas kernels  22.3 us (20%)
  waiting for transfers between devices  15.5 us (14%)
  local copies, waits for them, and re-layouts  13 us (12%)
  starting transfers between devices  10.9 us (10%)
  between operations  1.36 us (1%)
    all_to_all x1, blocking collectives, body(): parts = lax.all_to_all(parts, ('yh', 'yl', 'xh', 'xl'), 0, 0, tiled=True)  30.6 us
    pallas_call x1, Pallas kernels, body(): call(main, [((3584, C), F32), ((3584, C), BF16)], [SMEM] + [VMEM] * 11, [...  17.5 us
    all_to_all x1, blocking collectives, body(): parts = lax.all_to_all(parts, ('zh', 'zm', 'zl'), 0, 0, tiled=True)  16.5 us
    unnamed x34, local copies, waits for them, and re-layouts  13 us
    ppermute x1, starting transfers between devices, body(): from_e = lax.ppermute(west, LON, ring(32, -1))  6.3 us
    ppermute x1, waiting for transfers between devices, body(): from_n = lax.ppermute(south, LAT, ring(8, 1))  5.01 us
    ppermute x1, waiting for transfers between devices, body(): from_w = lax.ppermute(east, LON, ring(32, 1))  4.07 us
    ppermute x1, waiting for transfers between devices, body(): recv = lax.ppermute(send, 'core', ring(2, 1))  3.77 us
  transfers between devices with their start and end apart: 5, of which 4 were waited for; matrix products, arithmetic and copies ran while one was open for 0% of the time, Pallas kernels for 0%

profile of v2, /device:TPU:8, one launch (start us, length us, event | category | flops | bytes accessed | tf_op | source)
XLA Modules:
  0.0 110.2 jit_solution(7383000502796720051)
XLA Ops:
  1.3 0.0 copy-start
  1.3 1.1 copy-done
  2.3 0.0 copy-start.2
  2.3 1.1 copy-done.2
  3.4 0.0 copy-start.9
  3.4 0.8 copy-done.9
  4.2 0.0 copy-start.4
  4.3 0.2 pack_lon.1
  4.4 0.1 collective-permute-start
  4.5 6.3 %collective-permute-start.1 = (bf16[64,8,256]{2,1,0:T(8,128)(2,1)S(1)}, bf16[64,8,256]{2,1,0:T(8,128)(2,1)S(1)}, u32[]{:S(2)}, u32[]{:S(2)}) collective-permute-start(bf16[64,8,256]{2,1,0:T(8,128)(2,1)S(1)} %get-tuple-element.17), channel_id=1, source_target_pairs={{0,31},{1,0},{2,1},{3,2},{4,3},{5,4},{6,5},{7,6},{8,7},{9,8},{10,9... | collective-permute-start | bytes 786440 | tf_op jit(solution)/shard_map/ppermute | solution.py:377
  10.8 4.1 %collective-permute-done.w_ref = bf16[64,8,256]{2,1,0:T(8,128)(2,1)S(1)} collective-permute-done((bf16[64,8,256]{2,1,0:T(8,128)(2,1)S(1)}, bf16[64,8,256]{2,1,0:T(8,128)(2,1)S(1)}, u32[]{:S(2)}, u32[]{:S(2)}) %collective-permute-start) | collective-permute-done | bytes 262176 | tf_op jit(solution)/shard_map/ppermute | solution.py:378
  14.9 0.0 collective-permute-done.1.e_ref
  14.9 0.0 copy-start.1
  14.9 1.1 copy-done.1
  15.9 0.0 copy-start.3
  15.9 1.1 copy-done.3
  17.0 0.0 copy-start.10
  17.0 0.8 copy-done.10
  17.8 0.0 copy-start.5
  17.8 0.0 copy-start.11
  17.8 0.9 widen.1
  18.7 0.0 copy-start.7
  18.7 0.9 copy-done.7
  19.6 0.0 copy-start.13
  19.6 0.6 copy-done.13
  20.3 0.0 copy-start.15
  20.3 0.6 copy-done.15
  20.9 2.7 %collective-permute-start.2 = (bf16[304,256]{1,0:T(8,128)(2,1)}, bf16[304,256]{1,0:T(8,128)(2,1)S(1)}, u32[]{:S(2)}, u32[]{:S(2)}) collective-permute-start(bf16[304,256]{1,0:T(8,128)(2,1)} %get-tuple-element.22), channel_id=1, source_target_pairs={{0,32},{32,64},{64,96},{96,128},{128,160},{160,192},{192,224},{224... | collective-permute-start | bytes 466952 | tf_op jit(solution)/shard_map/ppermute | solution.py:387
  23.6 1.7 %collective-permute-start.3 = (bf16[304,256]{1,0:T(8,128)(2,1)}, bf16[304,256]{1,0:T(8,128)(2,1)}, u32[]{:S(2)}, u32[]{:S(2)}) collective-permute-start(bf16[304,256]{1,0:T(8,128)(2,1)} %get-tuple-element.23), channel_id=1, source_target_pairs={{0,224},{32,0},{64,32},{96,64},{128,96},{160,128},{192,160},{224,1... | collective-permute-start | bytes 466952 | tf_op jit(solution)/shard_map/ppermute | solution.py:386
  25.3 0.1 pad_add_fusion.pos_ref
  25.4 5.0 %collective-permute-done.2.n_ref = bf16[304,256]{1,0:T(8,128)(2,1)S(1)} collective-permute-done((bf16[304,256]{1,0:T(8,128)(2,1)}, bf16[304,256]{1,0:T(8,128)(2,1)S(1)}, u32[]{:S(2)}, u32[]{:S(2)}) %collective-permute-start.2) | collective-permute-done | bytes 155680 | tf_op jit(solution)/shard_map/ppermute | solution.py:387
  30.4 2.6 %collective-permute-done.3.s_ref = bf16[304,256]{1,0:T(8,128)(2,1)} collective-permute-done((bf16[304,256]{1,0:T(8,128)(2,1)}, bf16[304,256]{1,0:T(8,128)(2,1)}, u32[]{:S(2)}, u32[]{:S(2)}) %collective-permute-start.3) | collective-permute-done | bytes 155680 | tf_op jit(solution)/shard_map/ppermute | solution.py:386
  33.0 0.0 copy-done.4
  33.0 0.0 copy-done.5
  33.0 0.0 copy-done.11
  33.0 0.0 copy-start.6
  33.0 1.3 %copy-done.6 = bf16[3,3,256,256]{3,2,1,0:T(8,128)(2,1)S(1)} copy-done((bf16[3,3,256,256]{3,2,1,0:T(8,128)(2,1)S(1)}, bf16[3,3,256,256]{3,2,1,0:T(8,128)(2,1)}, u32[]{:S(2)}) %copy-start.6) | copy-done | bytes 1179672
  34.3 0.0 copy-start.8
  34.3 1.1 %copy-done.8 = bf16[1536,256]{1,0:T(8,128)(2,1)S(1)} copy-done((bf16[1536,256]{1,0:T(8,128)(2,1)S(1)}, bf16[1536,256]{1,0:T(8,128)(2,1)}, u32[]{:S(2)}) %copy-start.8) | copy-done | bytes 786456
  35.4 0.0 copy-start.12
  35.4 0.9 copy-done.12
  36.4 0.0 copy-start.14
  36.4 0.9 copy-done.14
  37.3 0.0 copy-start.16
  37.3 0.8 copy-done.16
  38.0 17.5 %main.1 = (f32[3584,256]{1,0:T(8,128)S(1)}, bf16[3584,256]{1,0:T(8,128)(2,1)S(1)}) custom-call(s32[2]{0:T(128)S(1)} %pad_add_fusion.pos_ref, bf16[1536,256]{1,0:T(8,128)(2,1)S(1)} %get-tuple-element.18.hiw_ref, bf16[1536,256]{1,0:T(8,128)(2,1)S(1)} %copy-done.8, bf16[256,256]{1,0:T(8,128)(2,1)S(1)} %copy-done.14, bf16[64,256]{1,0:T(8,128)(2,1)S(1)} %copy-done.16, ...), custom_call_target="tpu_custom_call" | custom-call | tf_op jit(solution)/shard_map/main/pallas_call | solution.py:389
  55.5 0.1 collective-permute-start.4
  55.6 3.8 %collective-permute-done.4.recv_ref = bf16[3584,256]{1,0:T(8,128)(2,1)S(1)} collective-permute-done((bf16[3584,256]{1,0:T(8,128)(2,1)S(1)}, bf16[3584,256]{1,0:T(8,128)(2,1)S(1)}, u32[]{:S(2)}, u32[]{:S(2)}) %collective-permute-start.4) | collective-permute-done | bytes 1835040 | tf_op jit(solution)/shard_map/ppermute | solution.py:415
  59.4 2.7 %merge.1 = bf16[16,8,56,128]{3,2,1,0:T(8,128)(2,1)S(1)} custom-call(f32[3584,256]{1,0:T(8,128)S(1)} %get-tuple-element.24.keep_ref, bf16[3584,256]{1,0:T(8,128)(2,1)S(1)} %collective-permute-done.4.recv_ref), custom_call_target="tpu_custom_call" | custom-call | tf_op jit(solution)/shard_map/merge/pallas_call | solution.py:416
  62.0 30.6 %all_to_all.10.in_ref = bf16[16,8,56,128]{3,2,1,0:T(8,128)(2,1)S(1)} all-to-all(bf16[16,8,56,128]{3,2,1,0:T(8,128)(2,1)S(1)} %merge.1), channel_id=1, replica_groups=mesh['yh'=2,'yl'=2,'xh'=2,'zh'=2,'zm'=2,'zl'=2,'xl'=2,'core'=2] {'yh','y..., dimensions={0} | all-to-all | bytes 3670016 | tf_op jit(solution)/shard_map/all_to_all | solution.py:417
  92.6 0.3 total.1
  92.9 16.5 %all_to_all.11.in_ref = f32[8,56,128]{2,1,0:T(8,128)S(1)} all-to-all(f32[8,56,128]{2,1,0:T(8,128)S(1)} %total.1), channel_id=1, replica_groups=mesh['yh'=2,'yl'=2,'xh'=2,'zh'=2,'zm'=2,'zl'=2,'xl'=2,'core'=2] {'zh','z..., dimensions={0} | all-to-all | bytes 458752 | tf_op jit(solution)/shard_map/all_to_all | solution.py:419
  109.4 0.8 finish.1
Async XLA Ops:
  1.3 1.1 copy-start
  2.3 1.1 copy-start.2
  3.4 0.8 copy-start.9
  4.2 28.8 %copy-start.4 = (bf16[3,3,256,256]{3,2,1,0:T(8,128)(2,1)S(1)}, bf16[3,3,256,256]{3,2,1,0:T(8,128)(2,1)}, u32[]{:S(2)}) copy-start(bf16[3,3,256,256]{3,2,1,0:T(8,128)(2,1)} %param.11) | copy-start | bytes 3538948
  4.4 10.5 %collective-permute-start = (bf16[64,8,256]{2,1,0:T(8,128)(2,1)S(1)}, bf16[64,8,256]{2,1,0:T(8,128)(2,1)S(1)}, u32[]{:S(2)}, u32[]{:S(2)}) collective-permute-start(bf16[64,8,256]{2,1,0:T(8,128)(2,1)S(1)} %get-tuple-element.16), channel_id=1, source_target_pairs={{0,1},{1,2},{2,3},{3,4},{4,5},{5,6},{6,7},{7,8},{8,9},{9,10},{10,1... | collective-permute-start | bytes 786440 | tf_op jit(solution)/shard_map/ppermute | solution.py:378
  4.5 10.4 %collective-permute-start.1 = (bf16[64,8,256]{2,1,0:T(8,128)(2,1)S(1)}, bf16[64,8,256]{2,1,0:T(8,128)(2,1)S(1)}, u32[]{:S(2)}, u32[]{:S(2)}) collective-permute-start(bf16[64,8,256]{2,1,0:T(8,128)(2,1)S(1)} %get-tuple-element.17), channel_id=1, source_target_pairs={{0,31},{1,0},{2,1},{3,2},{4,3},{5,4},{6,5},{7,6},{8,7},{9,8},{10,9... | collective-permute-start | bytes 786440 | tf_op jit(solution)/shard_map/ppermute | solution.py:377
  14.9 1.1 copy-start.1
  15.9 1.1 copy-start.3
  17.0 0.8 copy-start.10
  17.8 15.2 %copy-start.5 = (bf16[3,3,256,256]{3,2,1,0:T(8,128)(2,1)S(1)}, bf16[3,3,256,256]{3,2,1,0:T(8,128)(2,1)}, u32[]{:S(2)}) copy-start(bf16[3,3,256,256]{3,2,1,0:T(8,128)(2,1)} %param.12) | copy-start | bytes 3538948
  17.8 15.2 %copy-start.11 = (bf16[128,832]{1,0:T(8,128)(2,1)S(1)}, bf16[128,832]{1,0:T(8,128)(2,1)}, u32[]{:S(2)}) copy-start(bf16[128,832]{1,0:T(8,128)(2,1)} %constant.25.clone.down_ref) | copy-start | bytes 638980
  18.7 0.9 copy-start.7
  19.6 0.6 copy-start.13
  20.3 0.6 copy-start.15
  20.9 9.5 %collective-permute-start.2 = (bf16[304,256]{1,0:T(8,128)(2,1)}, bf16[304,256]{1,0:T(8,128)(2,1)S(1)}, u32[]{:S(2)}, u32[]{:S(2)}) collective-permute-start(bf16[304,256]{1,0:T(8,128)(2,1)} %get-tuple-element.22), channel_id=1, source_target_pairs={{0,32},{32,64},{64,96},{96,128},{128,160},{160,192},{192,224},{224... | collective-permute-start | bytes 466952 | tf_op jit(solution)/shard_map/ppermute | solution.py:387
  23.6 9.4 %collective-permute-start.3 = (bf16[304,256]{1,0:T(8,128)(2,1)}, bf16[304,256]{1,0:T(8,128)(2,1)}, u32[]{:S(2)}, u32[]{:S(2)}) collective-permute-start(bf16[304,256]{1,0:T(8,128)(2,1)} %get-tuple-element.23), channel_id=1, source_target_pairs={{0,224},{32,0},{64,32},{96,64},{128,96},{160,128},{192,160},{224,1... | collective-permute-start | bytes 466952 | tf_op jit(solution)/shard_map/ppermute | solution.py:386
  33.0 1.3 %copy-start.6 = (bf16[3,3,256,256]{3,2,1,0:T(8,128)(2,1)S(1)}, bf16[3,3,256,256]{3,2,1,0:T(8,128)(2,1)}, u32[]{:S(2)}) copy-start(bf16[3,3,256,256]{3,2,1,0:T(8,128)(2,1)} %param.13) | copy-start | bytes 3538948
  34.3 1.1 %copy-start.8 = (bf16[1536,256]{1,0:T(8,128)(2,1)S(1)}, bf16[1536,256]{1,0:T(8,128)(2,1)}, u32[]{:S(2)}) copy-start(bf16[1536,256]{1,0:T(8,128)(2,1)} %copy-done.7) | copy-start | bytes 2359300
  35.4 0.9 copy-start.12
  36.4 0.9 copy-start.14
  37.3 0.8 copy-start.16
  55.5 3.9 %collective-permute-start.4 = (bf16[3584,256]{1,0:T(8,128)(2,1)S(1)}, bf16[3584,256]{1,0:T(8,128)(2,1)S(1)}, u32[]{:S(2)}, u32[]{:S(2)}) collective-permute-start(bf16[3584,256]{1,0:T(8,128)(2,1)S(1)} %get-tuple-element.25), channel_id=1, source_target_pairs={{0,1},{1,0},{2,3},{3,2},{4,5},{5,4},{6,7},{7,6},{8,9},{9,8},{10,11... | collective-permute-start | bytes 5505032 | tf_op jit(solution)/shard_map/ppermute | solution.py:415

commit v3 on v2

v3 whole, which is shorter than its diff:
```python
import jax
import jax.numpy as jnp
from jax import lax
from jax.experimental import pallas as pl
from jax.experimental.pallas import tpu as pltpu
from jax.sharding import Mesh, PartitionSpec as P

F32 = jnp.float32
BF16 = jnp.bfloat16
C = 256
H, W = 48, 24
LH, LW = 16, 8
WW = 32
LWW = 16
LAT = ("yh", "yl", "xh")
LON = ("zh", "zm", "zl", "xl", "core")
SCALE = 2.0 / (H * W * H * W)
NINTH = 1.0 / 9.0
PK = 304
PAD = 8
MIB = 1024 * 1024
FULL = 60 * 1024 * 1024
MAIN_LIMIT = 64 * MIB - 12_000_000
VMEM = pl.BlockSpec(memory_space=pltpu.VMEM)
SMEM = pl.BlockSpec(memory_space=pltpu.SMEM)
HBM = pl.BlockSpec(memory_space=pltpu.HBM)


def up_matrix():
    def weight(m, r, cell):
        return jnp.where(
            r == 1,
            jnp.where(cell == m, 3.0, 0.0),
            jnp.where(cell == m, 2.0, jnp.where(cell == m + r - 1, 1.0, 0.0)),
        )

    p = lax.broadcasted_iota(jnp.int32, (18 * WW, 8 * LWW), 0)
    q = lax.broadcasted_iota(jnp.int32, (18 * WW, 8 * LWW), 1)
    i, j = p // WW, p % WW + 2
    e, f = q // LWW, q % LWW
    return (weight(i // 3 + 1, i % 3, e) * weight(j // 3 + 1, j % 3, f)).astype(BF16)


def down_matrix():
    def weight(tap):
        return jnp.maximum(3 - jnp.abs(tap - 2), 0).astype(F32)

    p = lax.broadcasted_iota(jnp.int32, (8 * LWW, 26 * WW), 0)
    q = lax.broadcasted_iota(jnp.int32, (8 * LWW, 26 * WW), 1)
    m, f = p // LWW, p % LWW - 3
    d, j = q // WW, q % WW - 3
    return jnp.where((f >= 0) & (f < LW), weight(d - 3 * m) * weight(j - 3 * f), 0.0).astype(BF16)


def pack_lon(land_ref, hi_ref, tgt_ref, low_ref, west_ref, east_ref, edge_ref, hi_v, tgt_v, low_v, sem):
    copies = [
        pltpu.make_async_copy(src.at[:, pl.ds(start, 8), :], dst.at[side], sem.at[2 * n + side])
        for n, (src, dst) in enumerate(((hi_ref, hi_v), (tgt_ref, tgt_v)))
        for side, start in enumerate((0, 16))
    ]
    copies.append(pltpu.make_async_copy(low_ref, low_v, sem.at[4]))
    for side in range(2):
        copies.append(pltpu.make_async_copy(hi_ref.at[pl.ds(44 * side, 4)], edge_ref.at[side, 0:4], sem.at[5 + side]))
        copies.append(pltpu.make_async_copy(tgt_ref.at[pl.ds(46 * side, 2)], edge_ref.at[side, 4:6], sem.at[7 + side]))
    for copy in copies:
        copy.start()
    land = land_ref[0, 0]
    sub = lax.broadcasted_iota(jnp.int32, (H, 8, C), 1)
    land_a = (land // 32).astype(F32)
    land_b = (land % 32).astype(F32)
    lands = jnp.where(sub == 6, land_a, land_b)
    for copy in copies:
        copy.wait()
    west = jnp.where(
        sub < 4, hi_v[0].astype(F32), jnp.where(sub < 6, pltpu.roll(tgt_v[0].astype(F32), 4, 1), lands)
    )
    east = jnp.where(
        sub < 4,
        pltpu.roll(hi_v[1].astype(F32), 4, 1),
        jnp.where(sub < 6, pltpu.roll(tgt_v[1].astype(F32), 6, 1), lands),
    )
    west_ref[0:H] = west.astype(BF16)
    east_ref[0:H] = east.astype(BF16)
    west_ref[H:] = low_v[...]
    east_ref[H:] = low_v[...]
    for side in range(2):
        edge_ref[side, 6] = low_v[13 * side : 13 * side + 3].astype(F32).reshape(24, C).astype(BF16)


def widen_pixels(own, left, right):
    turned = [pltpu.roll(own[:, 8 * g : 8 * g + 8], 4, 1) for g in range(3)]
    parts = [left] + turned + [right]
    low_half = lax.broadcasted_iota(jnp.int32, left.shape, 1) < 4
    return jnp.concatenate([jnp.where(low_half, parts[g], parts[g + 1]) for g in range(4)], axis=1)


def widen_hi(own, wpk, epk):
    return widen_pixels(own, wpk, pltpu.roll(epk, 4, 1))


def widen_tgt(own, wpk, epk):
    return widen_pixels(own, pltpu.roll(wpk, 6, 1), epk)


def widen_low(own, w_low, e_low):
    own, w_low, e_low = (pltpu.roll(v, 3, 1) for v in (own, w_low, e_low))
    head = lax.broadcasted_iota(jnp.int32, own.shape, 1) < 3
    return jnp.concatenate([jnp.where(head, w_low, own), jnp.where(head, own, e_low)], axis=1)


def land_row(part, own, wpk, epk):
    col = lax.broadcasted_iota(jnp.int32, (WW, C), 0)
    left = wpk[0, part : part + 1, :]
    right = epk[0, part : part + 1, :]
    return jnp.where(col < 4, left, jnp.where(col < 4 + W, own, right))


def pack_lat(land_ref, own_ref, w_ref, e_ref, north_ref, south_ref):
    land = land_ref[0, 0]
    wpk = w_ref[0:1].astype(F32)
    epk = e_ref[0:1].astype(F32)
    lands = jnp.concatenate(
        [
            land_row(6, (land // 32).astype(F32), wpk, epk),
            land_row(7, (land % 32).astype(F32), wpk, epk),
        ],
        axis=0,
    ).astype(BF16)
    for side, out_ref in enumerate((north_ref, south_ref)):
        def edge(ref, depth, size, base=0):
            start = base + (size - depth) * side
            return ref[start : start + depth].astype(F32)

        own = own_ref[side].astype(F32)
        hi = widen_hi(own[0:4], edge(w_ref, 4, H), edge(e_ref, 4, H))
        tgt = widen_tgt(own[4:6], edge(w_ref, 2, H), edge(e_ref, 2, H))
        low = widen_low(own[6].reshape(3, 8, C), edge(w_ref, 3, LH, H), edge(e_ref, 3, LH, H))
        out_ref[0:128] = hi.reshape(128, C).astype(BF16)
        out_ref[128:192] = tgt.reshape(64, C).astype(BF16)
        out_ref[192:240] = low.reshape(48, C).astype(BF16)
        out_ref[240:304] = lands


def main(
    pos_ref, land_ref, hi_hbm, tgt_hbm, low_hbm, w_ref, e_ref, n_ref, s_ref, kh_hbm, kl_hbm, kj_hbm,
    keep_ref, send_ref,
    x3_ref, j3_ref, o3_ref, l3_ref, f_ref, ha_ref, la_ref, jg_ref, og_ref, lg_ref, tg_ref, kt_ref, g_ref, up_ref,
    hi_v, tgt_v, low_v, kh_ref, kl_ref, kj_ref, sem, keep_sem,
):
    fetch = [
        pltpu.make_async_copy(src, dst, sem.at[n])
        for n, (src, dst) in enumerate(
            (
                (low_hbm, low_v),
                (kl_hbm, kl_ref),
                (hi_hbm, hi_v),
                (kh_hbm, kh_ref),
                (tgt_hbm, tgt_v),
                (kj_hbm, kj_ref),
            )
        )
    ]
    for copy in fetch:
        copy.start()
    fetch_low, fetch_kl, fetch_hi, fetch_kh, fetch_tgt, fetch_kj = fetch
    lat = pos_ref[0]
    core = pos_ref[1]
    first = lat == 0
    last = lat == 7

    def spread(dst, count, step):
        def one(t, _):
            s = pl.multiple_of(t * step, 16)
            v = f_ref[pl.ds(s, step + 2 * PAD), :]
            dst[pl.ds(s, step), 0:C] = v[PAD - 1 : PAD - 1 + step].astype(BF16)
            dst[pl.ds(s, step), C : 2 * C] = v[PAD : PAD + step].astype(BF16)
            dst[pl.ds(s, step), 2 * C : 3 * C] = v[PAD + 1 : PAD + 1 + step].astype(BF16)
            return 0

        lax.fori_loop(0, count // step, one, 0)

    def window(src, start, rows, stride):
        return jnp.concatenate(
            [src[pl.ds(pl.multiple_of(start + d * stride, 16), rows), :] for d in range(3)], axis=1
        )

    def zero_rows(start, rows):
        f_ref[PAD + start : PAD + start + rows, :] = jnp.zeros((rows, C), F32)

    f_ref[0:PAD, :] = jnp.zeros((PAD, C), F32)
    f_ref[PAD + 56 * WW :, :] = jnp.zeros((PAD, C), F32)
    f_ref[PAD : PAD + 48, :] = n_ref[192:240, :].astype(F32)
    fetch_low.wait()
    f_ref[PAD + 48 : PAD + 304, :] = widen_low(
        low_v[...].astype(F32), w_ref[H:].astype(F32), e_ref[H:].astype(F32)
    ).reshape(256, C)
    f_ref[PAD + 304 : PAD + 352, :] = s_ref[192:240, :].astype(F32)
    f_ref[PAD + 352 : PAD + 368, :] = jnp.zeros((16, C), F32)

    @pl.when(first)
    def _():
        zero_rows(0, 48)

    @pl.when(last)
    def _():
        zero_rows(304, 48)

    spread(l3_ref, 352, 176)
    fetch_kl.wait()
    low_act = jnp.maximum(
        jnp.dot(window(l3_ref, 0, 320, LWW), kl_ref[...], preferred_element_type=F32), 0.0
    ).astype(BF16)
    la_ref[...] = low_act

    @pl.when(first)
    def _():
        la_ref[0:32, :] = jnp.zeros((32, C), BF16)

    @pl.when(last)
    def _():
        la_ref[288:320, :] = jnp.zeros((32, C), BF16)

    f_ref[PAD : PAD + 128, :] = n_ref[0:128, :].astype(F32)
    f_ref[PAD + 1664 : PAD + 1792, :] = s_ref[0:128, :].astype(F32)

    fetch_hi.wait()

    def widen_rows(t, _):
        rows = pl.ds(pl.multiple_of(t * 8, 8), 8)
        wide = widen_hi(hi_v[rows].astype(F32), w_ref[rows].astype(F32), e_ref[rows].astype(F32))
        f_ref[pl.ds(pl.multiple_of(PAD + 128 + t * 256, 8), 256), :] = wide.reshape(256, C)
        return 0

    lax.fori_loop(0, 6, widen_rows, 0)

    @pl.when(first)
    def _():
        zero_rows(0, 128)

    @pl.when(last)
    def _():
        zero_rows(1664, 128)

    spread(x3_ref, 1792, 256)
    up_ref[...] = up_matrix()
    fetch_kh.wait()

    def high(b, _):
        s = pl.multiple_of(b * 576, 64)
        act = jnp.maximum(
            jnp.dot(window(x3_ref, s, 576, WW), kh_ref[...], preferred_element_type=F32), 0.0
        ).astype(BF16)
        ha_ref[pl.ds(s, 576), :] = act
        cells = la_ref[pl.ds(pl.multiple_of(b * 96, 32), 128), :]
        lift = jnp.dot(up_ref[...], cells, preferred_element_type=F32) * NINTH
        f_ref[pl.ds(PAD + s, 576), :] = act.astype(F32) + lift
        return 0

    lax.fori_loop(0, 3, high, 0)

    @pl.when(first)
    def _():
        zero_rows(0, 96)

    @pl.when(last)
    def _():
        zero_rows(51 * WW, 96)

    spread(j3_ref, 1728, 288)
    tg_ref[0:64, :] = n_ref[128:192, :]
    tg_ref[1600:1664, :] = s_ref[128:192, :]

    fetch_tgt.wait()

    def widen_targets(t, _):
        rows = pl.ds(pl.multiple_of(t * 8, 8), 8)
        wide = widen_tgt(tgt_v[rows].astype(F32), w_ref[rows].astype(F32), e_ref[rows].astype(F32))
        tg_ref[pl.ds(pl.multiple_of(64 + t * 256, 64), 256), :] = wide.reshape(256, C).astype(BF16)
        return 0

    lax.fori_loop(0, 6, widen_targets, 0)
    fetch_kj.wait()
    for tap in range(9):
        kt_ref[(8 - tap) * C : (9 - tap) * C, :] = kj_ref[tap * C : (tap + 1) * C, :].T

    def weight_of(ref, base):
        return (ref[base : base + 32, :].astype(F32) * 32.0 + ref[base + 32 : base + 64, :].astype(F32)) * SCALE

    top = weight_of(n_ref, 240)[None]
    own = land_ref[0, 0]
    wland = w_ref[0:1].astype(F32)
    eland = e_ref[0:1].astype(F32)
    mid_a = land_row(6, (own // 32).astype(F32), wland, eland)
    mid_b = land_row(7, (own % 32).astype(F32), wland, eland)
    mid = ((mid_a * 32.0 + mid_b) * SCALE)[None]
    bot = weight_of(s_ref, 240)[None]

    def join(b, _):
        s = pl.multiple_of(b * 416, 32)
        y = jnp.dot(window(j3_ref, s, 416, WW), kj_ref[...], preferred_element_type=F32)
        diff = (y - tg_ref[pl.ds(s, 416), :].astype(F32)).reshape(13, WW, C)
        row = lax.broadcasted_iota(jnp.int32, (13, WW, C), 0) + b * 13
        weight = jnp.where(row < 2, top, jnp.where(row >= 50, bot, mid))
        f_ref[pl.ds(PAD + s, 416), :] = (weight * diff).reshape(416, C)
        return 0

    lax.fori_loop(0, 4, join, 0)

    @pl.when(first)
    def _():
        zero_rows(0, 64)

    @pl.when(last)
    def _():
        zero_rows(50 * WW, 64)

    spread(o3_ref, 1664, 416)

    def own_columns(rows):
        col = lax.broadcasted_iota(jnp.int32, (rows // WW, WW, C), 1).reshape(rows, C)
        return (col >= 4) & (col < 4 + W)

    def contract(x_ref, g_val, base, stride, rows, slot):
        for d in range(3):
            g_ref[slot, d * 768 : (d + 1) * 768, :] = lax.dot_general(
                x_ref[base + d * stride : base + d * stride + rows, :],
                g_val,
                (((0,), (0,)), ((), ())),
                preferred_element_type=F32,
            )

        def one(t, _):
            pltpu.make_async_copy(
                g_ref.at[slot, pl.ds(block_start(t, core), 72)],
                keep_ref.at[pl.ds(pl.multiple_of(t * 224 + slot * 72, 8), 72)],
                keep_sem.at[slot],
            ).start()
            return 0

        lax.fori_loop(0, 16, one, 0)

    def block_start(t, half):
        return pl.multiple_of((t % 8 * 4 + t // 8 * 2 + half) * 72, 8)

    def own_grad(t, _):
        s = pl.multiple_of(t * 256, 64)
        v = f_ref[pl.ds(PAD + 64 + s, 256), :]
        og_ref[pl.ds(s, 256), :] = jnp.where(own_columns(256), v, 0.0).astype(BF16)
        return 0

    lax.fori_loop(0, 6, own_grad, 0)
    contract(j3_ref, og_ref[...], 64, WW, 1536, 2)

    def back(b, _):
        s = pl.multiple_of(b * 320, 32)
        y = jnp.dot(window(o3_ref, s, 320, WW), kt_ref[...], preferred_element_type=F32)
        jg_ref[pl.ds(s, 320), :] = y.astype(BF16)
        return 0

    lax.fori_loop(0, 5, back, 0)

    @pl.when(first)
    def _():
        jg_ref[0:32, :] = jnp.zeros((32, C), BF16)

    @pl.when(last)
    def _():
        jg_ref[49 * WW :, :] = jnp.zeros((32, C), BF16)

    def high_grad(t, _):
        s = pl.multiple_of(t * 256, 64)
        v = jg_ref[pl.ds(s + 32, 256), :].astype(F32)
        on = ha_ref[pl.ds(s + 96, 256), :].astype(F32) > 0
        og_ref[pl.ds(s, 256), :] = jnp.where(own_columns(256) & on, v, 0.0).astype(BF16)
        return 0

    lax.fori_loop(0, 6, high_grad, 0)
    contract(x3_ref, og_ref[...], 96, WW, 1536, 0)

    down = down_matrix()
    for b in range(2):
        lifted = jnp.dot(down, jg_ref[b * 768 : b * 768 + 832, :], preferred_element_type=F32) * NINTH
        on = la_ref[32 + b * 128 : 160 + b * 128, :].astype(F32) > 0
        lg_ref[b * 128 : (b + 1) * 128, :] = jnp.where(on, lifted, 0.0).astype(BF16)
    contract(l3_ref, lg_ref[...], 32, LWW, 256, 1)

    def split(t, _):
        src = block_start(t, 1 - core)
        block = jnp.concatenate(
            [g_ref[g, pl.ds(src, 72), :] for g in range(3)] + [jnp.zeros((8, C), F32)], axis=0
        )
        send_ref[pl.ds(pl.multiple_of(t * 224, 32), 224), :] = block.astype(BF16)
        return 0

    lax.fori_loop(0, 16, split, 0)
    for g in range(3):
        pltpu.make_async_copy(g_ref.at[g, 0:1152], keep_ref.at[0:1152], keep_sem.at[g]).wait()


def regroup_lanes(parts, rows):
    quarter = lax.broadcasted_iota(jnp.int32, (rows, 128), 1) // 32
    for q in range(4):
        out = None
        for g in range(4):
            shift = ((g - q) * 32) % 128
            turned = pltpu.roll(parts[g], shift, 1) if shift else parts[g]
            out = turned if out is None else jnp.where(quarter == g, turned, out)
        yield q, out


def merge(keep_ref, recv_ref, out_ref):
    def one(t, _):
        xl = t // 8
        z = t % 8
        s = pl.multiple_of(t * 224, 32)
        v = keep_ref[pl.ds(s, 224), :] + recv_ref[pl.ds(s, 224), :].astype(F32)
        for h in range(2):
            parts = [v[g * 56 : (g + 1) * 56, h * 128 : (h + 1) * 128] for g in range(4)]
            for q, out in regroup_lanes(parts, 56):
                out_ref[(h * 4 + q) * 2 + xl, z] = out.astype(BF16)
        return 0

    lax.fori_loop(0, 16, one, 0)


def total(in_ref, out_ref):
    def one(z, _):
        acc = in_ref[0, z].astype(F32)
        for i in range(1, 16):
            acc = acc + in_ref[i, z].astype(F32)
        out_ref[z] = acc.astype(out_ref.dtype)
        return 0

    lax.fori_loop(0, 8, one, 0)


def finish(in_ref, a_ref, b_ref, c_ref):
    acc = in_ref[0].astype(F32)
    for i in range(1, 8):
        acc = acc + in_ref[i].astype(F32)
    rows = jnp.concatenate(
        [acc if s == 0 else pltpu.roll(acc, 128 - 32 * s, 1) for s in range(4)], axis=0
    )
    for g, ref in enumerate((a_ref, b_ref, c_ref)):
        ref[...] = rows[g * 72 : (g + 1) * 72].T[0:32]


def call(kernel, out, specs, scratch=(), outs=None, name=None, vmem=None):
    return pl.pallas_call(
        kernel,
        out_shape=tuple(jax.ShapeDtypeStruct(s, d) for s, d in out),
        in_specs=list(specs),
        out_specs=outs or tuple(VMEM for _ in out),
        scratch_shapes=list(scratch),
        name=name,
        compiler_params=pltpu.CompilerParams(vmem_limit_bytes=vmem) if vmem else None,
    )


def ring(count, step):
    return [(i, (i + step) % count) for i in range(count)]


XY = ("yh", "yl", "xh", "xl")
Z = ("zh", "zm", "zl")


def body(hi, low, kh, kl, kj, tgt, land):
    dma = pltpu.SemaphoreType.DMA
    west, east, edges = call(
        pack_lon,
        [((H + LH, 8, C), BF16)] * 2 + [((2, 7, W, C), BF16)],
        [SMEM] + [HBM] * 3,
        [pltpu.VMEM((2, H, 8, C), BF16), pltpu.VMEM((2, H, 8, C), BF16), pltpu.VMEM((LH, LW, C), BF16), dma((9,))],
        name="pack_lon",
        vmem=FULL,
    )(land, hi, tgt, low)
    from_e = lax.ppermute(west, LON, ring(32, -1))
    from_w = lax.ppermute(east, LON, ring(32, 1))
    north, south = call(
        pack_lat, [((PK, C), BF16)] * 2, [SMEM] + [VMEM] * 3, name="pack_lat", vmem=6 * MIB
    )(land, edges, from_w, from_e)
    from_s = lax.ppermute(north, LAT, ring(8, -1))
    from_n = lax.ppermute(south, LAT, ring(8, 1))
    pos = jnp.stack([lax.axis_index(LAT), lax.axis_index("core")]).astype(jnp.int32)
    keep, send = call(
        main,
        [((3584, C), F32), ((3584, C), BF16)],
        [SMEM] * 2 + [HBM] * 3 + [VMEM] * 4 + [HBM] * 3,
        [
            pltpu.VMEM((1792, 768), BF16),
            pltpu.VMEM((1728, 768), BF16),
            pltpu.VMEM((1664, 768), BF16),
            pltpu.VMEM((352, 768), BF16),
            pltpu.VMEM((1792 + 2 * PAD, C), F32),
            pltpu.VMEM((1728, C), BF16),
            pltpu.VMEM((320, C), BF16),
            pltpu.VMEM((1600, C), BF16),
            pltpu.VMEM((1536, C), BF16),
            pltpu.VMEM((256, C), BF16),
            pltpu.VMEM((1664, C), BF16),
            pltpu.VMEM((2304, C), BF16),
            pltpu.VMEM((3, 2304, C), F32),
            pltpu.VMEM((576, 128), BF16),
            pltpu.VMEM((H, W, C), BF16),
            pltpu.VMEM((H, W, C), BF16),
            pltpu.VMEM((LH, LW, C), BF16),
            pltpu.VMEM((2304, C), BF16),
            pltpu.VMEM((2304, C), BF16),
            pltpu.VMEM((2304, C), BF16),
            dma((6,)),
            dma((3,)),
        ],
        outs=(HBM, VMEM),
        name="main",
        vmem=MAIN_LIMIT,
    )(
        pos, land, hi, tgt, low, from_w, from_e, from_n, from_s,
        kh.reshape(9 * C, C), kl.reshape(9 * C, C), kj.reshape(9 * C, C),
    )
    recv = lax.ppermute(send, "core", ring(2, 1))
    (parts,) = call(merge, [((16, 8, 56, 128), BF16)], [VMEM] * 2, name="merge", vmem=12 * MIB)(keep, recv)
    parts = lax.all_to_all(parts, XY, 0, 0, tiled=True)
    (parts,) = call(total, [((8, 56, 128), F32)], [VMEM], name="total", vmem=6 * MIB)(parts)
    parts = lax.all_to_all(parts, Z, 0, 0, tiled=True)
    grads = call(finish, [((32, 72), F32)] * 3, [VMEM], name="finish", vmem=2 * MIB)(parts)
    return tuple(g.T for g in grads)


def solution(mesh):
    fine = Mesh(mesh.devices.reshape((2,) * 8), LAT + LON)
    tile = P(LAT, LON, None)
    return jax.shard_map(
        body,
        mesh=fine,
        in_specs=(tile, tile, P(), P(), P(), tile, P(LAT, LON)),
        out_specs=(P(LON, LAT),) * 3,
        check_vma=False,
    )
```

time: 112 us -> 108 us (0.964)
  local copies, waits for them, and re-layouts: 13 us -> 2.96 us
  Pallas kernels: 22.3 us -> 28.6 us
    unnamed x34 -> x6, local copies, waits for them, and re-layouts: 13 us -> 2.96 us
    pallas_call x3, Pallas kernels: 18.5 us -> 25 us  [the longest x1 22.6 us: body(): call(main, [((3584, C), F32), ((3584, C), BF16)], [SMEM] * 2 + [HBM] * 3...]
where the time goes in v3:
time: 108 us; the launch traced here: 107 us
  blocking collectives  47.1 us (44%)
  Pallas kernels  28.6 us (26%)
  waiting for transfers between devices  15.6 us (14%)
  starting transfers between devices  11 us (10%)
  local copies, waits for them, and re-layouts  2.96 us (3%)
  between operations  1.37 us (1%)
    all_to_all x1, blocking collectives, body(): parts = lax.all_to_all(parts, XY, 0, 0, tiled=True)  30.5 us
    pallas_call x1, Pallas kernels, body(): call(main, [((3584, C), F32), ((3584, C), BF16)], [SMEM] * 2 + [HBM] * 3...  22.6 us
    all_to_all x1, blocking collectives, body(): parts = lax.all_to_all(parts, Z, 0, 0, tiled=True)  16.5 us
    ppermute x1, starting transfers between devices, body(): from_e = lax.ppermute(west, LON, ring(32, -1))  6.3 us
    ppermute x1, waiting for transfers between devices, body(): from_n = lax.ppermute(south, LAT, ring(8, 1))  4.8 us
    ppermute x1, waiting for transfers between devices, body(): from_w = lax.ppermute(east, LON, ring(32, 1))  4.28 us
    ppermute x1, waiting for transfers between devices, body(): recv = lax.ppermute(send, 'core', ring(2, 1))  3.98 us
    unnamed x6, local copies, waits for them, and re-layouts  2.96 us
  transfers between devices with their start and end apart: 5, of which 4 were waited for; matrix products, arithmetic and copies ran while one was open for 0% of the time, Pallas kernels for 0%

profile of v3, /device:TPU:8, one launch (start us, length us, event | category | flops | bytes accessed | tf_op | source)
XLA Modules:
  0.0 106.7 jit_solution(15808372400347088182)
XLA Ops:
  0.6 0.0 copy-start.1
  1.3 2.3 %pack_lon.1 = (bf16[64,8,256]{2,1,0:T(8,128)(2,1)}, bf16[64,8,256]{2,1,0:T(8,128)(2,1)}, bf16[2,7,24,256]{3,2,1,0:T(8,128)(2,1)}) custom-call(s32[1,1]{1,0:T(1,128)S(6)} %copy.10.land_ref, bf16[48,24,256]{2,1,0:T(8,128)(2,1)} %hi_hbm.1, bf16[48,24,256]{2,1,0:T(8,128)(2,1)} %tgt_hbm.1, bf16[16,8,256]{2,1,0:T(8,128)(2,1)} %low_hbm.1), custom_call_target="tpu_custom_call" | custom-call | tf_op jit(solution)/shard_map/pack_lon/pallas_call | solution.py:470
  3.6 0.1 collective-permute-start
  3.7 6.3 %collective-permute-start.1 = (bf16[64,8,256]{2,1,0:T(8,128)(2,1)}, bf16[64,8,256]{2,1,0:T(8,128)(2,1)S(1)}, u32[]{:S(2)}, u32[]{:S(2)}) collective-permute-start(bf16[64,8,256]{2,1,0:T(8,128)(2,1)} %get-tuple-element.14), channel_id=1, source_target_pairs={{0,31},{1,0},{2,1},{3,2},{4,3},{5,4},{6,5},{7,6},{8,7},{9,8},{10,9... | collective-permute-start | bytes 786440 | tf_op jit(solution)/shard_map/ppermute | solution.py:478
  10.0 4.3 %collective-permute-done.w_ref = bf16[64,8,256]{2,1,0:T(8,128)(2,1)S(1)} collective-permute-done((bf16[64,8,256]{2,1,0:T(8,128)(2,1)}, bf16[64,8,256]{2,1,0:T(8,128)(2,1)S(1)}, u32[]{:S(2)}, u32[]{:S(2)}) %collective-permute-start) | collective-permute-done | bytes 262176 | tf_op jit(solution)/shard_map/ppermute | solution.py:479
  14.3 0.0 collective-permute-done.1.e_ref
  14.3 0.0 copy-start.2
  14.3 0.9 copy-done.2
  15.2 0.1 pack_lat.1
  15.3 2.8 %collective-permute-start.2 = (bf16[304,256]{1,0:T(8,128)(2,1)S(1)}, bf16[304,256]{1,0:T(8,128)(2,1)S(1)}, u32[]{:S(2)}, u32[]{:S(2)}) collective-permute-start(bf16[304,256]{1,0:T(8,128)(2,1)S(1)} %get-tuple-element.16), channel_id=1, source_target_pairs={{0,32},{32,64},{64,96},{96,128},{128,160},{160,192},{192,224},{224... | collective-permute-start | bytes 466952 | tf_op jit(solution)/shard_map/ppermute | solution.py:484
  18.1 1.7 %collective-permute-start.3 = (bf16[304,256]{1,0:T(8,128)(2,1)S(1)}, bf16[304,256]{1,0:T(8,128)(2,1)S(1)}, u32[]{:S(2)}, u32[]{:S(2)}) collective-permute-start(bf16[304,256]{1,0:T(8,128)(2,1)S(1)} %get-tuple-element.17), channel_id=1, source_target_pairs={{0,224},{32,0},{64,32},{96,64},{128,96},{160,128},{192,160},{224,1... | collective-permute-start | bytes 466952 | tf_op jit(solution)/shard_map/ppermute | solution.py:483
  19.8 0.1 pad_add_fusion.pos_ref
  19.8 4.8 %collective-permute-done.2.n_ref = bf16[304,256]{1,0:T(8,128)(2,1)S(1)} collective-permute-done((bf16[304,256]{1,0:T(8,128)(2,1)S(1)}, bf16[304,256]{1,0:T(8,128)(2,1)S(1)}, u32[]{:S(2)}, u32[]{:S(2)}) %collective-permute-start.2) | collective-permute-done | bytes 155680 | tf_op jit(solution)/shard_map/ppermute | solution.py:484
  24.6 2.5 %collective-permute-done.3.s_ref = bf16[304,256]{1,0:T(8,128)(2,1)S(1)} collective-permute-done((bf16[304,256]{1,0:T(8,128)(2,1)S(1)}, bf16[304,256]{1,0:T(8,128)(2,1)S(1)}, u32[]{:S(2)}, u32[]{:S(2)}) %collective-permute-start.3) | collective-permute-done | bytes 155680 | tf_op jit(solution)/shard_map/ppermute | solution.py:483
  27.2 0.0 copy-done.1
  27.2 22.6 %main.1 = (f32[3584,256]{1,0:T(8,128)}, bf16[3584,256]{1,0:T(8,128)(2,1)}) custom-call(s32[2]{0:T(128)S(1)} %pad_add_fusion.pos_ref, s32[1,1]{1,0:T(1,128)S(6)} %copy.10.land_ref, bf16[48,24,256]{2,1,0:T(8,128)(2,1)} %hi_hbm.1, bf16[48,24,256]{2,1,0:T(8,128)(2,1)} %tgt_hbm.1, bf16[16,8,256]{2,1,0:T(8,128)(2,1)S(1)} %copy-done.1, ...), custom_call_target="tpu_custom_call" | custom-call | tf_op jit(solution)/shard_map/main/pallas_call | solution.py:486
  49.8 0.1 collective-permute-start.4
  49.9 4.0 %collective-permute-done.4.recv_ref = bf16[3584,256]{1,0:T(8,128)(2,1)S(1)} collective-permute-done((bf16[3584,256]{1,0:T(8,128)(2,1)}, bf16[3584,256]{1,0:T(8,128)(2,1)S(1)}, u32[]{:S(2)}, u32[]{:S(2)}) %collective-permute-start.4) | collective-permute-done | bytes 1835040 | tf_op jit(solution)/shard_map/ppermute | solution.py:521
  53.9 0.0 copy-start
  53.9 2.0 %copy-done = f32[3584,256]{1,0:T(8,128)S(1)} copy-done((f32[3584,256]{1,0:T(8,128)S(1)}, f32[3584,256]{1,0:T(8,128)}, u32[]{:S(2)}) %copy-start) | copy-done | bytes 3670040
  55.9 2.6 %merge.1 = bf16[16,8,56,128]{3,2,1,0:T(8,128)(2,1)S(1)} custom-call(f32[3584,256]{1,0:T(8,128)S(1)} %copy-done, bf16[3584,256]{1,0:T(8,128)(2,1)S(1)} %collective-permute-done.4.recv_ref), custom_call_target="tpu_custom_call" | custom-call | tf_op jit(solution)/shard_map/merge/pallas_call | solution.py:522
  58.5 30.5 %all_to_all.10.in_ref = bf16[16,8,56,128]{3,2,1,0:T(8,128)(2,1)S(1)} all-to-all(bf16[16,8,56,128]{3,2,1,0:T(8,128)(2,1)S(1)} %merge.1), channel_id=1, replica_groups=mesh['yh'=2,'yl'=2,'xh'=2,'zh'=2,'zm'=2,'zl'=2,'xl'=2,'core'=2] {'yh','y..., dimensions={0} | all-to-all | bytes 3670016 | tf_op jit(solution)/shard_map/all_to_all | solution.py:523
  89.1 0.3 total.1
  89.4 16.5 %all_to_all.11.in_ref = f32[8,56,128]{2,1,0:T(8,128)S(1)} all-to-all(f32[8,56,128]{2,1,0:T(8,128)S(1)} %total.1), channel_id=1, replica_groups=mesh['yh'=2,'yl'=2,'xh'=2,'zh'=2,'zm'=2,'zl'=2,'xl'=2,'core'=2] {'zh','z..., dimensions={0} | all-to-all | bytes 458752 | tf_op jit(solution)/shard_map/all_to_all | solution.py:525
  105.9 0.8 finish.1
Async XLA Ops:
  0.6 26.5 %copy-start.1 = (bf16[16,8,256]{2,1,0:T(8,128)(2,1)S(1)}, bf16[16,8,256]{2,1,0:T(8,128)(2,1)}, u32[]{:S(2)}) copy-start(bf16[16,8,256]{2,1,0:T(8,128)(2,1)} %low_hbm.1) | copy-start | bytes 196612
  3.6 10.7 %collective-permute-start = (bf16[64,8,256]{2,1,0:T(8,128)(2,1)}, bf16[64,8,256]{2,1,0:T(8,128)(2,1)S(1)}, u32[]{:S(2)}, u32[]{:S(2)}) collective-permute-start(bf16[64,8,256]{2,1,0:T(8,128)(2,1)} %get-tuple-element.13), channel_id=1, source_target_pairs={{0,1},{1,2},{2,3},{3,4},{4,5},{5,6},{6,7},{7,8},{8,9},{9,10},{10,1... | collective-permute-start | bytes 786440 | tf_op jit(solution)/shard_map/ppermute | solution.py:479
  3.7 10.6 %collective-permute-start.1 = (bf16[64,8,256]{2,1,0:T(8,128)(2,1)}, bf16[64,8,256]{2,1,0:T(8,128)(2,1)S(1)}, u32[]{:S(2)}, u32[]{:S(2)}) collective-permute-start(bf16[64,8,256]{2,1,0:T(8,128)(2,1)} %get-tuple-element.14), channel_id=1, source_target_pairs={{0,31},{1,0},{2,1},{3,2},{4,3},{5,4},{6,5},{7,6},{8,7},{9,8},{10,9... | collective-permute-start | bytes 786440 | tf_op jit(solution)/shard_map/ppermute | solution.py:478
  14.3 0.9 copy-start.2
  15.3 9.4 %collective-permute-start.2 = (bf16[304,256]{1,0:T(8,128)(2,1)S(1)}, bf16[304,256]{1,0:T(8,128)(2,1)S(1)}, u32[]{:S(2)}, u32[]{:S(2)}) collective-permute-start(bf16[304,256]{1,0:T(8,128)(2,1)S(1)} %get-tuple-element.16), channel_id=1, source_target_pairs={{0,32},{32,64},{64,96},{96,128},{128,160},{160,192},{192,224},{224... | collective-permute-start | bytes 466952 | tf_op jit(solution)/shard_map/ppermute | solution.py:484
  18.1 9.1 %collective-permute-start.3 = (bf16[304,256]{1,0:T(8,128)(2,1)S(1)}, bf16[304,256]{1,0:T(8,128)(2,1)S(1)}, u32[]{:S(2)}, u32[]{:S(2)}) collective-permute-start(bf16[304,256]{1,0:T(8,128)(2,1)S(1)} %get-tuple-element.17), channel_id=1, source_target_pairs={{0,224},{32,0},{64,32},{96,64},{128,96},{160,128},{192,160},{224,1... | collective-permute-start | bytes 466952 | tf_op jit(solution)/shard_map/ppermute | solution.py:483
  49.8 4.1 %collective-permute-start.4 = (bf16[3584,256]{1,0:T(8,128)(2,1)}, bf16[3584,256]{1,0:T(8,128)(2,1)S(1)}, u32[]{:S(2)}, u32[]{:S(2)}) collective-permute-start(bf16[3584,256]{1,0:T(8,128)(2,1)} %get-tuple-element.19), channel_id=1, source_target_pairs={{0,1},{1,0},{2,3},{3,2},{4,5},{5,4},{6,7},{7,6},{8,9},{9,8},{10,11... | collective-permute-start | bytes 5505032 | tf_op jit(solution)/shard_map/ppermute | solution.py:521
  53.9 2.0 %copy-start = (f32[3584,256]{1,0:T(8,128)S(1)}, f32[3584,256]{1,0:T(8,128)}, u32[]{:S(2)}) copy-start(f32[3584,256]{1,0:T(8,128)} %get-tuple-element.18.keep_ref) | copy-start | bytes 11010052

commit v4 on v3

v4 whole, which is shorter than its diff:
```python
import jax
import jax.numpy as jnp
from jax import lax
from jax.experimental import pallas as pl
from jax.experimental.pallas import tpu as pltpu
from jax.sharding import Mesh, PartitionSpec as P

F32 = jnp.float32
BF16 = jnp.bfloat16
C = 256
H, W = 48, 24
LH, LW = 16, 8
WW = 32
LWW = 16
LAT = ("yh", "yl", "xh")
LON = ("zh", "zm", "zl", "xl", "core")
SCALE = 2.0 / (H * W * H * W)
NINTH = 1.0 / 9.0
PK = 304
MIB = 1024 * 1024
FULL = 60 * 1024 * 1024
MAIN_LIMIT = 64 * MIB - 12_000_000
JOIN_LIMIT = 64 * MIB - 12_300_000
REST_LIMIT = 64 * MIB - 13_500_000
VMEM = pl.BlockSpec(memory_space=pltpu.VMEM)
SMEM = pl.BlockSpec(memory_space=pltpu.SMEM)
HBM = pl.BlockSpec(memory_space=pltpu.HBM)


def up_matrix():
    def weight(m, r, cell):
        side = jnp.where(cell == m, 2.0, jnp.where(cell == m + r - 1, 1.0, 0.0))
        return jnp.where(r == 1, jnp.where(cell == m, 3.0, 0.0), side)

    i = lax.broadcasted_iota(jnp.int32, (18, 1, 8 * LWW), 0)
    e = lax.broadcasted_iota(jnp.int32, (18, 1, 8 * LWW), 2) // LWW
    j = lax.broadcasted_iota(jnp.int32, (1, WW, 8 * LWW), 1) + 2
    f = lax.broadcasted_iota(jnp.int32, (1, WW, 8 * LWW), 2) % LWW
    both = weight(i // 3 + 1, i % 3, e) * weight(j // 3 + 1, j % 3, f)
    return both.reshape(18 * WW, 8 * LWW).astype(BF16)


def down_matrix():
    def weight(tap):
        return jnp.maximum(3 - jnp.abs(tap - 2), 0).astype(F32)

    m = lax.broadcasted_iota(jnp.int32, (8, 1, 26 * WW), 0)
    d = lax.broadcasted_iota(jnp.int32, (8, 1, 26 * WW), 2) // WW
    f = lax.broadcasted_iota(jnp.int32, (1, LWW, 26 * WW), 1) - 3
    j = lax.broadcasted_iota(jnp.int32, (1, LWW, 26 * WW), 2) % WW - 3
    both = weight(d - 3 * m) * jnp.where((f >= 0) & (f < LW), weight(j - 3 * f), 0.0)
    return both.reshape(8 * LWW, 26 * WW).astype(BF16)


def pack_lon(land_ref, hi_ref, tgt_ref, low_ref, west_ref, east_ref, edge_ref, hi_v, tgt_v, low_v, sem):
    copies = [
        pltpu.make_async_copy(src.at[:, pl.ds(start, 8), :], dst.at[side], sem.at[2 * n + side])
        for n, (src, dst) in enumerate(((hi_ref, hi_v), (tgt_ref, tgt_v)))
        for side, start in enumerate((0, 16))
    ]
    copies.append(pltpu.make_async_copy(low_ref, low_v, sem.at[4]))
    for side in range(2):
        copies.append(pltpu.make_async_copy(hi_ref.at[pl.ds(44 * side, 4)], edge_ref.at[side, 0:4], sem.at[5 + side]))
        copies.append(pltpu.make_async_copy(tgt_ref.at[pl.ds(46 * side, 2)], edge_ref.at[side, 4:6], sem.at[7 + side]))
    for copy in copies:
        copy.start()
    land = land_ref[0, 0]
    sub = lax.broadcasted_iota(jnp.int32, (H, 8, C), 1)
    land_a = (land // 32).astype(F32)
    land_b = (land % 32).astype(F32)
    lands = jnp.where(sub == 6, land_a, land_b)
    for copy in copies:
        copy.wait()
    west = jnp.where(
        sub < 4, hi_v[0].astype(F32), jnp.where(sub < 6, pltpu.roll(tgt_v[0].astype(F32), 4, 1), lands)
    )
    east = jnp.where(
        sub < 4,
        pltpu.roll(hi_v[1].astype(F32), 4, 1),
        jnp.where(sub < 6, pltpu.roll(tgt_v[1].astype(F32), 6, 1), lands),
    )
    west_ref[0:H] = west.astype(BF16)
    east_ref[0:H] = east.astype(BF16)
    west_ref[H:] = low_v[...]
    east_ref[H:] = low_v[...]
    for side in range(2):
        edge_ref[side, 6] = low_v[13 * side : 13 * side + 3].astype(F32).reshape(24, C).astype(BF16)


def widen_pixels(own, left, right):
    turned = [pltpu.roll(own[:, 8 * g : 8 * g + 8], 4, 1) for g in range(3)]
    parts = [left] + turned + [right]
    low_half = lax.broadcasted_iota(jnp.int32, left.shape, 1) < 4
    return jnp.concatenate([jnp.where(low_half, parts[g], parts[g + 1]) for g in range(4)], axis=1)


def widen_hi(own, wpk, epk):
    return widen_pixels(own, wpk, pltpu.roll(epk, 4, 1))


def widen_tgt(own, wpk, epk):
    return widen_pixels(own, pltpu.roll(wpk, 6, 1), epk)


def widen_low(own, w_low, e_low):
    own, w_low, e_low = (pltpu.roll(v, 3, 1) for v in (own, w_low, e_low))
    head = lax.broadcasted_iota(jnp.int32, own.shape, 1) < 3
    return jnp.concatenate([jnp.where(head, w_low, own), jnp.where(head, own, e_low)], axis=1)


def land_row(part, own, wpk, epk):
    col = lax.broadcasted_iota(jnp.int32, (WW, C), 0)
    left = wpk[0, part : part + 1, :]
    right = epk[0, part : part + 1, :]
    return jnp.where(col < 4, left, jnp.where(col < 4 + W, own, right))


def pack_lat(land_ref, own_ref, w_ref, e_ref, north_ref, south_ref):
    land = land_ref[0, 0]
    wpk = w_ref[0:1].astype(F32)
    epk = e_ref[0:1].astype(F32)
    lands = jnp.concatenate(
        [
            land_row(6, (land // 32).astype(F32), wpk, epk),
            land_row(7, (land % 32).astype(F32), wpk, epk),
        ],
        axis=0,
    ).astype(BF16)
    for side, out_ref in enumerate((north_ref, south_ref)):
        def edge(ref, depth, size, base=0):
            start = base + (size - depth) * side
            return ref[start : start + depth].astype(F32)

        own = own_ref[side].astype(F32)
        hi = widen_hi(own[0:4], edge(w_ref, 4, H), edge(e_ref, 4, H))
        tgt = widen_tgt(own[4:6], edge(w_ref, 2, H), edge(e_ref, 2, H))
        low = widen_low(own[6].reshape(3, 8, C), edge(w_ref, 3, LH, H), edge(e_ref, 3, LH, H))
        out_ref[0:128] = hi.reshape(128, C).astype(BF16)
        out_ref[128:192] = tgt.reshape(64, C).astype(BF16)
        out_ref[192:240] = low.reshape(48, C).astype(BF16)
        out_ref[240:304] = lands


def put3(dst, start, v):
    rows = v.shape[0]
    dst[pl.ds(start, rows), 0:C] = pltpu.roll(v, 1, 0).astype(BF16)
    dst[pl.ds(start, rows), C : 2 * C] = v.astype(BF16)
    dst[pl.ds(start, rows), 2 * C : 3 * C] = pltpu.roll(v, rows - 1, 0).astype(BF16)


def window(src, start, rows, stride):
    return jnp.concatenate(
        [src[pl.ds(pl.multiple_of(start + d * stride, 16), rows), :] for d in range(3)], axis=1
    )


def own_columns(rows):
    col = lax.broadcasted_iota(jnp.int32, (rows // WW, WW, C), 1).reshape(rows, C)
    return (col >= 4) & (col < 4 + W)


def zero_at(flag, ref, start, rows):
    @pl.when(flag)
    def _():
        ref[start : start + rows, :] = jnp.zeros((rows, ref.shape[1]), ref.dtype)


def contract(x_ref, g_val, base, stride, rows, out):
    for d in range(3):
        out[d * 768 : (d + 1) * 768, :] = lax.dot_general(
            x_ref[base + d * stride : base + d * stride + rows, :],
            g_val,
            (((0,), (0,)), ((), ())),
            preferred_element_type=F32,
        )


def block_start(t, half):
    return pl.multiple_of((t % 8 * 4 + t // 8 * 2 + half) * 72, 8)


def hand_out(g_ref, keep_ref, send_ref, core, sem):
    for t in range(16):
        pltpu.make_async_copy(g_ref.at[pl.ds(block_start(t, core), 72)], keep_ref.at[t], sem).start()

    def one(t, _):
        send_ref[t] = g_ref[pl.ds(block_start(t, 1 - core), 72), :].astype(BF16)
        return 0

    lax.fori_loop(0, 16, one, 0)


def wait_out(src, dst, sem):
    pltpu.make_async_copy(src, dst, sem).wait()


def forward(
    pos_ref, land_ref, hi_hbm, tgt_hbm, low_hbm, w_ref, e_ref, n_ref, s_ref, kh_hbm, kl_hbm, kj_hbm,
    keep_ref, send_ref, x3_hbm, o3_hbm, l3_hbm, ha_hbm, la_hbm,
    x3_ref, j3_ref, o3_ref, l3_ref, ha_ref, la_ref, og_ref, tg_ref, g_ref, up_ref,
    hi_v, tgt_v, low_v, kh_ref, kl_ref, kj_ref, sem, out_sem, keep_sem,
):
    fetch = [
        pltpu.make_async_copy(src, dst, sem.at[n])
        for n, (src, dst) in enumerate(
            (
                (low_hbm, low_v),
                (hi_hbm, hi_v),
                (kl_hbm, kl_ref),
                (kh_hbm, kh_ref),
                (tgt_hbm, tgt_v),
                (kj_hbm, kj_ref),
            )
        )
    ]
    for copy in fetch:
        copy.start()
    fetch_low, fetch_hi, fetch_kl, fetch_kh, fetch_tgt, fetch_kj = fetch
    leave = [
        pltpu.make_async_copy(src, dst, out_sem.at[n])
        for n, (src, dst) in enumerate(
            ((x3_ref, x3_hbm), (o3_ref, o3_hbm), (l3_ref, l3_hbm), (ha_ref, ha_hbm), (la_ref, la_hbm))
        )
    ]
    leave_x3, leave_o3, leave_l3, leave_ha, leave_la = leave
    first = pos_ref[0] == 0
    last = pos_ref[0] == 7
    core = pos_ref[1]
    up_ref[...] = up_matrix()

    put3(l3_ref, 0, n_ref[192:240, :].astype(F32))
    put3(l3_ref, 304, s_ref[192:240, :].astype(F32))
    put3(x3_ref, 0, n_ref[0:128, :].astype(F32))
    put3(x3_ref, 1664, s_ref[0:128, :].astype(F32))
    zero_at(first, l3_ref, 0, 48)
    zero_at(last, l3_ref, 304, 48)
    zero_at(first, x3_ref, 0, 128)
    zero_at(last, x3_ref, 1664, 128)
    fetch_low.wait()
    put3(
        l3_ref,
        48,
        widen_low(low_v[...].astype(F32), w_ref[H:].astype(F32), e_ref[H:].astype(F32)).reshape(256, C),
    )
    leave_l3.start()
    fetch_hi.wait()

    def widen_rows(t, _):
        rows = pl.ds(pl.multiple_of(t * 8, 8), 8)
        wide = widen_hi(hi_v[rows].astype(F32), w_ref[rows].astype(F32), e_ref[rows].astype(F32))
        put3(x3_ref, pl.multiple_of(128 + t * 256, 128), wide.reshape(256, C))
        return 0

    lax.fori_loop(0, 6, widen_rows, 0)
    leave_x3.start()
    fetch_kl.wait()
    la_ref[...] = jnp.maximum(
        jnp.dot(window(l3_ref, 0, 320, LWW), kl_ref[...], preferred_element_type=F32), 0.0
    ).astype(BF16)
    zero_at(first, la_ref, 0, 32)
    zero_at(last, la_ref, 288, 32)
    leave_la.start()
    fetch_kh.wait()

    def high(b, _):
        s = pl.multiple_of(b * 576, 64)
        act = jnp.maximum(
            jnp.dot(window(x3_ref, s, 576, WW), kh_ref[...], preferred_element_type=F32), 0.0
        ).astype(BF16)
        ha_ref[pl.ds(s, 576), :] = act
        cells = la_ref[pl.ds(pl.multiple_of(b * 96, 32), 128), :]
        lift = jnp.dot(up_ref[...], cells, preferred_element_type=F32) * NINTH
        put3(j3_ref, s, act.astype(F32) + lift)
        return 0

    lax.fori_loop(0, 3, high, 0)
    leave_ha.start()
    zero_at(first, j3_ref, 0, 96)
    zero_at(last, j3_ref, 51 * WW, 96)
    tg_ref[0:64, :] = n_ref[128:192, :]
    tg_ref[1600:1664, :] = s_ref[128:192, :]
    fetch_tgt.wait()

    def widen_targets(t, _):
        rows = pl.ds(pl.multiple_of(t * 8, 8), 8)
        wide = widen_tgt(tgt_v[rows].astype(F32), w_ref[rows].astype(F32), e_ref[rows].astype(F32))
        tg_ref[pl.ds(pl.multiple_of(64 + t * 256, 64), 256), :] = wide.reshape(256, C).astype(BF16)
        return 0

    lax.fori_loop(0, 6, widen_targets, 0)
    fetch_kj.wait()

    def weight_of(high_part, low_part):
        return ((high_part * 32.0 + low_part) * SCALE)[None]

    own = land_ref[0, 0]
    wland = w_ref[0:1].astype(F32)
    eland = e_ref[0:1].astype(F32)
    top = weight_of(n_ref[240:272, :].astype(F32), n_ref[272:304, :].astype(F32))
    mid = weight_of(
        land_row(6, (own // 32).astype(F32), wland, eland), land_row(7, (own % 32).astype(F32), wland, eland)
    )
    bot = weight_of(s_ref[240:272, :].astype(F32), s_ref[272:304, :].astype(F32))

    def join(b, _):
        s = pl.multiple_of(b * 416, 32)
        y = jnp.dot(window(j3_ref, s, 416, WW), kj_ref[...], preferred_element_type=F32)
        diff = (y - tg_ref[pl.ds(s, 416), :].astype(F32)).reshape(13, WW, C)
        row = lax.broadcasted_iota(jnp.int32, (13, WW, C), 0) + b * 13
        weight = jnp.where(row < 2, top, jnp.where(row >= 50, bot, mid))
        grad = (weight * diff).reshape(416, C)
        put3(o3_ref, s, grad)
        og_ref[pl.ds(s, 416), :] = jnp.where(own_columns(416), grad, 0.0).astype(BF16)
        return 0

    lax.fori_loop(0, 4, join, 0)
    zero_at(first, o3_ref, 0, 64)
    zero_at(last, o3_ref, 50 * WW, 64)
    leave_o3.start()
    contract(j3_ref, og_ref[64:1600, :], 64, WW, 1536, g_ref)
    hand_out(g_ref, keep_ref, send_ref, core, keep_sem)
    for copy in leave:
        copy.wait()
    wait_out(g_ref.at[0:1152], keep_ref.at[:], keep_sem)


def backward(
    pos_ref, x3_hbm, o3_hbm, l3_hbm, ha_hbm, la_hbm, kj_hbm,
    keep_ref, send_ref,
    x3_ref, o3_ref, l3_ref, ha_ref, la_ref, jg_ref, hg_ref, lg_ref, kj_ref, kt_ref, g_ref, sem, keep_sem,
):
    fetch = [
        pltpu.make_async_copy(src, dst, sem.at[n])
        for n, (src, dst) in enumerate(
            (
                (kj_hbm, kj_ref),
                (o3_hbm, o3_ref),
                (ha_hbm, ha_ref),
                (x3_hbm, x3_ref),
                (la_hbm, la_ref),
                (l3_hbm, l3_ref),
            )
        )
    ]
    for copy in fetch:
        copy.start()
    fetch_kj, fetch_o3, fetch_ha, fetch_x3, fetch_la, fetch_l3 = fetch
    first = pos_ref[0] == 0
    last = pos_ref[0] == 7
    core = pos_ref[1]
    fetch_kj.wait()
    for tap in range(9):
        kt_ref[(8 - tap) * C : (9 - tap) * C, :] = kj_ref[tap * C : (tap + 1) * C, :].T
    fetch_o3.wait()
    fetch_ha.wait()

    def back(b, _):
        s = pl.multiple_of(b * 320, 32)
        y = jnp.dot(window(o3_ref, s, 320, WW), kt_ref[...], preferred_element_type=F32)
        jg_ref[pl.ds(s, 320), :] = y.astype(BF16)
        on = ha_ref[pl.ds(pl.multiple_of(s + 64, 32), 320), :].astype(F32) > 0
        hg_ref[pl.ds(s, 320), :] = jnp.where(own_columns(320) & on, y, 0.0).astype(BF16)
        return 0

    lax.fori_loop(0, 5, back, 0)
    zero_at(first, jg_ref, 0, 32)
    zero_at(last, jg_ref, 49 * WW, 32)
    fetch_la.wait()
    fetch_l3.wait()
    fetch_x3.wait()
    contract(x3_ref, hg_ref[32:1568, :], 96, WW, 1536, g_ref.at[0])
    hand_out(g_ref.at[0], keep_ref.at[0], send_ref.at[0], core, keep_sem.at[0])
    down = down_matrix()
    for b in range(2):
        lifted = jnp.dot(down, jg_ref[b * 768 : b * 768 + 832, :], preferred_element_type=F32) * NINTH
        on = la_ref[32 + b * 128 : 160 + b * 128, :].astype(F32) > 0
        lg_ref[b * 128 : (b + 1) * 128, :] = jnp.where(on, lifted, 0.0).astype(BF16)
    contract(l3_ref, lg_ref[...], 32, LWW, 256, g_ref.at[1])
    hand_out(g_ref.at[1], keep_ref.at[1], send_ref.at[1], core, keep_sem.at[1])
    for n in range(2):
        wait_out(g_ref.at[n, 0:1152], keep_ref.at[n], keep_sem.at[n])


def regroup_lanes(parts, rows):
    quarter = lax.broadcasted_iota(jnp.int32, (rows, 128), 1) // 32
    for q in range(4):
        out = None
        for g in range(4):
            shift = ((g - q) * 32) % 128
            turned = pltpu.roll(parts[g], shift, 1) if shift else parts[g]
            out = turned if out is None else jnp.where(quarter == g, turned, out)
        yield q, out


def merge(keep_hbm, recv_ref, out_ref, keep_ref, sem):
    copies = [pltpu.make_async_copy(keep_hbm.at[n], keep_ref.at[n], sem.at[n]) for n in range(keep_ref.shape[0])]
    for copy in copies:
        copy.start()
    for n, copy in enumerate(copies):
        copy.wait()

        def one(t, _):
            xl = t // 2
            p = t % 2
            blocks = []
            for g in range(4):
                at = xl * 8 + 2 * g + p
                blocks.append(keep_ref[n, at] + recv_ref[n, at].astype(F32))
            for h in range(2):
                parts = [v[:, h * 128 : (h + 1) * 128] for v in blocks]
                for q, out in regroup_lanes(parts, 72):
                    out_ref[(h * 4 + q) * 2 + xl, n * 2 + p] = out.astype(BF16)
            return 0

        lax.fori_loop(0, 4, one, 0)


def total(join_ref, rest_ref, out_ref):
    quarter = lax.broadcasted_iota(jnp.int32, (56, 128), 1) // 32
    for p in range(2):
        sums = []
        for ref, n in ((rest_ref, p), (rest_ref, 2 + p), (join_ref, p)):
            acc = ref[0, n].astype(F32)
            for i in range(1, 16):
                acc = acc + ref[i, n].astype(F32)
            sums.append(acc)
        rows = jnp.concatenate(sums + [jnp.zeros((8, 128), F32)], axis=0)
        for g in range(4):
            out = None
            for s in range(4):
                shift = ((s - g) * 32) % 128
                part = rows[s * 56 : (s + 1) * 56]
                turned = pltpu.roll(part, shift, 1) if shift else part
                out = turned if out is None else jnp.where(quarter == s, turned, out)
            out_ref[2 * g + p] = out


def finish(in_ref, a_ref, b_ref, c_ref):
    acc = in_ref[0].astype(F32)
    for i in range(1, 8):
        acc = acc + in_ref[i].astype(F32)
    rows = jnp.concatenate(
        [acc if s == 0 else pltpu.roll(acc, 128 - 32 * s, 1) for s in range(4)], axis=0
    )
    for g, ref in enumerate((a_ref, b_ref, c_ref)):
        ref[...] = rows[g * 72 : (g + 1) * 72].T[0:32]


def call(kernel, out, specs, scratch=(), outs=None, vmem=None):
    return pl.pallas_call(
        kernel,
        out_shape=tuple(jax.ShapeDtypeStruct(s, d) for s, d in out),
        in_specs=list(specs),
        out_specs=outs or tuple(VMEM for _ in out),
        scratch_shapes=list(scratch),
        compiler_params=pltpu.CompilerParams(vmem_limit_bytes=vmem) if vmem else None,
    )


def ring(count, step):
    return [(i, (i + step) % count) for i in range(count)]


XY = ("yh", "yl", "xh", "xl")
Z = ("zh", "zm", "zl")


def step(hi, low, kh, kl, kj, tgt, land):
    dma = pltpu.SemaphoreType.DMA
    west, east, edges = call(
        pack_lon,
        [((H + LH, 8, C), BF16)] * 2 + [((2, 7, W, C), BF16)],
        [SMEM] + [HBM] * 3,
        [pltpu.VMEM((2, H, 8, C), BF16), pltpu.VMEM((2, H, 8, C), BF16), pltpu.VMEM((LH, LW, C), BF16), dma((9,))],
        vmem=FULL,
    )(land, hi, tgt, low)
    from_e = lax.ppermute(west, LON, ring(32, -1))
    from_w = lax.ppermute(east, LON, ring(32, 1))
    north, south = call(pack_lat, [((PK, C), BF16)] * 2, [SMEM] + [VMEM] * 3, vmem=6 * MIB)(land, edges, from_w, from_e)
    from_s = lax.ppermute(north, LAT, ring(8, -1))
    from_n = lax.ppermute(south, LAT, ring(8, 1))
    pos = jnp.stack([lax.axis_index(LAT), lax.axis_index("core")]).astype(jnp.int32)
    weights = [k.reshape(9 * C, C) for k in (kh, kl, kj)]
    stored = [((1792, 768), BF16), ((1664, 768), BF16), ((352, 768), BF16), ((1728, C), BF16), ((320, C), BF16)]
    x3, o3, l3, ha, la = (pltpu.VMEM(*one) for one in stored)
    keep_join, send_join, *saved = call(
        forward,
        [((16, 72, C), F32), ((16, 72, C), BF16)] + stored,
        [SMEM] * 2 + [HBM] * 3 + [VMEM] * 4 + [HBM] * 3,
        [
            x3, pltpu.VMEM((1728, 768), BF16), o3, l3, ha, la,
            pltpu.VMEM((1664, C), BF16),
            pltpu.VMEM((1664, C), BF16),
            pltpu.VMEM((2304, C), F32),
            pltpu.VMEM((576, 128), BF16),
            pltpu.VMEM((H, W, C), BF16),
            pltpu.VMEM((H, W, C), BF16),
            pltpu.VMEM((LH, LW, C), BF16),
            pltpu.VMEM((2304, C), BF16),
            pltpu.VMEM((2304, C), BF16),
            pltpu.VMEM((2304, C), BF16),
            dma((6,)),
            dma((5,)),
            dma(()),
        ],
        outs=(HBM, VMEM) + (HBM,) * 5,
        vmem=MAIN_LIMIT,
    )(pos, land, hi, tgt, low, from_w, from_e, from_n, from_s, *weights)
    recv_join = lax.ppermute(send_join, "core", ring(2, 1))
    keep_rest, send_rest = call(
        backward,
        [((2, 16, 72, C), F32), ((2, 16, 72, C), BF16)],
        [SMEM] + [HBM] * 6,
        [
            x3, o3, l3, ha, la,
            pltpu.VMEM((1600, C), BF16),
            pltpu.VMEM((1600, C), BF16),
            pltpu.VMEM((256, C), BF16),
            pltpu.VMEM((2304, C), BF16),
            pltpu.VMEM((2304, C), BF16),
            pltpu.VMEM((2, 2304, C), F32),
            dma((6,)),
            dma((2,)),
        ],
        outs=(HBM, VMEM),
        vmem=FULL,
    )(pos, *saved, weights[2])

    def merged(keep, recv, count, limit):
        (out,) = call(
            merge,
            [((16, 2 * count, 72, 128), BF16)],
            [HBM, VMEM],
            [pltpu.VMEM((count, 16, 72, C), F32), dma((count,))],
            vmem=limit,
        )(keep, recv)
        return out

    parts_join = merged(keep_join[None], recv_join[None], 1, JOIN_LIMIT)
    parts_join = lax.all_to_all(parts_join, XY, 0, 0, tiled=True)
    recv_rest = lax.ppermute(send_rest, "core", ring(2, 1))
    parts_rest = merged(keep_rest, recv_rest, 2, REST_LIMIT)
    parts_rest = lax.all_to_all(parts_rest, XY, 0, 0, tiled=True)
    (parts,) = call(total, [((8, 56, 128), F32)], [VMEM] * 2, vmem=6 * MIB)(parts_join, parts_rest)
    parts = lax.all_to_all(parts, Z, 0, 0, tiled=True)
    grads = call(finish, [((32, 72), F32)] * 3, [VMEM], vmem=2 * MIB)(parts)
    return tuple(g.T for g in grads)


def solution(mesh):
    fine = Mesh(mesh.devices.reshape((2,) * 8), LAT + LON)
    tile = P(LAT, LON, None)
    return jax.shard_map(
        step,
        mesh=fine,
        in_specs=(tile, tile, P(), P(), P(), tile, P(LAT, LON)),
        out_specs=(P(LON, LAT),) * 3,
        check_vma=False,
    )
```

time: 108 us -> 118 us (1.093)
  blocking collectives: 47.1 us -> 38.9 us
  starting transfers between devices: 11 us -> 18.3 us
  waiting for transfers between devices: 15.6 us -> 22.1 us
  Pallas kernels: 28.6 us -> 34.4 us
  local copies, waits for them, and re-layouts: 2.96 us -> 1.59 us
    all_to_all x2, blocking collectives: 47.1 us -> 38.9 us  [the longest x1 21.8 us: step(): parts_rest = lax.all_to_all(parts_rest, XY, 0, 0, tiled=True)]
    all_to_all x0 -> x1, waiting for transfers between devices: none -> 7.09 us  [step(): parts_join = lax.all_to_all(parts_join, XY, 0, 0, tiled=True)]
    all_to_all x0 -> x1, starting transfers between devices: none -> 6.82 us  [step(): parts_join = lax.all_to_all(parts_join, XY, 0, 0, tiled=True)]
    pallas_call x6 -> x8, Pallas kernels: 28.6 us -> 34.4 us  [the longest x1 13.4 us: step(): call(forward, [((16, 72, C), F32), ((16, 72, C), BF16)] + stored, [SMEM]...]
    unnamed x6 -> x10, local copies, waits for them, and re-layouts: 2.96 us -> 1.59 us
    ppermute x5 -> x6, waiting for transfers between devices: 15.6 us -> 15 us  [the longest x1 4.79 us: step(): from_n = lax.ppermute(south, LAT, ring(8, 1))]
    ppermute x5 -> x6, starting transfers between devices: 11 us -> 11.5 us  [the longest x1 6.3 us: step(): from_e = lax.ppermute(west, LON, ring(32, -1))]
  transfers between devices with their start and end apart: 5 -> 7, of which waited for: 4 -> 5; matrix products, arithmetic and copies ran while one was open for 0% -> 0% of each run, Pallas kernels for 0% -> 5%
where the time goes in v4:
time: 118 us; the launch traced here: 117 us
  blocking collectives  38.9 us (33%)
  Pallas kernels  34.4 us (29%)
  waiting for transfers between devices  22.1 us (19%)
  starting transfers between devices  18.3 us (16%)
  local copies, waits for them, and re-layouts  1.59 us (1%)
  between operations  1.42 us (1%)
    all_to_all x1, blocking collectives, step(): parts_rest = lax.all_to_all(parts_rest, XY, 0, 0, tiled=True)  21.8 us
    all_to_all x1, blocking collectives, step(): parts = lax.all_to_all(parts, Z, 0, 0, tiled=True)  17 us
    pallas_call x1, Pallas kernels, step(): call(forward, [((16, 72, C), F32), ((16, 72, C), BF16)] + stored, [SMEM]...  13.4 us
    pallas_call x1, Pallas kernels, step(): call(backward, [((2, 16, 72, C), F32), ((2, 16, 72, C), BF16)], [SMEM] +...  11.8 us
    all_to_all x1, waiting for transfers between devices, step(): parts_join = lax.all_to_all(parts_join, XY, 0, 0, tiled=True)  7.09 us
    all_to_all x1, starting transfers between devices, step(): parts_join = lax.all_to_all(parts_join, XY, 0, 0, tiled=True)  6.82 us
    ppermute x1, starting transfers between devices, step(): from_e = lax.ppermute(west, LON, ring(32, -1))  6.3 us
    pallas_call x2, Pallas kernels, merged(): call(merge, [((16, 2 * count, 72, 128), BF16)], [HBM, VMEM], [pltpu.VMEM(...  5.75 us
  transfers between devices with their start and end apart: 7, of which 5 were waited for; matrix products, arithmetic and copies ran while one was open for 0% of the time, Pallas kernels for 5%

profile of v4, /device:TPU:8, one launch (start us, length us, event | category | flops | bytes accessed | tf_op | source)
XLA Modules:
  0.0 116.8 jit_solution(6771679032239669644)
XLA Ops:
  0.6 0.0 copy-start
  1.3 2.3 %shard_map.94 = (bf16[64,8,256]{2,1,0:T(8,128)(2,1)}, bf16[64,8,256]{2,1,0:T(8,128)(2,1)}, bf16[2,7,24,256]{3,2,1,0:T(8,128)(2,1)}) custom-call(s32[1,1]{1,0:T(1,128)S(6)} %copy.10.land_ref, bf16[48,24,256]{2,1,0:T(8,128)(2,1)} %hi_hbm.1, bf16[48,24,256]{2,1,0:T(8,128)(2,1)} %tgt_hbm.1, bf16[16,8,256]{2,1,0:T(8,128)(2,1)} %low_hbm.1), custom_call_target="tpu_custom_call" | custom-call | tf_op jit(solution)/shard_map/pallas_call | solution.py:470
  3.6 0.1 collective-permute-start
  3.7 6.3 %collective-permute-start.1 = (bf16[64,8,256]{2,1,0:T(8,128)(2,1)}, bf16[64,8,256]{2,1,0:T(8,128)(2,1)S(1)}, u32[]{:S(2)}, u32[]{:S(2)}) collective-permute-start(bf16[64,8,256]{2,1,0:T(8,128)(2,1)} %get-tuple-element.21), channel_id=1, source_target_pairs={{0,31},{1,0},{2,1},{3,2},{4,3},{5,4},{6,5},{7,6},{8,7},{9,8},{10,9... | collective-permute-start | bytes 786440 | tf_op jit(solution)/shard_map/ppermute | solution.py:477
  10.0 4.3 %collective-permute-done.w_ref = bf16[64,8,256]{2,1,0:T(8,128)(2,1)S(1)} collective-permute-done((bf16[64,8,256]{2,1,0:T(8,128)(2,1)}, bf16[64,8,256]{2,1,0:T(8,128)(2,1)S(1)}, u32[]{:S(2)}, u32[]{:S(2)}) %collective-permute-start) | collective-permute-done | bytes 262176 | tf_op jit(solution)/shard_map/ppermute | solution.py:478
  14.3 0.0 collective-permute-done.1.e_ref
  14.3 0.0 copy-start.1
  14.3 0.9 copy-done.1
  15.2 0.1 shard_map.95
  15.2 2.8 %collective-permute-start.2 = (bf16[304,256]{1,0:T(8,128)(2,1)S(1)}, bf16[304,256]{1,0:T(8,128)(2,1)S(1)}, u32[]{:S(2)}, u32[]{:S(2)}) collective-permute-start(bf16[304,256]{1,0:T(8,128)(2,1)S(1)} %get-tuple-element.23), channel_id=1, source_target_pairs={{0,32},{32,64},{64,96},{96,128},{128,160},{160,192},{192,224},{224... | collective-permute-start | bytes 466952 | tf_op jit(solution)/shard_map/ppermute | solution.py:481
  18.1 1.7 %collective-permute-start.3 = (bf16[304,256]{1,0:T(8,128)(2,1)S(1)}, bf16[304,256]{1,0:T(8,128)(2,1)S(1)}, u32[]{:S(2)}, u32[]{:S(2)}) collective-permute-start(bf16[304,256]{1,0:T(8,128)(2,1)S(1)} %get-tuple-element.24), channel_id=1, source_target_pairs={{0,224},{32,0},{64,32},{96,64},{128,96},{160,128},{192,160},{224,1... | collective-permute-start | bytes 466952 | tf_op jit(solution)/shard_map/ppermute | solution.py:480
  19.8 0.1 pad_add_fusion.pos_ref
  19.8 0.0 copy-start.3
  19.8 4.8 %collective-permute-done.2.n_ref = bf16[304,256]{1,0:T(8,128)(2,1)S(1)} collective-permute-done((bf16[304,256]{1,0:T(8,128)(2,1)S(1)}, bf16[304,256]{1,0:T(8,128)(2,1)S(1)}, u32[]{:S(2)}, u32[]{:S(2)}) %collective-permute-start.2) | collective-permute-done | bytes 155680 | tf_op jit(solution)/shard_map/ppermute | solution.py:481
  24.6 2.5 %collective-permute-done.3.s_ref = bf16[304,256]{1,0:T(8,128)(2,1)S(1)} collective-permute-done((bf16[304,256]{1,0:T(8,128)(2,1)S(1)}, bf16[304,256]{1,0:T(8,128)(2,1)S(1)}, u32[]{:S(2)}, u32[]{:S(2)}) %collective-permute-start.3) | collective-permute-done | bytes 155680 | tf_op jit(solution)/shard_map/ppermute | solution.py:480
  27.2 0.0 copy-done
  27.2 13.4 %shard_map.96 = (f32[16,72,256]{2,1,0:T(8,128)}, bf16[16,72,256]{2,1,0:T(8,128)(2,1)}, bf16[1792,768]{1,0:T(8,128)(2,1)}, bf16[1664,768]{1,0:T(8,128)(2,1)}, bf1...) custom-call(s32[2]{0:T(128)S(1)} %pad_add_fusion.pos_ref, ...), custom_call_target="tpu_custom_call" | custom-call | tf_op jit(solution)/shard_map/pallas_call | solution.py:486
  40.6 0.0 copy-done.3
  40.6 0.0 copy-start.2
  40.6 0.7 copy-done.2
  41.3 0.0 copy-start.4
  41.3 11.8 %shard_map.98 = (f32[2,16,72,256]{3,2,1,0:T(8,128)}, bf16[2,16,72,256]{3,2,1,0:T(8,128)(2,1)}) custom-call(s32[2]{0:T(128)} %copy-done.3, bf16[1792,768]{1,0:T(8,128)(2,1)} %get-tuple-element.27.x3_hbm, bf16[1664,768]{1,0:T(8,128)(2,1)} %get-tuple-element.28.o3_hbm, bf16[352,768]{1,0:T(8,128)(2,1)} %get-tuple-element.29.l3_hbm, ...), custom_call_target="tpu_custom_call" | custom-call | tf_op jit(solution)/shard_map/pallas_call | solution.py:510
  53.1 0.1 collective-permute-start.5
  53.2 0.0 copy-done.4
  53.2 0.5 collective-permute-start.4
  53.7 3.4 %collective-permute-done.4 = bf16[16,72,256]{2,1,0:T(8,128)(2,1)S(1)} collective-permute-done((bf16[16,72,256]{2,1,0:T(8,128)(2,1)S(1)}, bf16[16,72,256]{2,1,0:T(8,128)(2,1)S(1)}, u32[]{:S(2)}, u32[]{:S(2)}) %collective-permute-start.4) | collective-permute-done | bytes 589856 | tf_op jit(solution)/shard_map/ppermute | solution.py:509
  57.1 2.9 %shard_map.97 = bf16[16,2,72,128]{3,2,1,0:T(8,128)(2,1)} custom-call(f32[1,16,72,256]{3,2,1,0:T(8,128)} %bitcast.13, bf16[1,16,72,256]{3,2,1,0:T(8,128)(2,1)S(1)} %bitcast.10), custom_call_target="tpu_custom_call" | custom-call | tf_op jit(solution)/shard_map/pallas_call | solution.py:530
  60.0 6.8 %all-to-all-start = ((bf16[16,2,72,128]{3,2,1,0:T(8,128)(2,1)}), bf16[16,2,72,128]{3,2,1,0:T(8,128)(2,1)S(1)}, u32[]{:S(2)}, u32[]{:S(2)}) async-start(bf16[16,2,72,128]{3,2,1,0:T(8,128)(2,1)} %shard_map.97), calls=%async_computation | async-start | bytes 1179648 | tf_op jit(solution)/shard_map/all_to_all | solution.py:540
  66.8 0.0 collective-permute-done.5.recv_ref
  66.8 2.9 %shard_map.99 = bf16[16,4,72,128]{3,2,1,0:T(8,128)(2,1)S(1)} custom-call(f32[2,16,72,256]{3,2,1,0:T(8,128)} %get-tuple-element.32.keep_hbm, bf16[2,16,72,256]{3,2,1,0:T(8,128)(2,1)S(1)} %collective-permute-done.5.recv_ref), custom_call_target="tpu_custom_call" | custom-call | tf_op jit(solution)/shard_map/pallas_call | solution.py:530
  69.7 7.1 %all-to-all-done.join_ref = bf16[16,2,72,128]{3,2,1,0:T(8,128)(2,1)S(1)} async-done(((bf16[16,2,72,128]{3,2,1,0:T(8,128)(2,1)}), bf16[16,2,72,128]{3,2,1,0:T(8,128)(2,1)S(1)}, u32[]{:S(2)}, u32[]{:S(2)}) %all-to-all-start) | async-done | bytes 589856 | tf_op jit(solution)/shard_map/all_to_all | solution.py:540
  76.8 21.8 %all_to_all.15.rest_ref = bf16[16,4,72,128]{3,2,1,0:T(8,128)(2,1)S(1)} all-to-all(bf16[16,4,72,128]{3,2,1,0:T(8,128)(2,1)S(1)} %shard_map.99), channel_id=1, replica_groups=mesh['yh'=2,'yl'=2,'xh'=2,'zh'=2,'zm'=2,'zl'=2,'xl'=2,'core'=2] {'yh','y..., dimensions={0} | all-to-all | bytes 2359296 | tf_op jit(solution)/shard_map/all_to_all | solution.py:543
  98.6 0.4 shard_map.100
  99.0 17.0 %all_to_all.16.in_ref = f32[8,56,128]{2,1,0:T(8,128)S(1)} all-to-all(f32[8,56,128]{2,1,0:T(8,128)S(1)} %shard_map.100), channel_id=1, replica_groups=mesh['yh'=2,'yl'=2,'xh'=2,'zh'=2,'zm'=2,'zl'=2,'xl'=2,'core'=2] {'zh','z..., dimensions={0} | all-to-all | bytes 458752 | tf_op jit(solution)/shard_map/all_to_all | solution.py:545
  116.0 0.8 shard_map.101
Async XLA Ops:
  0.6 26.5 %copy-start = (bf16[16,8,256]{2,1,0:T(8,128)(2,1)S(1)}, bf16[16,8,256]{2,1,0:T(8,128)(2,1)}, u32[]{:S(2)}) copy-start(bf16[16,8,256]{2,1,0:T(8,128)(2,1)} %low_hbm.1) | copy-start | bytes 196612
  3.6 10.7 %collective-permute-start = (bf16[64,8,256]{2,1,0:T(8,128)(2,1)}, bf16[64,8,256]{2,1,0:T(8,128)(2,1)S(1)}, u32[]{:S(2)}, u32[]{:S(2)}) collective-permute-start(bf16[64,8,256]{2,1,0:T(8,128)(2,1)} %get-tuple-element.20), channel_id=1, source_target_pairs={{0,1},{1,2},{2,3},{3,4},{4,5},{5,6},{6,7},{7,8},{8,9},{9,10},{10,1... | collective-permute-start | bytes 786440 | tf_op jit(solution)/shard_map/ppermute | solution.py:478
  3.7 10.6 %collective-permute-start.1 = (bf16[64,8,256]{2,1,0:T(8,128)(2,1)}, bf16[64,8,256]{2,1,0:T(8,128)(2,1)S(1)}, u32[]{:S(2)}, u32[]{:S(2)}) collective-permute-start(bf16[64,8,256]{2,1,0:T(8,128)(2,1)} %get-tuple-element.21), channel_id=1, source_target_pairs={{0,31},{1,0},{2,1},{3,2},{4,3},{5,4},{6,5},{7,6},{8,7},{9,8},{10,9... | collective-permute-start | bytes 786440 | tf_op jit(solution)/shard_map/ppermute | solution.py:477
  14.3 0.9 copy-start.1
  15.2 9.4 %collective-permute-start.2 = (bf16[304,256]{1,0:T(8,128)(2,1)S(1)}, bf16[304,256]{1,0:T(8,128)(2,1)S(1)}, u32[]{:S(2)}, u32[]{:S(2)}) collective-permute-start(bf16[304,256]{1,0:T(8,128)(2,1)S(1)} %get-tuple-element.23), channel_id=1, source_target_pairs={{0,32},{32,64},{64,96},{96,128},{128,160},{160,192},{192,224},{224... | collective-permute-start | bytes 466952 | tf_op jit(solution)/shard_map/ppermute | solution.py:481
  18.1 9.1 %collective-permute-start.3 = (bf16[304,256]{1,0:T(8,128)(2,1)S(1)}, bf16[304,256]{1,0:T(8,128)(2,1)S(1)}, u32[]{:S(2)}, u32[]{:S(2)}) collective-permute-start(bf16[304,256]{1,0:T(8,128)(2,1)S(1)} %get-tuple-element.24), channel_id=1, source_target_pairs={{0,224},{32,0},{64,32},{96,64},{128,96},{160,128},{192,160},{224,1... | collective-permute-start | bytes 466952 | tf_op jit(solution)/shard_map/ppermute | solution.py:480
  19.8 20.8 %copy-start.3 = (s32[2]{0:T(128)}, s32[2]{0:T(128)S(1)}, u32[]{:S(2)}) copy-start(s32[2]{0:T(128)S(1)} %pad_add_fusion.pos_ref) | copy-start | bytes 28
  40.6 0.7 copy-start.2
  41.3 11.9 %copy-start.4 = (bf16[16,72,256]{2,1,0:T(8,128)(2,1)S(1)}, bf16[16,72,256]{2,1,0:T(8,128)(2,1)}, u32[]{:S(2)}) copy-start(bf16[16,72,256]{2,1,0:T(8,128)(2,1)} %get-tuple-element.26) | copy-start | bytes 1769476
  53.1 13.7 %collective-permute-start.5 = (bf16[2,16,72,256]{3,2,1,0:T(8,128)(2,1)}, bf16[2,16,72,256]{3,2,1,0:T(8,128)(2,1)S(1)}, u32[]{:S(2)}, u32[]{:S(2)}) collective-permute-start(bf16[2,16,72,256]{3,2,1,0:T(8,128)(2,1)} %get-tuple-element.33), channel_id=1, source_target_pairs={{0,1},{1,0},{2,3},{3,2},{4,5},{5,4},{6,7},{7,6},{8,9},{9,8},{10,11... | collective-permute-start | bytes 3538952 | tf_op jit(solution)/shard_map/ppermute | solution.py:541
  53.2 3.9 %collective-permute-start.4 = (bf16[16,72,256]{2,1,0:T(8,128)(2,1)S(1)}, bf16[16,72,256]{2,1,0:T(8,128)(2,1)S(1)}, u32[]{:S(2)}, u32[]{:S(2)}) collective-permute-start(bf16[16,72,256]{2,1,0:T(8,128)(2,1)S(1)} %copy-done.4), channel_id=1, source_target_pairs={{0,1},{1,0},{2,3},{3,2},{4,5},{5,4},{6,7},{7,6},{8,9},{9,8},{10,11... | collective-permute-start | bytes 1769480 | tf_op jit(solution)/shard_map/ppermute | solution.py:509
  60.0 16.8 %all-to-all-start = ((bf16[16,2,72,128]{3,2,1,0:T(8,128)(2,1)}), bf16[16,2,72,128]{3,2,1,0:T(8,128)(2,1)S(1)}, u32[]{:S(2)}, u32[]{:S(2)}) async-start(bf16[16,2,72,128]{3,2,1,0:T(8,128)(2,1)} %shard_map.97), calls=%async_computation | async-start | bytes 1179648 | tf_op jit(solution)/shard_map/all_to_all | solution.py:540

commit v5 on v4

v5 whole, which is shorter than its diff:
```python
import jax
import jax.numpy as jnp
from jax import lax
from jax.experimental import pallas as pl
from jax.experimental.pallas import tpu as pltpu
from jax.sharding import Mesh, PartitionSpec as P

F32 = jnp.float32
BF16 = jnp.bfloat16
C = 256
H, W = 48, 24
LH, LW = 16, 8
WW = 32
LWW = 16
LAT = ("yh", "yl", "xh")
LON = ("zh", "zm", "zl", "xl", "core")
SCALE = 2.0 / (H * W * H * W)
NINTH = 1.0 / 9.0
PK = 304
MIB = 1024 * 1024
FULL = 60 * 1024 * 1024
MAIN_LIMIT = 64 * MIB - 12_000_000
MERGE_LIMIT = 64 * MIB - 15_500_000
VMEM = pl.BlockSpec(memory_space=pltpu.VMEM)
SMEM = pl.BlockSpec(memory_space=pltpu.SMEM)
HBM = pl.BlockSpec(memory_space=pltpu.HBM)


def up_matrix():
    def weight(m, r, cell):
        side = jnp.where(cell == m, 2.0, jnp.where(cell == m + r - 1, 1.0, 0.0))
        return jnp.where(r == 1, jnp.where(cell == m, 3.0, 0.0), side)

    i = lax.broadcasted_iota(jnp.int32, (18, 1, 8 * LWW), 0)
    e = lax.broadcasted_iota(jnp.int32, (18, 1, 8 * LWW), 2) // LWW
    j = lax.broadcasted_iota(jnp.int32, (1, WW, 8 * LWW), 1) + 2
    f = lax.broadcasted_iota(jnp.int32, (1, WW, 8 * LWW), 2) % LWW
    both = weight(i // 3 + 1, i % 3, e) * weight(j // 3 + 1, j % 3, f)
    return both.reshape(18 * WW, 8 * LWW).astype(BF16)


def down_matrix():
    def weight(tap):
        return jnp.maximum(3 - jnp.abs(tap - 2), 0).astype(F32)

    m = lax.broadcasted_iota(jnp.int32, (8, 1, 26 * WW), 0)
    d = lax.broadcasted_iota(jnp.int32, (8, 1, 26 * WW), 2) // WW
    f = lax.broadcasted_iota(jnp.int32, (1, LWW, 26 * WW), 1) - 3
    j = lax.broadcasted_iota(jnp.int32, (1, LWW, 26 * WW), 2) % WW - 3
    both = weight(d - 3 * m) * jnp.where((f >= 0) & (f < LW), weight(j - 3 * f), 0.0)
    return both.reshape(8 * LWW, 26 * WW).astype(BF16)


def pack_lon(land_ref, hi_ref, tgt_ref, low_ref, west_ref, east_ref, edge_ref, hi_v, tgt_v, low_v, sem):
    copies = [
        pltpu.make_async_copy(src.at[:, pl.ds(start, 8), :], dst.at[side], sem.at[2 * n + side])
        for n, (src, dst) in enumerate(((hi_ref, hi_v), (tgt_ref, tgt_v)))
        for side, start in enumerate((0, 16))
    ]
    copies.append(pltpu.make_async_copy(low_ref, low_v, sem.at[4]))
    for side in range(2):
        copies.append(pltpu.make_async_copy(hi_ref.at[pl.ds(44 * side, 4)], edge_ref.at[side, 0:4], sem.at[5 + side]))
        copies.append(pltpu.make_async_copy(tgt_ref.at[pl.ds(46 * side, 2)], edge_ref.at[side, 4:6], sem.at[7 + side]))
    for copy in copies:
        copy.start()
    land = land_ref[0, 0]
    sub = lax.broadcasted_iota(jnp.int32, (H, 8, C), 1)
    row = lax.broadcasted_iota(jnp.int32, (H, 8, C), 0)
    lands = jnp.where(row % 2 == 0, (land // 32).astype(F32), (land % 32).astype(F32))
    for copy in copies:
        copy.wait()
    low = low_v[...].astype(F32)

    def rest(start):
        cells = jnp.stack([pltpu.roll(low, (7 - start - b) % 8, 1) for b in range(3)], axis=1)
        return jnp.where(sub == 6, lands, cells.reshape(H, 8, C))

    west = jnp.where(
        sub < 4, hi_v[0].astype(F32), jnp.where(sub < 6, pltpu.roll(tgt_v[0].astype(F32), 4, 1), rest(0))
    )
    east = jnp.where(
        sub < 4,
        pltpu.roll(hi_v[1].astype(F32), 4, 1),
        jnp.where(sub < 6, pltpu.roll(tgt_v[1].astype(F32), 6, 1), rest(5)),
    )
    west_ref[...] = west.astype(BF16)
    east_ref[...] = east.astype(BF16)
    for side in range(2):
        edge_ref[side, 6] = low_v[13 * side : 13 * side + 3].astype(F32).reshape(24, C).astype(BF16)


def widen_pixels(own, left, right):
    turned = [pltpu.roll(own[:, 8 * g : 8 * g + 8], 4, 1) for g in range(3)]
    parts = [left] + turned + [right]
    low_half = lax.broadcasted_iota(jnp.int32, left.shape, 1) < 4
    return jnp.concatenate([jnp.where(low_half, parts[g], parts[g + 1]) for g in range(4)], axis=1)


def widen_hi(own, wpk, epk):
    return widen_pixels(own, wpk, pltpu.roll(epk, 4, 1))


def widen_tgt(own, wpk, epk):
    return widen_pixels(own, pltpu.roll(wpk, 6, 1), epk)


def widen_low(own, wpk, epk):
    rows = own.shape[0]
    own = pltpu.roll(own, 3, 1)
    sub = lax.broadcasted_iota(jnp.int32, own.shape, 1)
    wpk = wpk.reshape(rows, 3, 8, C)
    epk = epk.reshape(rows, 3, 8, C)
    left, right = own, own
    for b in range(3):
        left = jnp.where(sub == b, pltpu.roll(wpk[:, b], b + 1, 1), left)
        right = jnp.where(sub == 3 + b, pltpu.roll(epk[:, b], b + 4, 1), right)
    return jnp.concatenate([left, right], axis=1)


def land_row(part, own, wpk, epk):
    col = lax.broadcasted_iota(jnp.int32, (WW, C), 0)
    left = wpk[part, 6:7, :]
    right = epk[part, 6:7, :]
    return jnp.where(col < 4, left, jnp.where(col < 4 + W, own, right))


def pack_lat(land_ref, own_ref, w_ref, e_ref, north_ref, south_ref):
    land = land_ref[0, 0]
    wpk = w_ref[0:2].astype(F32)
    epk = e_ref[0:2].astype(F32)
    lands = jnp.concatenate(
        [
            land_row(0, (land // 32).astype(F32), wpk, epk),
            land_row(1, (land % 32).astype(F32), wpk, epk),
        ],
        axis=0,
    ).astype(BF16)
    for side, out_ref in enumerate((north_ref, south_ref)):
        def edge(ref, depth):
            start = (H - depth) * side
            return ref[start : start + depth].astype(F32)

        own = own_ref[side].astype(F32)
        hi = widen_hi(own[0:4], edge(w_ref, 4), edge(e_ref, 4))
        tgt = widen_tgt(own[4:6], edge(w_ref, 2), edge(e_ref, 2))
        low = widen_low(own[6].reshape(3, 8, C), edge(w_ref, 9), edge(e_ref, 9))
        out_ref[0:128] = hi.reshape(128, C).astype(BF16)
        out_ref[128:192] = tgt.reshape(64, C).astype(BF16)
        out_ref[192:240] = low.reshape(48, C).astype(BF16)
        out_ref[240:304] = lands


def put3(dst, start, v):
    rows = v.shape[0]
    dst[pl.ds(start, rows), 0:C] = pltpu.roll(v, 1, 0).astype(BF16)
    dst[pl.ds(start, rows), C : 2 * C] = v.astype(BF16)
    dst[pl.ds(start, rows), 2 * C : 3 * C] = pltpu.roll(v, rows - 1, 0).astype(BF16)


def window(src, start, rows, stride):
    return jnp.concatenate(
        [src[pl.ds(pl.multiple_of(start + d * stride, 16), rows), :] for d in range(3)], axis=1
    )


def own_columns(rows):
    col = lax.broadcasted_iota(jnp.int32, (rows // WW, WW, C), 1).reshape(rows, C)
    return (col >= 4) & (col < 4 + W)


def zero_at(flag, ref, start, rows):
    @pl.when(flag)
    def _():
        ref[start : start + rows, :] = jnp.zeros((rows, ref.shape[1]), ref.dtype)


def contract(x_ref, g_val, base, stride, rows, out):
    for d in range(3):
        out[d * 768 : (d + 1) * 768, :] = lax.dot_general(
            x_ref[base + d * stride : base + d * stride + rows, :],
            g_val,
            (((0,), (0,)), ((), ())),
            preferred_element_type=F32,
        )


def block_start(t, half):
    return pl.multiple_of((t % 8 * 4 + t // 8 * 2 + half) * 72, 8)


def hand_out(g_ref, keep_hbm, sent_ref, send_hbm, core, keep_sem, send_sem):
    for t in range(16):
        pltpu.make_async_copy(g_ref.at[pl.ds(block_start(t, core), 72)], keep_hbm.at[t], keep_sem).start()

    def one(t, _):
        sent_ref[t] = g_ref[pl.ds(block_start(t, 1 - core), 72), :].astype(BF16)
        return 0

    lax.fori_loop(0, 16, one, 0)
    pltpu.make_async_copy(sent_ref, send_hbm, send_sem).start()


def main(
    pos_ref, land_ref, hi_hbm, tgt_hbm, low_hbm, w_ref, e_ref, n_ref, s_ref, kh_hbm, kl_hbm, kj_hbm,
    keep_hbm, send_hbm,
    x3_ref, j3_ref, o3_ref, l3_ref, ha_ref, la_ref, og_ref, tg_ref, jg_ref, lg_ref, g_ref, sent_ref, up_ref,
    hi_v, tgt_v, low_v, kh_ref, kl_ref, kj_ref, kt_ref, sem, keep_sem, send_sem,
):
    fetch = [
        pltpu.make_async_copy(src, dst, sem.at[n])
        for n, (src, dst) in enumerate(
            (
                (low_hbm, low_v),
                (hi_hbm, hi_v),
                (kl_hbm, kl_ref),
                (kh_hbm, kh_ref),
                (tgt_hbm, tgt_v),
                (kj_hbm, kj_ref),
            )
        )
    ]
    for copy in fetch:
        copy.start()
    fetch_low, fetch_hi, fetch_kl, fetch_kh, fetch_tgt, fetch_kj = fetch
    first = pos_ref[0] == 0
    last = pos_ref[0] == 7
    core = pos_ref[1]
    up_ref[...] = up_matrix()

    put3(l3_ref, 0, n_ref[192:240, :].astype(F32))
    put3(l3_ref, 304, s_ref[192:240, :].astype(F32))
    put3(x3_ref, 0, n_ref[0:128, :].astype(F32))
    put3(x3_ref, 1664, s_ref[0:128, :].astype(F32))
    zero_at(first, l3_ref, 0, 48)
    zero_at(last, l3_ref, 304, 48)
    zero_at(first, x3_ref, 0, 128)
    zero_at(last, x3_ref, 1664, 128)
    fetch_low.wait()
    put3(
        l3_ref,
        48,
        widen_low(low_v[...].astype(F32), w_ref[...].astype(F32), e_ref[...].astype(F32)).reshape(256, C),
    )
    fetch_hi.wait()

    def widen_rows(t, _):
        rows = pl.ds(pl.multiple_of(t * 8, 8), 8)
        wide = widen_hi(hi_v[rows].astype(F32), w_ref[rows].astype(F32), e_ref[rows].astype(F32))
        put3(x3_ref, pl.multiple_of(128 + t * 256, 128), wide.reshape(256, C))
        return 0

    lax.fori_loop(0, 6, widen_rows, 0)
    fetch_kl.wait()
    la_ref[...] = jnp.maximum(
        jnp.dot(window(l3_ref, 0, 320, LWW), kl_ref[...], preferred_element_type=F32), 0.0
    ).astype(BF16)
    zero_at(first, la_ref, 0, 32)
    zero_at(last, la_ref, 288, 32)
    fetch_kh.wait()

    def high(b, _):
        s = pl.multiple_of(b * 576, 64)
        act = jnp.maximum(
            jnp.dot(window(x3_ref, s, 576, WW), kh_ref[...], preferred_element_type=F32), 0.0
        ).astype(BF16)
        ha_ref[pl.ds(s, 576), :] = act
        cells = la_ref[pl.ds(pl.multiple_of(b * 96, 32), 128), :]
        lift = jnp.dot(up_ref[...], cells, preferred_element_type=F32) * NINTH
        put3(j3_ref, s, act.astype(F32) + lift)
        return 0

    lax.fori_loop(0, 3, high, 0)
    zero_at(first, j3_ref, 0, 96)
    zero_at(last, j3_ref, 51 * WW, 96)
    tg_ref[0:64, :] = n_ref[128:192, :]
    tg_ref[1600:1664, :] = s_ref[128:192, :]
    fetch_tgt.wait()

    def widen_targets(t, _):
        rows = pl.ds(pl.multiple_of(t * 8, 8), 8)
        wide = widen_tgt(tgt_v[rows].astype(F32), w_ref[rows].astype(F32), e_ref[rows].astype(F32))
        tg_ref[pl.ds(pl.multiple_of(64 + t * 256, 64), 256), :] = wide.reshape(256, C).astype(BF16)
        return 0

    lax.fori_loop(0, 6, widen_targets, 0)
    fetch_kj.wait()

    def weight_of(high_part, low_part):
        return ((high_part * 32.0 + low_part) * SCALE)[None]

    own = land_ref[0, 0]
    wland = w_ref[0:2].astype(F32)
    eland = e_ref[0:2].astype(F32)
    top = weight_of(n_ref[240:272, :].astype(F32), n_ref[272:304, :].astype(F32))
    mid = weight_of(
        land_row(0, (own // 32).astype(F32), wland, eland), land_row(1, (own % 32).astype(F32), wland, eland)
    )
    bot = weight_of(s_ref[240:272, :].astype(F32), s_ref[272:304, :].astype(F32))

    def join(b, _):
        s = pl.multiple_of(b * 416, 32)
        y = jnp.dot(window(j3_ref, s, 416, WW), kj_ref[...], preferred_element_type=F32)
        diff = (y - tg_ref[pl.ds(s, 416), :].astype(F32)).reshape(13, WW, C)
        row = lax.broadcasted_iota(jnp.int32, (13, WW, C), 0) + b * 13
        weight = jnp.where(row < 2, top, jnp.where(row >= 50, bot, mid))
        grad = (weight * diff).reshape(416, C)
        put3(o3_ref, s, grad)
        og_ref[pl.ds(s, 416), :] = jnp.where(own_columns(416), grad, 0.0).astype(BF16)
        return 0

    lax.fori_loop(0, 4, join, 0)
    zero_at(first, o3_ref, 0, 64)
    zero_at(last, o3_ref, 50 * WW, 64)
    contract(j3_ref, og_ref[64:1600, :], 64, WW, 1536, g_ref.at[2])
    hand_out(g_ref.at[2], keep_hbm.at[2], sent_ref.at[2], send_hbm.at[2], core, keep_sem.at[2], send_sem.at[2])
    for tap in range(9):
        kt_ref[(8 - tap) * C : (9 - tap) * C, :] = kj_ref[tap * C : (tap + 1) * C, :].T

    def back(b, _):
        s = pl.multiple_of(b * 320, 32)
        y = jnp.dot(window(o3_ref, s, 320, WW), kt_ref[...], preferred_element_type=F32)
        jg_ref[pl.ds(s, 320), :] = y.astype(BF16)
        on = ha_ref[pl.ds(pl.multiple_of(s + 64, 32), 320), :].astype(F32) > 0
        og_ref[pl.ds(s, 320), :] = jnp.where(own_columns(320) & on, y, 0.0).astype(BF16)
        return 0

    lax.fori_loop(0, 5, back, 0)
    zero_at(first, jg_ref, 0, 32)
    zero_at(last, jg_ref, 49 * WW, 32)
    contract(x3_ref, og_ref[32:1568, :], 96, WW, 1536, g_ref.at[0])
    hand_out(g_ref.at[0], keep_hbm.at[0], sent_ref.at[0], send_hbm.at[0], core, keep_sem.at[0], send_sem.at[0])
    down = down_matrix()
    for b in range(2):
        lifted = jnp.dot(down, jg_ref[b * 768 : b * 768 + 832, :], preferred_element_type=F32) * NINTH
        on = la_ref[32 + b * 128 : 160 + b * 128, :].astype(F32) > 0
        lg_ref[b * 128 : (b + 1) * 128, :] = jnp.where(on, lifted, 0.0).astype(BF16)
    contract(l3_ref, lg_ref[...], 32, LWW, 256, g_ref.at[1])
    hand_out(g_ref.at[1], keep_hbm.at[1], sent_ref.at[1], send_hbm.at[1], core, keep_sem.at[1], send_sem.at[1])
    for n in range(3):
        pltpu.make_async_copy(g_ref.at[n, 0:1152], keep_hbm.at[n], keep_sem.at[n]).wait()
        pltpu.make_async_copy(sent_ref.at[n], send_hbm.at[n], send_sem.at[n]).wait()


def regroup_lanes(parts, rows):
    quarter = lax.broadcasted_iota(jnp.int32, (rows, 128), 1) // 32
    for q in range(4):
        out = None
        for g in range(4):
            shift = ((g - q) * 32) % 128
            turned = pltpu.roll(parts[g], shift, 1) if shift else parts[g]
            out = turned if out is None else jnp.where(quarter == g, turned, out)
        yield q, out


def merge(keep_hbm, recv_ref, out_ref, keep_ref, sem):
    copies = [
        pltpu.make_async_copy(keep_hbm.at[n, pl.ds(8 * xl, 8)], keep_ref.at[n, pl.ds(8 * xl, 8)], sem.at[2 * n + xl])
        for n in range(3)
        for xl in range(2)
    ]
    for copy in copies:
        copy.start()
    for n in range(3):
        for xl in range(2):
            copies[2 * n + xl].wait()

            def one(p, _):
                blocks = []
                for g in range(4):
                    at = xl * 8 + 2 * g + p
                    blocks.append(keep_ref[n, at] + recv_ref[n, at].astype(F32))
                for h in range(2):
                    parts = [v[:, h * 128 : (h + 1) * 128] for v in blocks]
                    for q, out in regroup_lanes(parts, 72):
                        out_ref[(h * 4 + q) * 2 + xl, n * 2 + p] = out.astype(BF16)
                return 0

            lax.fori_loop(0, 2, one, 0)


def total(in_ref, out_ref):
    quarter = lax.broadcasted_iota(jnp.int32, (56, 128), 1) // 32
    for p in range(2):
        sums = []
        for n in range(3):
            acc = in_ref[0, 2 * n + p].astype(F32)
            for i in range(1, 16):
                acc = acc + in_ref[i, 2 * n + p].astype(F32)
            sums.append(acc)
        rows = jnp.concatenate(sums + [jnp.zeros((8, 128), F32)], axis=0)
        for g in range(4):
            out = None
            for s in range(4):
                shift = ((s - g) * 32) % 128
                part = rows[s * 56 : (s + 1) * 56]
                turned = pltpu.roll(part, shift, 1) if shift else part
                out = turned if out is None else jnp.where(quarter == s, turned, out)
            out_ref[2 * g + p] = out


def finish(in_ref, a_ref, b_ref, c_ref):
    acc = in_ref[0].astype(F32)
    for i in range(1, 8):
        acc = acc + in_ref[i].astype(F32)
    rows = jnp.concatenate(
        [acc if s == 0 else pltpu.roll(acc, 128 - 32 * s, 1) for s in range(4)], axis=0
    )
    for g, ref in enumerate((a_ref, b_ref, c_ref)):
        ref[...] = rows[g * 72 : (g + 1) * 72].T[0:32]


def call(kernel, out, specs, scratch=(), outs=None, name=None, vmem=None):
    return pl.pallas_call(
        kernel,
        out_shape=tuple(jax.ShapeDtypeStruct(s, d) for s, d in out),
        in_specs=list(specs),
        out_specs=outs or tuple(VMEM for _ in out),
        scratch_shapes=list(scratch),
        name=name,
        compiler_params=pltpu.CompilerParams(vmem_limit_bytes=vmem) if vmem else None,
    )


def ring(count, step):
    return [(i, (i + step) % count) for i in range(count)]


XY = ("yh", "yl", "xh", "xl")
Z = ("zh", "zm", "zl")


def body(hi, low, kh, kl, kj, tgt, land):
    dma = pltpu.SemaphoreType.DMA
    west, east, edges = call(
        pack_lon,
        [((H, 8, C), BF16)] * 2 + [((2, 7, W, C), BF16)],
        [SMEM] + [HBM] * 3,
        [pltpu.VMEM((2, H, 8, C), BF16), pltpu.VMEM((2, H, 8, C), BF16), pltpu.VMEM((LH, LW, C), BF16), dma((9,))],
        name="pack_lon",
        vmem=FULL,
    )(land, hi, tgt, low)
    from_e = lax.ppermute(west, LON, ring(32, -1))
    from_w = lax.ppermute(east, LON, ring(32, 1))
    north, south = call(
        pack_lat, [((PK, C), BF16)] * 2, [SMEM] + [VMEM] * 3, name="pack_lat", vmem=6 * MIB
    )(land, edges, from_w, from_e)
    from_s = lax.ppermute(north, LAT, ring(8, -1))
    from_n = lax.ppermute(south, LAT, ring(8, 1))
    pos = jnp.stack([lax.axis_index(LAT), lax.axis_index("core")]).astype(jnp.int32)
    keep, send = call(
        main,
        [((3, 16, 72, C), F32), ((3, 16, 72, C), BF16)],
        [SMEM] * 2 + [HBM] * 3 + [VMEM] * 4 + [HBM] * 3,
        [
            pltpu.VMEM((1792, 768), BF16),
            pltpu.VMEM((1728, 768), BF16),
            pltpu.VMEM((1664, 768), BF16),
            pltpu.VMEM((352, 768), BF16),
            pltpu.VMEM((1728, C), BF16),
            pltpu.VMEM((320, C), BF16),
            pltpu.VMEM((1664, C), BF16),
            pltpu.VMEM((1664, C), BF16),
            pltpu.VMEM((1600, C), BF16),
            pltpu.VMEM((256, C), BF16),
            pltpu.VMEM((3, 2304, C), F32),
            pltpu.VMEM((3, 16, 72, C), BF16),
            pltpu.VMEM((576, 128), BF16),
            pltpu.VMEM((H, W, C), BF16),
            pltpu.VMEM((H, W, C), BF16),
            pltpu.VMEM((LH, LW, C), BF16),
            pltpu.VMEM((2304, C), BF16),
            pltpu.VMEM((2304, C), BF16),
            pltpu.VMEM((2304, C), BF16),
            pltpu.VMEM((2304, C), BF16),
            dma((6,)),
            dma((3,)),
            dma((3,)),
        ],
        outs=(HBM, HBM),
        name="main",
        vmem=MAIN_LIMIT,
    )(pos, land, hi, tgt, low, from_w, from_e, from_n, from_s, *[k.reshape(9 * C, C) for k in (kh, kl, kj)])
    recv = lax.ppermute(send, "core", ring(2, 1))
    (parts,) = call(
        merge,
        [((16, 6, 72, 128), BF16)],
        [HBM, VMEM],
        [pltpu.VMEM((3, 16, 72, C), F32), dma((6,))],
        name="merge",
        vmem=MERGE_LIMIT,
    )(keep, recv)
    parts = lax.all_to_all(parts, XY, 0, 0, tiled=True)
    (parts,) = call(total, [((8, 56, 128), F32)], [VMEM], name="total", vmem=6 * MIB)(parts)
    parts = lax.all_to_all(parts, Z, 0, 0, tiled=True)
    grads = call(finish, [((32, 72), F32)] * 3, [VMEM], name="finish", vmem=2 * MIB)(parts)
    return tuple(g.T for g in grads)


def solution(mesh):
    fine = Mesh(mesh.devices.reshape((2,) * 8), LAT + LON)
    tile = P(LAT, LON, None)
    mapped = jax.shard_map(
        body,
        mesh=fine,
        in_specs=(tile, tile, P(), P(), P(), tile, P(LAT, LON)),
        out_specs=(P(LON, LAT),) * 3,
        check_vma=False,
    )
    return mapped
```

time: 118 us -> 103 us (0.87)
  blocking collectives: 38.9 us -> 49.2 us
  waiting for transfers between devices: 22.1 us -> 12.4 us
  Pallas kernels: 34.4 us -> 26.4 us
  starting transfers between devices: 18.3 us -> 11 us
    all_to_all x2, blocking collectives: 38.9 us -> 49.2 us  [the longest x1 29.8 us: body(): parts = lax.all_to_all(parts, XY, 0, 0, tiled=True)]
    pallas_call x8 -> x6, Pallas kernels: 34.4 us -> 26.4 us  [the longest x1 19.5 us: body(): call(main, [((3, 16, 72, C), F32), ((3, 16, 72, C), BF16)], [SMEM] * 2 +...]
    all_to_all x1 -> x0, waiting for transfers between devices: 7.09 us -> none  [step(): parts_join = lax.all_to_all(parts_join, XY, 0, 0, tiled=True)]
    all_to_all x1 -> x0, starting transfers between devices: 6.82 us -> none  [step(): parts_join = lax.all_to_all(parts_join, XY, 0, 0, tiled=True)]
    ppermute x6 -> x5, waiting for transfers between devices: 15 us -> 12.4 us  [the longest x1 3.89 us: body(): recv = lax.ppermute(send, 'core', ring(2, 1))]
    ppermute x6 -> x5, starting transfers between devices: 11.5 us -> 11 us  [the longest x1 6.3 us: body(): from_e = lax.ppermute(west, LON, ring(32, -1))]
  transfers between devices with their start and end apart: 7 -> 5, of which waited for: 5 -> 4; matrix products, arithmetic and copies ran while one was open for 0% -> 0% of each run, Pallas kernels for 5% -> 0%
where the time goes in v5:
time: 103 us; the launch traced here: 101 us
  blocking collectives  49.2 us (48%)
  Pallas kernels  26.4 us (26%)
  waiting for transfers between devices  12.4 us (12%)
  starting transfers between devices  11 us (11%)
  between operations  1.41 us (1%)
    all_to_all x1, blocking collectives, body(): parts = lax.all_to_all(parts, XY, 0, 0, tiled=True)  29.8 us
    pallas_call x1, Pallas kernels, body(): call(main, [((3, 16, 72, C), F32), ((3, 16, 72, C), BF16)], [SMEM] * 2 +...  19.5 us
    all_to_all x1, blocking collectives, body(): parts = lax.all_to_all(parts, Z, 0, 0, tiled=True)  19.5 us
    ppermute x1, starting transfers between devices, body(): from_e = lax.ppermute(west, LON, ring(32, -1))  6.3 us
    ppermute x1, waiting for transfers between devices, body(): recv = lax.ppermute(send, 'core', ring(2, 1))  3.89 us
    ppermute x1, waiting for transfers between devices, body(): from_w = lax.ppermute(east, LON, ring(32, 1))  3.47 us
    pallas_call x1, Pallas kernels, body(): call(merge, [((16, 6, 72, 128), BF16)], [HBM, VMEM], [pltpu.VMEM((3, 16,...  3.42 us
    ppermute x1, waiting for transfers between devices, body(): from_n = lax.ppermute(south, LAT, ring(8, 1))  3.13 us
  transfers between devices with their start and end apart: 5, of which 4 were waited for; matrix products, arithmetic and copies ran while one was open for 0% of the time, Pallas kernels for 0%

profile of v5, /device:TPU:8, one launch (start us, length us, event | category | flops | bytes accessed | tf_op | source)
XLA Modules:
  0.0 101.4 jit_solution(14642637714701201366)
XLA Ops:
  0.6 0.0 copy-start.1
  0.6 0.0 copy-start
  1.4 2.2 %pack_lon.1 = (bf16[48,8,256]{2,1,0:T(8,128)(2,1)}, bf16[48,8,256]{2,1,0:T(8,128)(2,1)}, bf16[2,7,24,256]{3,2,1,0:T(8,128)(2,1)}) custom-call(s32[1,1]{1,0:T(1,128)S(6)} %copy.10.land_ref, bf16[48,24,256]{2,1,0:T(8,128)(2,1)} %hi_hbm.1, bf16[48,24,256]{2,1,0:T(8,128)(2,1)} %tgt_hbm.1, bf16[16,8,256]{2,1,0:T(8,128)(2,1)} %low_hbm.1), custom_call_target="tpu_custom_call" | custom-call | tf_op jit(solution)/shard_map/pack_lon/pallas_call | solution.py:434
  3.6 0.1 collective-permute-start
  3.7 6.3 %collective-permute-start.1 = (bf16[48,8,256]{2,1,0:T(8,128)(2,1)}, bf16[48,8,256]{2,1,0:T(8,128)(2,1)S(1)}, u32[]{:S(2)}, u32[]{:S(2)}) collective-permute-start(bf16[48,8,256]{2,1,0:T(8,128)(2,1)} %get-tuple-element.14), channel_id=1, source_target_pairs={{0,31},{1,0},{2,1},{3,2},{4,3},{5,4},{6,5},{7,6},{8,7},{9,8},{10,9... | collective-permute-start | bytes 589832 | tf_op jit(solution)/shard_map/ppermute | solution.py:442
  10.0 3.5 %collective-permute-done.w_ref = bf16[48,8,256]{2,1,0:T(8,128)(2,1)S(1)} collective-permute-done((bf16[48,8,256]{2,1,0:T(8,128)(2,1)}, bf16[48,8,256]{2,1,0:T(8,128)(2,1)S(1)}, u32[]{:S(2)}, u32[]{:S(2)}) %collective-permute-start) | collective-permute-done | bytes 196640 | tf_op jit(solution)/shard_map/ppermute | solution.py:443
  13.5 0.0 collective-permute-done.1.e_ref
  13.5 0.0 copy-start.2
  13.5 0.9 copy-done.2
  14.4 0.1 pack_lat.1
  14.5 2.8 %collective-permute-start.2 = (bf16[304,256]{1,0:T(8,128)(2,1)S(1)}, bf16[304,256]{1,0:T(8,128)(2,1)S(1)}, u32[]{:S(2)}, u32[]{:S(2)}) collective-permute-start(bf16[304,256]{1,0:T(8,128)(2,1)S(1)} %get-tuple-element.16), channel_id=1, source_target_pairs={{0,32},{32,64},{64,96},{96,128},{128,160},{160,192},{192,224},{224... | collective-permute-start | bytes 466952 | tf_op jit(solution)/shard_map/ppermute | solution.py:448
  17.3 1.7 %collective-permute-start.3 = (bf16[304,256]{1,0:T(8,128)(2,1)S(1)}, bf16[304,256]{1,0:T(8,128)(2,1)S(1)}, u32[]{:S(2)}, u32[]{:S(2)}) collective-permute-start(bf16[304,256]{1,0:T(8,128)(2,1)S(1)} %get-tuple-element.17), channel_id=1, source_target_pairs={{0,224},{32,0},{64,32},{96,64},{128,96},{160,128},{192,160},{224,1... | collective-permute-start | bytes 466952 | tf_op jit(solution)/shard_map/ppermute | solution.py:447
  19.0 0.1 pad_add_fusion.pos_ref
  19.1 3.1 %collective-permute-done.2.n_ref = bf16[304,256]{1,0:T(8,128)(2,1)S(1)} collective-permute-done((bf16[304,256]{1,0:T(8,128)(2,1)S(1)}, bf16[304,256]{1,0:T(8,128)(2,1)S(1)}, u32[]{:S(2)}, u32[]{:S(2)}) %collective-permute-start.2) | collective-permute-done | bytes 155680 | tf_op jit(solution)/shard_map/ppermute | solution.py:448
  22.2 1.8 %collective-permute-done.3.s_ref = bf16[304,256]{1,0:T(8,128)(2,1)S(1)} collective-permute-done((bf16[304,256]{1,0:T(8,128)(2,1)S(1)}, bf16[304,256]{1,0:T(8,128)(2,1)S(1)}, u32[]{:S(2)}, u32[]{:S(2)}) %collective-permute-start.3) | collective-permute-done | bytes 155680 | tf_op jit(solution)/shard_map/ppermute | solution.py:447
  24.0 0.0 copy-done.1
  24.0 0.0 copy-done
  24.1 19.5 %main.1 = (f32[3,16,72,256]{3,2,1,0:T(8,128)}, bf16[3,16,72,256]{3,2,1,0:T(8,128)(2,1)}) custom-call(s32[2]{0:T(128)S(1)} %pad_add_fusion.pos_ref, s32[1,1]{1,0:T(1,128)S(6)} %copy.10.land_ref, bf16[48,24,256]{2,1,0:T(8,128)(2,1)S(1)} %copy-done, bf16[48,24,256]{2,1,0:T(8,128)(2,1)} %tgt_hbm.1, bf16[16,8,256]{2,1,0:T(8,128)(2,1)S(1)} %copy-done.1, ...), custom_call_target="tpu_custom_call" | custom-call | tf_op jit(solution)/shard_map/main/pallas_call | solution.py:450
  43.6 0.1 collective-permute-start.4
  43.7 3.9 %collective-permute-done.4.recv_ref = bf16[3,16,72,256]{3,2,1,0:T(8,128)(2,1)S(1)} collective-permute-done((bf16[3,16,72,256]{3,2,1,0:T(8,128)(2,1)}, bf16[3,16,72,256]{3,2,1,0:T(8,128)(2,1)S(1)}, u32[]{:S(2)}, u32[]{:S(2)}) %collective-permute-start.4) | collective-permute-done | bytes 1769504 | tf_op jit(solution)/shard_map/ppermute | solution.py:483
  47.6 3.4 %merge.1 = bf16[16,6,72,128]{3,2,1,0:T(8,128)(2,1)S(1)} custom-call(f32[3,16,72,256]{3,2,1,0:T(8,128)} %get-tuple-element.18.keep_hbm, bf16[3,16,72,256]{3,2,1,0:T(8,128)(2,1)S(1)} %collective-permute-done.4.recv_ref), custom_call_target="tpu_custom_call" | custom-call | tf_op jit(solution)/shard_map/merge/pallas_call | solution.py:484
  51.0 29.8 %all_to_all.10.in_ref = bf16[16,6,72,128]{3,2,1,0:T(8,128)(2,1)S(1)} all-to-all(bf16[16,6,72,128]{3,2,1,0:T(8,128)(2,1)S(1)} %merge.1), channel_id=1, replica_groups=mesh['yh'=2,'yl'=2,'xh'=2,'zh'=2,'zm'=2,'zl'=2,'xl'=2,'core'=2] {'yh','y..., dimensions={0} | all-to-all | bytes 3538944 | tf_op jit(solution)/shard_map/all_to_all | solution.py:492
  80.8 0.4 total.1
  81.2 19.5 %all_to_all.11.in_ref = f32[8,56,128]{2,1,0:T(8,128)S(1)} all-to-all(f32[8,56,128]{2,1,0:T(8,128)S(1)} %total.1), channel_id=1, replica_groups=mesh['yh'=2,'yl'=2,'xh'=2,'zh'=2,'zm'=2,'zl'=2,'xl'=2,'core'=2] {'zh','z..., dimensions={0} | all-to-all | bytes 458752 | tf_op jit(solution)/shard_map/all_to_all | solution.py:494
  100.6 0.8 finish.1
Async XLA Ops:
  0.6 23.4 %copy-start.1 = (bf16[16,8,256]{2,1,0:T(8,128)(2,1)S(1)}, bf16[16,8,256]{2,1,0:T(8,128)(2,1)}, u32[]{:S(2)}) copy-start(bf16[16,8,256]{2,1,0:T(8,128)(2,1)} %low_hbm.1) | copy-start | bytes 196612
  0.6 23.4 %copy-start = (bf16[48,24,256]{2,1,0:T(8,128)(2,1)S(1)}, bf16[48,24,256]{2,1,0:T(8,128)(2,1)}, u32[]{:S(2)}) copy-start(bf16[48,24,256]{2,1,0:T(8,128)(2,1)} %hi_hbm.1) | copy-start | bytes 1769476
  3.6 9.9 %collective-permute-start = (bf16[48,8,256]{2,1,0:T(8,128)(2,1)}, bf16[48,8,256]{2,1,0:T(8,128)(2,1)S(1)}, u32[]{:S(2)}, u32[]{:S(2)}) collective-permute-start(bf16[48,8,256]{2,1,0:T(8,128)(2,1)} %get-tuple-element.13), channel_id=1, source_target_pairs={{0,1},{1,2},{2,3},{3,4},{4,5},{5,6},{6,7},{7,8},{8,9},{9,10},{10,1... | collective-permute-start | bytes 589832 | tf_op jit(solution)/shard_map/ppermute | solution.py:443
  3.7 9.8 %collective-permute-start.1 = (bf16[48,8,256]{2,1,0:T(8,128)(2,1)}, bf16[48,8,256]{2,1,0:T(8,128)(2,1)S(1)}, u32[]{:S(2)}, u32[]{:S(2)}) collective-permute-start(bf16[48,8,256]{2,1,0:T(8,128)(2,1)} %get-tuple-element.14), channel_id=1, source_target_pairs={{0,31},{1,0},{2,1},{3,2},{4,3},{5,4},{6,5},{7,6},{8,7},{9,8},{10,9... | collective-permute-start | bytes 589832 | tf_op jit(solution)/shard_map/ppermute | solution.py:442
  13.5 0.9 copy-start.2
  14.5 7.7 %collective-permute-start.2 = (bf16[304,256]{1,0:T(8,128)(2,1)S(1)}, bf16[304,256]{1,0:T(8,128)(2,1)S(1)}, u32[]{:S(2)}, u32[]{:S(2)}) collective-permute-start(bf16[304,256]{1,0:T(8,128)(2,1)S(1)} %get-tuple-element.16), channel_id=1, source_target_pairs={{0,32},{32,64},{64,96},{96,128},{128,160},{160,192},{192,224},{224... | collective-permute-start | bytes 466952 | tf_op jit(solution)/shard_map/ppermute | solution.py:448
  17.3 6.7 %collective-permute-start.3 = (bf16[304,256]{1,0:T(8,128)(2,1)S(1)}, bf16[304,256]{1,0:T(8,128)(2,1)S(1)}, u32[]{:S(2)}, u32[]{:S(2)}) collective-permute-start(bf16[304,256]{1,0:T(8,128)(2,1)S(1)} %get-tuple-element.17), channel_id=1, source_target_pairs={{0,224},{32,0},{64,32},{96,64},{128,96},{160,128},{192,160},{224,1... | collective-permute-start | bytes 466952 | tf_op jit(solution)/shard_map/ppermute | solution.py:447
  43.6 4.0 %collective-permute-start.4 = (bf16[3,16,72,256]{3,2,1,0:T(8,128)(2,1)}, bf16[3,16,72,256]{3,2,1,0:T(8,128)(2,1)S(1)}, u32[]{:S(2)}, u32[]{:S(2)}) collective-permute-start(bf16[3,16,72,256]{3,2,1,0:T(8,128)(2,1)} %get-tuple-element.19), channel_id=1, source_target_pairs={{0,1},{1,0},{2,3},{3,2},{4,5},{5,4},{6,7},{7,6},{8,9},{9,8},{10,11... | collective-permute-start | bytes 5308424 | tf_op jit(solution)/shard_map/ppermute | solution.py:483

commit v6 on v5

--- a/solution.py
+++ b/solution.py
@@ -192,11 +192,8 @@
     for t in range(16):
         pltpu.make_async_copy(g_ref.at[pl.ds(block_start(t, core), 72)], keep_hbm.at[t], keep_sem).start()
 
-    def one(t, _):
+    for t in range(16):
         sent_ref[t] = g_ref[pl.ds(block_start(t, 1 - core), 72), :].astype(BF16)
-        return 0
-
-    lax.fori_loop(0, 16, one, 0)
     pltpu.make_async_copy(sent_ref, send_hbm, send_sem).start()
 
 
@@ -236,28 +233,36 @@
     zero_at(first, x3_ref, 0, 128)
     zero_at(last, x3_ref, 1664, 128)
     fetch_low.wait()
+    fetch_kl.wait()
+    fetch_hi.wait()
     put3(
         l3_ref,
         48,
         widen_low(low_v[...].astype(F32), w_ref[...].astype(F32), e_ref[...].astype(F32)).reshape(256, C),
     )
-    fetch_hi.wait()
-
     def widen_rows(t, _):
         rows = pl.ds(pl.multiple_of(t * 8, 8), 8)
         wide = widen_hi(hi_v[rows].astype(F32), w_ref[rows].astype(F32), e_ref[rows].astype(F32))
         put3(x3_ref, pl.multiple_of(128 + t * 256, 128), wide.reshape(256, C))
         return 0
 
-    lax.fori_loop(0, 6, widen_rows, 0)
-    fetch_kl.wait()
+    lax.fori_loop(0, 6, widen_rows, 0, unroll=True)
     la_ref[...] = jnp.maximum(
         jnp.dot(window(l3_ref, 0, 320, LWW), kl_ref[...], preferred_element_type=F32), 0.0
     ).astype(BF16)
     zero_at(first, la_ref, 0, 32)
     zero_at(last, la_ref, 288, 32)
+    fetch_tgt.wait()
     fetch_kh.wait()
-
+    tg_ref[0:64, :] = n_ref[128:192, :]
+    tg_ref[1600:1664, :] = s_ref[128:192, :]
+    def widen_targets(t, _):
+        rows = pl.ds(pl.multiple_of(t * 8, 8), 8)
+        wide = widen_tgt(tgt_v[rows].astype(F32), w_ref[rows].astype(F32), e_ref[rows].astype(F32))
+        tg_ref[pl.ds(pl.multiple_of(64 + t * 256, 64), 256), :] = wide.reshape(256, C).astype(BF16)
+        return 0
+
+    lax.fori_loop(0, 6, widen_targets, 0, unroll=True)
     def high(b, _):
         s = pl.multiple_of(b * 576, 64)
         act = jnp.maximum(
@@ -269,20 +274,9 @@
         put3(j3_ref, s, act.astype(F32) + lift)
         return 0
 
-    lax.fori_loop(0, 3, high, 0)
+    lax.fori_loop(0, 3, high, 0, unroll=True)
     zero_at(first, j3_ref, 0, 96)
     zero_at(last, j3_ref, 51 * WW, 96)
-    tg_ref[0:64, :] = n_ref[128:192, :]
-    tg_ref[1600:1664, :] = s_ref[128:192, :]
-    fetch_tgt.wait()
-
-    def widen_targets(t, _):
-        rows = pl.ds(pl.multiple_of(t * 8, 8), 8)
-        wide = widen_tgt(tgt_v[rows].astype(F32), w_ref[rows].astype(F32), e_ref[rows].astype(F32))
-        tg_ref[pl.ds(pl.multiple_of(64 + t * 256, 64), 256), :] = wide.reshape(256, C).astype(BF16)
-        return 0
-
-    lax.fori_loop(0, 6, widen_targets, 0)
     fetch_kj.wait()
 
     def weight_of(high_part, low_part):
@@ -298,17 +292,17 @@
     bot = weight_of(s_ref[240:272, :].astype(F32), s_ref[272:304, :].astype(F32))
 
     def join(b, _):
-        s = pl.multiple_of(b * 416, 32)
-        y = jnp.dot(window(j3_ref, s, 416, WW), kj_ref[...], preferred_element_type=F32)
-        diff = (y - tg_ref[pl.ds(s, 416), :].astype(F32)).reshape(13, WW, C)
-        row = lax.broadcasted_iota(jnp.int32, (13, WW, C), 0) + b * 13
+        s = pl.multiple_of(b * 832, 32)
+        y = jnp.dot(window(j3_ref, s, 832, WW), kj_ref[...], preferred_element_type=F32)
+        diff = (y - tg_ref[pl.ds(s, 832), :].astype(F32)).reshape(26, WW, C)
+        row = lax.broadcasted_iota(jnp.int32, (26, WW, C), 0) + b * 26
         weight = jnp.where(row < 2, top, jnp.where(row >= 50, bot, mid))
-        grad = (weight * diff).reshape(416, C)
+        grad = (weight * diff).reshape(832, C)
         put3(o3_ref, s, grad)
-        og_ref[pl.ds(s, 416), :] = jnp.where(own_columns(416), grad, 0.0).astype(BF16)
+        og_ref[pl.ds(s, 832), :] = jnp.where(own_columns(832), grad, 0.0).astype(BF16)
         return 0
 
-    lax.fori_loop(0, 4, join, 0)
+    lax.fori_loop(0, 2, join, 0, unroll=True)
     zero_at(first, o3_ref, 0, 64)
     zero_at(last, o3_ref, 50 * WW, 64)
     contract(j3_ref, og_ref[64:1600, :], 64, WW, 1536, g_ref.at[2])
@@ -317,14 +311,14 @@
         kt_ref[(8 - tap) * C : (9 - tap) * C, :] = kj_ref[tap * C : (tap + 1) * C, :].T
 
     def back(b, _):
-        s = pl.multiple_of(b * 320, 32)
-        y = jnp.dot(window(o3_ref, s, 320, WW), kt_ref[...], preferred_element_type=F32)
-        jg_ref[pl.ds(s, 320), :] = y.astype(BF16)
-        on = ha_ref[pl.ds(pl.multiple_of(s + 64, 32), 320), :].astype(F32) > 0
-        og_ref[pl.ds(s, 320), :] = jnp.where(own_columns(320) & on, y, 0.0).astype(BF16)
+        s = pl.multiple_of(b * 800, 32)
+        y = jnp.dot(window(o3_ref, s, 800, WW), kt_ref[...], preferred_element_type=F32)
+        jg_ref[pl.ds(s, 800), :] = y.astype(BF16)
+        on = ha_ref[pl.ds(pl.multiple_of(s + 64, 32), 800), :].astype(F32) > 0
+        og_ref[pl.ds(s, 800), :] = jnp.where(own_columns(800) & on, y, 0.0).astype(BF16)
         return 0
 
-    lax.fori_loop(0, 5, back, 0)
+    lax.fori_loop(0, 2, back, 0, unroll=True)
     zero_at(first, jg_ref, 0, 32)
     zero_at(last, jg_ref, 49 * WW, 32)
     contract(x3_ref, og_ref[32:1568, :], 96, WW, 1536, g_ref.at[0])
@@ -372,7 +366,7 @@
                 for h in range(2):
                     parts = [v[:, h * 128 : (h + 1) * 128] for v in blocks]
                     for q, out in regroup_lanes(parts, 72):
-                        out_ref[(h * 4 + q) * 2 + xl, n * 2 + p] = out.astype(BF16)
+                        out_ref[(h * 4 + q) * 4 + 2 * xl + p, n] = out.astype(BF16)
                 return 0
 
             lax.fori_loop(0, 2, one, 0)
@@ -380,27 +374,26 @@
 
 def total(in_ref, out_ref):
     quarter = lax.broadcasted_iota(jnp.int32, (56, 128), 1) // 32
-    for p in range(2):
-        sums = []
-        for n in range(3):
-            acc = in_ref[0, 2 * n + p].astype(F32)
-            for i in range(1, 16):
-                acc = acc + in_ref[i, 2 * n + p].astype(F32)
-            sums.append(acc)
-        rows = jnp.concatenate(sums + [jnp.zeros((8, 128), F32)], axis=0)
-        for g in range(4):
-            out = None
-            for s in range(4):
-                shift = ((s - g) * 32) % 128
-                part = rows[s * 56 : (s + 1) * 56]
-                turned = pltpu.roll(part, shift, 1) if shift else part
-                out = turned if out is None else jnp.where(quarter == s, turned, out)
-            out_ref[2 * g + p] = out
+    sums = []
+    for n in range(3):
+        acc = in_ref[0, n].astype(F32)
+        for i in range(1, 32):
+            acc = acc + in_ref[i, n].astype(F32)
+        sums.append(acc)
+    rows = jnp.concatenate(sums + [jnp.zeros((8, 128), F32)], axis=0)
+    for g in range(4):
+        out = None
+        for s in range(4):
+            shift = ((s - g) * 32) % 128
+            part = rows[s * 56 : (s + 1) * 56]
+            turned = pltpu.roll(part, shift, 1) if shift else part
+            out = turned if out is None else jnp.where(quarter == s, turned, out)
+        out_ref[g] = out
 
 
 def finish(in_ref, a_ref, b_ref, c_ref):
     acc = in_ref[0].astype(F32)
-    for i in range(1, 8):
+    for i in range(1, 4):
         acc = acc + in_ref[i].astype(F32)
     rows = jnp.concatenate(
         [acc if s == 0 else pltpu.roll(acc, 128 - 32 * s, 1) for s in range(4)], axis=0
@@ -425,8 +418,8 @@
     return [(i, (i + step) % count) for i in range(count)]
 
 
-XY = ("yh", "yl", "xh", "xl")
-Z = ("zh", "zm", "zl")
+FIRST = ("yh", "yl", "xh", "xl", "zl")
+SECOND = ("zh", "zm")
 
 
 def body(hi, low, kh, kl, kj, tgt, land):
@@ -483,15 +476,15 @@
     recv = lax.ppermute(send, "core", ring(2, 1))
     (parts,) = call(
         merge,
-        [((16, 6, 72, 128), BF16)],
+        [((32, 3, 72, 128), BF16)],
         [HBM, VMEM],
         [pltpu.VMEM((3, 16, 72, C), F32), dma((6,))],
         name="merge",
         vmem=MERGE_LIMIT,
     )(keep, recv)
-    parts = lax.all_to_all(parts, XY, 0, 0, tiled=True)
-    (parts,) = call(total, [((8, 56, 128), F32)], [VMEM], name="total", vmem=6 * MIB)(parts)
-    parts = lax.all_to_all(parts, Z, 0, 0, tiled=True)
+    parts = lax.all_to_all(parts, FIRST, 0, 0, tiled=True)
+    (parts,) = call(total, [((4, 56, 128), F32)], [VMEM], name="total", vmem=6 * MIB)(parts)
+    parts = lax.all_to_all(parts, SECOND, 0, 0, tiled=True)
     grads = call(finish, [((32, 72), F32)] * 3, [VMEM], name="finish", vmem=2 * MIB)(parts)
     return tuple(g.T for g in grads)
 

time: 103 us -> 101 us (0.981)
  no operation moved by 1% of the time
where the time goes in v6:
time: 101 us; the launch traced here: 99.7 us
  blocking collectives  48.3 us (48%)
  Pallas kernels  25.6 us (25%)
  waiting for transfers between devices  12.4 us (12%)
  starting transfers between devices  11 us (11%)
  between operations  1.41 us (1%)
    all_to_all x1, blocking collectives, body(): parts = lax.all_to_all(parts, FIRST, 0, 0, tiled=True)  31.4 us
    pallas_call x1, Pallas kernels, body(): call(main, [((3, 16, 72, C), F32), ((3, 16, 72, C), BF16)], [SMEM] * 2 +...  18.7 us
    all_to_all x1, blocking collectives, body(): parts = lax.all_to_all(parts, SECOND, 0, 0, tiled=True)  16.9 us
    ppermute x1, starting transfers between devices, body(): from_e = lax.ppermute(west, LON, ring(32, -1))  6.3 us
    ppermute x1, waiting for transfers between devices, body(): recv = lax.ppermute(send, 'core', ring(2, 1))  3.89 us
    ppermute x1, waiting for transfers between devices, body(): from_w = lax.ppermute(east, LON, ring(32, 1))  3.47 us
    pallas_call x1, Pallas kernels, body(): call(merge, [((32, 3, 72, 128), BF16)], [HBM, VMEM], [pltpu.VMEM((3, 16,...  3.42 us
    ppermute x1, waiting for transfers between devices, body(): from_n = lax.ppermute(south, LAT, ring(8, 1))  3.13 us
  transfers between devices with their start and end apart: 5, of which 4 were waited for; matrix products, arithmetic and copies ran while one was open for 0% of the time, Pallas kernels for 0%

profile of v6, /device:TPU:8, one launch (start us, length us, event | category | flops | bytes accessed | tf_op | source)
XLA Modules:
  0.0 99.7 jit_solution(9792572032004428881)
XLA Ops:
  0.6 0.0 copy-start.1
  0.6 0.0 copy-start
  1.4 2.2 %pack_lon.1 = (bf16[48,8,256]{2,1,0:T(8,128)(2,1)}, bf16[48,8,256]{2,1,0:T(8,128)(2,1)}, bf16[2,7,24,256]{3,2,1,0:T(8,128)(2,1)}) custom-call(s32[1,1]{1,0:T(1,128)S(6)} %copy.10.land_ref, bf16[48,24,256]{2,1,0:T(8,128)(2,1)} %hi_hbm.1, bf16[48,24,256]{2,1,0:T(8,128)(2,1)} %tgt_hbm.1, bf16[16,8,256]{2,1,0:T(8,128)(2,1)} %low_hbm.1), custom_call_target="tpu_custom_call" | custom-call | tf_op jit(solution)/shard_map/pack_lon/pallas_call | solution.py:427
  3.6 0.1 collective-permute-start
  3.7 6.3 %collective-permute-start.1 = (bf16[48,8,256]{2,1,0:T(8,128)(2,1)}, bf16[48,8,256]{2,1,0:T(8,128)(2,1)S(1)}, u32[]{:S(2)}, u32[]{:S(2)}) collective-permute-start(bf16[48,8,256]{2,1,0:T(8,128)(2,1)} %get-tuple-element.14), channel_id=1, source_target_pairs={{0,31},{1,0},{2,1},{3,2},{4,3},{5,4},{6,5},{7,6},{8,7},{9,8},{10,9... | collective-permute-start | bytes 589832 | tf_op jit(solution)/shard_map/ppermute | solution.py:435
  10.0 3.5 %collective-permute-done.w_ref = bf16[48,8,256]{2,1,0:T(8,128)(2,1)S(1)} collective-permute-done((bf16[48,8,256]{2,1,0:T(8,128)(2,1)}, bf16[48,8,256]{2,1,0:T(8,128)(2,1)S(1)}, u32[]{:S(2)}, u32[]{:S(2)}) %collective-permute-start) | collective-permute-done | bytes 196640 | tf_op jit(solution)/shard_map/ppermute | solution.py:436
  13.5 0.0 collective-permute-done.1.e_ref
  13.5 0.0 copy-start.2
  13.5 0.9 copy-done.2
  14.4 0.1 pack_lat.1
  14.5 2.8 %collective-permute-start.2 = (bf16[304,256]{1,0:T(8,128)(2,1)S(1)}, bf16[304,256]{1,0:T(8,128)(2,1)S(1)}, u32[]{:S(2)}, u32[]{:S(2)}) collective-permute-start(bf16[304,256]{1,0:T(8,128)(2,1)S(1)} %get-tuple-element.16), channel_id=1, source_target_pairs={{0,32},{32,64},{64,96},{96,128},{128,160},{160,192},{192,224},{224... | collective-permute-start | bytes 466952 | tf_op jit(solution)/shard_map/ppermute | solution.py:441
  17.3 1.7 %collective-permute-start.3 = (bf16[304,256]{1,0:T(8,128)(2,1)S(1)}, bf16[304,256]{1,0:T(8,128)(2,1)S(1)}, u32[]{:S(2)}, u32[]{:S(2)}) collective-permute-start(bf16[304,256]{1,0:T(8,128)(2,1)S(1)} %get-tuple-element.17), channel_id=1, source_target_pairs={{0,224},{32,0},{64,32},{96,64},{128,96},{160,128},{192,160},{224,1... | collective-permute-start | bytes 466952 | tf_op jit(solution)/shard_map/ppermute | solution.py:440
  19.0 0.1 pad_add_fusion.pos_ref
  19.1 3.1 %collective-permute-done.2.n_ref = bf16[304,256]{1,0:T(8,128)(2,1)S(1)} collective-permute-done((bf16[304,256]{1,0:T(8,128)(2,1)S(1)}, bf16[304,256]{1,0:T(8,128)(2,1)S(1)}, u32[]{:S(2)}, u32[]{:S(2)}) %collective-permute-start.2) | collective-permute-done | bytes 155680 | tf_op jit(solution)/shard_map/ppermute | solution.py:441
  22.2 1.8 %collective-permute-done.3.s_ref = bf16[304,256]{1,0:T(8,128)(2,1)S(1)} collective-permute-done((bf16[304,256]{1,0:T(8,128)(2,1)S(1)}, bf16[304,256]{1,0:T(8,128)(2,1)S(1)}, u32[]{:S(2)}, u32[]{:S(2)}) %collective-permute-start.3) | collective-permute-done | bytes 155680 | tf_op jit(solution)/shard_map/ppermute | solution.py:440
  24.0 0.0 copy-done.1
  24.0 0.0 copy-done
  24.1 18.7 %main.1 = (f32[3,16,72,256]{3,2,1,0:T(8,128)}, bf16[3,16,72,256]{3,2,1,0:T(8,128)(2,1)}) custom-call(s32[2]{0:T(128)S(1)} %pad_add_fusion.pos_ref, s32[1,1]{1,0:T(1,128)S(6)} %copy.10.land_ref, bf16[48,24,256]{2,1,0:T(8,128)(2,1)S(1)} %copy-done, bf16[48,24,256]{2,1,0:T(8,128)(2,1)} %tgt_hbm.1, bf16[16,8,256]{2,1,0:T(8,128)(2,1)S(1)} %copy-done.1, ...), custom_call_target="tpu_custom_call" | custom-call | tf_op jit(solution)/shard_map/main/pallas_call | solution.py:443
  42.8 0.1 collective-permute-start.4
  42.9 3.9 %collective-permute-done.4.recv_ref = bf16[3,16,72,256]{3,2,1,0:T(8,128)(2,1)S(1)} collective-permute-done((bf16[3,16,72,256]{3,2,1,0:T(8,128)(2,1)}, bf16[3,16,72,256]{3,2,1,0:T(8,128)(2,1)S(1)}, u32[]{:S(2)}, u32[]{:S(2)}) %collective-permute-start.4) | collective-permute-done | bytes 1769504 | tf_op jit(solution)/shard_map/ppermute | solution.py:476
  46.8 3.4 %merge.1 = bf16[32,3,72,128]{3,2,1,0:T(8,128)(2,1)S(1)} custom-call(f32[3,16,72,256]{3,2,1,0:T(8,128)} %get-tuple-element.18.keep_hbm, bf16[3,16,72,256]{3,2,1,0:T(8,128)(2,1)S(1)} %collective-permute-done.4.recv_ref), custom_call_target="tpu_custom_call" | custom-call | tf_op jit(solution)/shard_map/merge/pallas_call | solution.py:477
  50.2 31.4 %all_to_all.10.in_ref = bf16[32,3,72,128]{3,2,1,0:T(8,128)(2,1)S(1)} all-to-all(bf16[32,3,72,128]{3,2,1,0:T(8,128)(2,1)S(1)} %merge.1), channel_id=1, replica_groups=mesh['yh'=2,'yl'=2,'xh'=2,'zh'=2,'zm'=2,'zl'=2,'xl'=2,'core'=2] {'yh','y..., dimensions={0} | all-to-all | bytes 3538944 | tf_op jit(solution)/shard_map/all_to_all | solution.py:485
  81.6 0.4 total.1
  81.9 16.9 %all_to_all.11.in_ref = f32[4,56,128]{2,1,0:T(8,128)S(1)} all-to-all(f32[4,56,128]{2,1,0:T(8,128)S(1)} %total.1), channel_id=1, replica_groups=mesh['yh'=2,'yl'=2,'xh'=2,'zh'=2,'zm'=2,'zl'=2,'xl'=2,'core'=2] {'zh','zm'}, dimensions={0} | all-to-all | bytes 229376 | tf_op jit(solution)/shard_map/all_to_all | solution.py:487
  98.9 0.8 finish.1
Async XLA Ops:
  0.6 23.4 %copy-start.1 = (bf16[16,8,256]{2,1,0:T(8,128)(2,1)S(1)}, bf16[16,8,256]{2,1,0:T(8,128)(2,1)}, u32[]{:S(2)}) copy-start(bf16[16,8,256]{2,1,0:T(8,128)(2,1)} %low_hbm.1) | copy-start | bytes 196612
  0.6 23.4 %copy-start = (bf16[48,24,256]{2,1,0:T(8,128)(2,1)S(1)}, bf16[48,24,256]{2,1,0:T(8,128)(2,1)}, u32[]{:S(2)}) copy-start(bf16[48,24,256]{2,1,0:T(8,128)(2,1)} %hi_hbm.1) | copy-start | bytes 1769476
  3.6 9.9 %collective-permute-start = (bf16[48,8,256]{2,1,0:T(8,128)(2,1)}, bf16[48,8,256]{2,1,0:T(8,128)(2,1)S(1)}, u32[]{:S(2)}, u32[]{:S(2)}) collective-permute-start(bf16[48,8,256]{2,1,0:T(8,128)(2,1)} %get-tuple-element.13), channel_id=1, source_target_pairs={{0,1},{1,2},{2,3},{3,4},{4,5},{5,6},{6,7},{7,8},{8,9},{9,10},{10,1... | collective-permute-start | bytes 589832 | tf_op jit(solution)/shard_map/ppermute | solution.py:436
  3.7 9.8 %collective-permute-start.1 = (bf16[48,8,256]{2,1,0:T(8,128)(2,1)}, bf16[48,8,256]{2,1,0:T(8,128)(2,1)S(1)}, u32[]{:S(2)}, u32[]{:S(2)}) collective-permute-start(bf16[48,8,256]{2,1,0:T(8,128)(2,1)} %get-tuple-element.14), channel_id=1, source_target_pairs={{0,31},{1,0},{2,1},{3,2},{4,3},{5,4},{6,5},{7,6},{8,7},{9,8},{10,9... | collective-permute-start | bytes 589832 | tf_op jit(solution)/shard_map/ppermute | solution.py:435
  13.5 0.9 copy-start.2
  14.5 7.7 %collective-permute-start.2 = (bf16[304,256]{1,0:T(8,128)(2,1)S(1)}, bf16[304,256]{1,0:T(8,128)(2,1)S(1)}, u32[]{:S(2)}, u32[]{:S(2)}) collective-permute-start(bf16[304,256]{1,0:T(8,128)(2,1)S(1)} %get-tuple-element.16), channel_id=1, source_target_pairs={{0,32},{32,64},{64,96},{96,128},{128,160},{160,192},{192,224},{224... | collective-permute-start | bytes 466952 | tf_op jit(solution)/shard_map/ppermute | solution.py:441
  17.3 6.7 %collective-permute-start.3 = (bf16[304,256]{1,0:T(8,128)(2,1)S(1)}, bf16[304,256]{1,0:T(8,128)(2,1)S(1)}, u32[]{:S(2)}, u32[]{:S(2)}) collective-permute-start(bf16[304,256]{1,0:T(8,128)(2,1)S(1)} %get-tuple-element.17), channel_id=1, source_target_pairs={{0,224},{32,0},{64,32},{96,64},{128,96},{160,128},{192,160},{224,1... | collective-permute-start | bytes 466952 | tf_op jit(solution)/shard_map/ppermute | solution.py:440
  42.8 4.0 %collective-permute-start.4 = (bf16[3,16,72,256]{3,2,1,0:T(8,128)(2,1)}, bf16[3,16,72,256]{3,2,1,0:T(8,128)(2,1)S(1)}, u32[]{:S(2)}, u32[]{:S(2)}) collective-permute-start(bf16[3,16,72,256]{3,2,1,0:T(8,128)(2,1)} %get-tuple-element.19), channel_id=1, source_target_pairs={{0,1},{1,0},{2,3},{3,2},{4,5},{5,4},{6,7},{7,6},{8,9},{9,8},{10,11... | collective-permute-start | bytes 5308424 | tf_op jit(solution)/shard_map/ppermute | solution.py:476

commit v7 on v6

--- a/solution.py
+++ b/solution.py
@@ -197,28 +197,74 @@
     pltpu.make_async_copy(sent_ref, send_hbm, send_sem).start()
 
 
+def inner(hi_hbm, tgt_hbm, w_ref, e_ref, kh_hbm, x3_hbm, ha_hbm, tgw_hbm, x3_ref, ha_ref, tgw_ref, hi_v, tgt_v, kh_ref, sem):
+    fetch = [
+        pltpu.make_async_copy(src, dst, sem.at[n])
+        for n, (src, dst) in enumerate(((hi_hbm, hi_v), (kh_hbm, kh_ref), (tgt_hbm, tgt_v)))
+    ]
+    for copy in fetch:
+        copy.start()
+    leave = [
+        pltpu.make_async_copy(src, dst, sem.at[3 + n])
+        for n, (src, dst) in enumerate(((x3_ref, x3_hbm), (tgw_ref, tgw_hbm), (ha_ref, ha_hbm)))
+    ]
+    fetch[0].wait()
+
+    def widen_rows(t, _):
+        rows = pl.ds(pl.multiple_of(t * 8, 8), 8)
+        wide = widen_hi(hi_v[rows].astype(F32), w_ref[rows].astype(F32), e_ref[rows].astype(F32))
+        put3(x3_ref, pl.multiple_of(t * 256, 128), wide.reshape(256, C))
+        return 0
+
+    lax.fori_loop(0, 6, widen_rows, 0)
+    leave[0].start()
+    fetch[1].wait()
+    fetch[2].wait()
+
+    def widen_targets(t, _):
+        rows = pl.ds(pl.multiple_of(t * 8, 8), 8)
+        wide = widen_tgt(tgt_v[rows].astype(F32), w_ref[rows].astype(F32), e_ref[rows].astype(F32))
+        tgw_ref[pl.ds(pl.multiple_of(t * 256, 128), 256), :] = wide.reshape(256, C).astype(BF16)
+        return 0
+
+    def conv(b, _):
+        s = pl.multiple_of(b * 736, 32)
+        ha_ref[pl.ds(s, 736), :] = jnp.maximum(
+            jnp.dot(window(x3_ref, s, 736, WW), kh_ref[...], preferred_element_type=F32), 0.0
+        ).astype(BF16)
+        return 0
+
+    lax.fori_loop(0, 6, widen_targets, 0, unroll=True)
+    lax.fori_loop(0, 2, conv, 0, unroll=True)
+    leave[1].start()
+    leave[2].start()
+    for copy in leave:
+        copy.wait()
+
+
 def main(
-    pos_ref, land_ref, hi_hbm, tgt_hbm, low_hbm, w_ref, e_ref, n_ref, s_ref, kh_hbm, kl_hbm, kj_hbm,
+    pos_ref, land_ref, low_hbm, w_ref, e_ref, n_ref, s_ref, x3_hbm, ha_hbm, tgw_hbm, kh_hbm, kl_hbm, kj_hbm,
     keep_hbm, send_hbm,
     x3_ref, j3_ref, o3_ref, l3_ref, ha_ref, la_ref, og_ref, tg_ref, jg_ref, lg_ref, g_ref, sent_ref, up_ref,
-    hi_v, tgt_v, low_v, kh_ref, kl_ref, kj_ref, kt_ref, sem, keep_sem, send_sem,
+    low_v, kh_ref, kl_ref, kj_ref, kt_ref, sem, keep_sem, send_sem,
 ):
     fetch = [
         pltpu.make_async_copy(src, dst, sem.at[n])
         for n, (src, dst) in enumerate(
             (
                 (low_hbm, low_v),
-                (hi_hbm, hi_v),
                 (kl_hbm, kl_ref),
                 (kh_hbm, kh_ref),
-                (tgt_hbm, tgt_v),
+                (x3_hbm, x3_ref.at[128:1664]),
+                (ha_hbm, ha_ref.at[128:1600]),
                 (kj_hbm, kj_ref),
+                (tgw_hbm, tg_ref.at[64:1600]),
             )
         )
     ]
     for copy in fetch:
         copy.start()
-    fetch_low, fetch_hi, fetch_kl, fetch_kh, fetch_tgt, fetch_kj = fetch
+    fetch_low, fetch_kl, fetch_kh, fetch_x3, fetch_ha, fetch_kj, fetch_tgt = fetch
     first = pos_ref[0] == 0
     last = pos_ref[0] == 7
     core = pos_ref[1]
@@ -228,56 +274,12 @@
     put3(l3_ref, 304, s_ref[192:240, :].astype(F32))
     put3(x3_ref, 0, n_ref[0:128, :].astype(F32))
     put3(x3_ref, 1664, s_ref[0:128, :].astype(F32))
+    tg_ref[0:64, :] = n_ref[128:192, :]
+    tg_ref[1600:1664, :] = s_ref[128:192, :]
     zero_at(first, l3_ref, 0, 48)
     zero_at(last, l3_ref, 304, 48)
     zero_at(first, x3_ref, 0, 128)
     zero_at(last, x3_ref, 1664, 128)
-    fetch_low.wait()
-    fetch_kl.wait()
-    fetch_hi.wait()
-    put3(
-        l3_ref,
-        48,
-        widen_low(low_v[...].astype(F32), w_ref[...].astype(F32), e_ref[...].astype(F32)).reshape(256, C),
-    )
-    def widen_rows(t, _):
-        rows = pl.ds(pl.multiple_of(t * 8, 8), 8)
-        wide = widen_hi(hi_v[rows].astype(F32), w_ref[rows].astype(F32), e_ref[rows].astype(F32))
-        put3(x3_ref, pl.multiple_of(128 + t * 256, 128), wide.reshape(256, C))
-        return 0
-
-    lax.fori_loop(0, 6, widen_rows, 0, unroll=True)
-    la_ref[...] = jnp.maximum(
-        jnp.dot(window(l3_ref, 0, 320, LWW), kl_ref[...], preferred_element_type=F32), 0.0
-    ).astype(BF16)
-    zero_at(first, la_ref, 0, 32)
-    zero_at(last, la_ref, 288, 32)
-    fetch_tgt.wait()
-    fetch_kh.wait()
-    tg_ref[0:64, :] = n_ref[128:192, :]
-    tg_ref[1600:1664, :] = s_ref[128:192, :]
-    def widen_targets(t, _):
-        rows = pl.ds(pl.multiple_of(t * 8, 8), 8)
-        wide = widen_tgt(tgt_v[rows].astype(F32), w_ref[rows].astype(F32), e_ref[rows].astype(F32))
-        tg_ref[pl.ds(pl.multiple_of(64 + t * 256, 64), 256), :] = wide.reshape(256, C).astype(BF16)
-        return 0
-
-    lax.fori_loop(0, 6, widen_targets, 0, unroll=True)
-    def high(b, _):
-        s = pl.multiple_of(b * 576, 64)
-        act = jnp.maximum(
-            jnp.dot(window(x3_ref, s, 576, WW), kh_ref[...], preferred_element_type=F32), 0.0
-        ).astype(BF16)
-        ha_ref[pl.ds(s, 576), :] = act
-        cells = la_ref[pl.ds(pl.multiple_of(b * 96, 32), 128), :]
-        lift = jnp.dot(up_ref[...], cells, preferred_element_type=F32) * NINTH
-        put3(j3_ref, s, act.astype(F32) + lift)
-        return 0
-
-    lax.fori_loop(0, 3, high, 0, unroll=True)
-    zero_at(first, j3_ref, 0, 96)
-    zero_at(last, j3_ref, 51 * WW, 96)
-    fetch_kj.wait()
 
     def weight_of(high_part, low_part):
         return ((high_part * 32.0 + low_part) * SCALE)[None]
@@ -290,6 +292,38 @@
         land_row(0, (own // 32).astype(F32), wland, eland), land_row(1, (own % 32).astype(F32), wland, eland)
     )
     bot = weight_of(s_ref[240:272, :].astype(F32), s_ref[272:304, :].astype(F32))
+    fetch_low.wait()
+    put3(
+        l3_ref,
+        48,
+        widen_low(low_v[...].astype(F32), w_ref[...].astype(F32), e_ref[...].astype(F32)).reshape(256, C),
+    )
+    fetch_kl.wait()
+    la_ref[...] = jnp.maximum(
+        jnp.dot(window(l3_ref, 0, 320, LWW), kl_ref[...], preferred_element_type=F32), 0.0
+    ).astype(BF16)
+    zero_at(first, la_ref, 0, 32)
+    zero_at(last, la_ref, 288, 32)
+    fetch_kh.wait()
+    fetch_x3.wait()
+    fetch_ha.wait()
+    edges = jnp.concatenate([window(x3_ref, 0, 128, WW), window(x3_ref, 1600, 128, WW)], axis=0)
+    act = jnp.maximum(jnp.dot(edges, kh_ref[...], preferred_element_type=F32), 0.0).astype(BF16)
+    ha_ref[0:128, :] = act[0:128]
+    ha_ref[1600:1728, :] = act[128:256]
+
+    def high(b, _):
+        s = pl.multiple_of(b * 576, 64)
+        cells = la_ref[pl.ds(pl.multiple_of(b * 96, 32), 128), :]
+        lift = jnp.dot(up_ref[...], cells, preferred_element_type=F32) * NINTH
+        put3(j3_ref, s, ha_ref[pl.ds(s, 576), :].astype(F32) + lift)
+        return 0
+
+    lax.fori_loop(0, 3, high, 0, unroll=True)
+    zero_at(first, j3_ref, 0, 96)
+    zero_at(last, j3_ref, 51 * WW, 96)
+    fetch_kj.wait()
+    fetch_tgt.wait()
 
     def join(b, _):
         s = pl.multiple_of(b * 832, 32)
@@ -402,14 +436,13 @@
         ref[...] = rows[g * 72 : (g + 1) * 72].T[0:32]
 
 
-def call(kernel, out, specs, scratch=(), outs=None, name=None, vmem=None):
+def call(kernel, out, specs, scratch=(), outs=None, vmem=None):
     return pl.pallas_call(
         kernel,
         out_shape=tuple(jax.ShapeDtypeStruct(s, d) for s, d in out),
         in_specs=list(specs),
         out_specs=outs or tuple(VMEM for _ in out),
         scratch_shapes=list(scratch),
-        name=name,
         compiler_params=pltpu.CompilerParams(vmem_limit_bytes=vmem) if vmem else None,
     )
 
@@ -422,28 +455,42 @@
 SECOND = ("zh", "zm")
 
 
-def body(hi, low, kh, kl, kj, tgt, land):
+def step(hi, low, kh, kl, kj, tgt, land):
     dma = pltpu.SemaphoreType.DMA
     west, east, edges = call(
         pack_lon,
         [((H, 8, C), BF16)] * 2 + [((2, 7, W, C), BF16)],
         [SMEM] + [HBM] * 3,
         [pltpu.VMEM((2, H, 8, C), BF16), pltpu.VMEM((2, H, 8, C), BF16), pltpu.VMEM((LH, LW, C), BF16), dma((9,))],
-        name="pack_lon",
         vmem=FULL,
     )(land, hi, tgt, low)
     from_e = lax.ppermute(west, LON, ring(32, -1))
     from_w = lax.ppermute(east, LON, ring(32, 1))
-    north, south = call(
-        pack_lat, [((PK, C), BF16)] * 2, [SMEM] + [VMEM] * 3, name="pack_lat", vmem=6 * MIB
-    )(land, edges, from_w, from_e)
+    north, south = call(pack_lat, [((PK, C), BF16)] * 2, [SMEM] + [VMEM] * 3, vmem=6 * MIB)(land, edges, from_w, from_e)
     from_s = lax.ppermute(north, LAT, ring(8, -1))
     from_n = lax.ppermute(south, LAT, ring(8, 1))
     pos = jnp.stack([lax.axis_index(LAT), lax.axis_index("core")]).astype(jnp.int32)
+    weights = [k.reshape(9 * C, C) for k in (kh, kl, kj)]
+    saved = call(
+        inner,
+        [((1536, 768), BF16), ((1472, C), BF16), ((1536, C), BF16)],
+        [HBM] * 2 + [VMEM] * 2 + [HBM],
+        [
+            pltpu.VMEM((1536, 768), BF16),
+            pltpu.VMEM((1472, C), BF16),
+            pltpu.VMEM((1536, C), BF16),
+            pltpu.VMEM((H, W, C), BF16),
+            pltpu.VMEM((H, W, C), BF16),
+            pltpu.VMEM((2304, C), BF16),
+            dma((6,)),
+        ],
+        outs=(HBM,) * 3,
+        vmem=MAIN_LIMIT,
+    )(hi, tgt, from_w, from_e, weights[0])
     keep, send = call(
         main,
         [((3, 16, 72, C), F32), ((3, 16, 72, C), BF16)],
-        [SMEM] * 2 + [HBM] * 3 + [VMEM] * 4 + [HBM] * 3,
+        [SMEM] * 2 + [HBM] + [VMEM] * 4 + [HBM] * 6,
         [
             pltpu.VMEM((1792, 768), BF16),
             pltpu.VMEM((1728, 768), BF16),
@@ -458,45 +505,36 @@
             pltpu.VMEM((3, 2304, C), F32),
             pltpu.VMEM((3, 16, 72, C), BF16),
             pltpu.VMEM((576, 128), BF16),
-            pltpu.VMEM((H, W, C), BF16),
-            pltpu.VMEM((H, W, C), BF16),
             pltpu.VMEM((LH, LW, C), BF16),
             pltpu.VMEM((2304, C), BF16),
             pltpu.VMEM((2304, C), BF16),
             pltpu.VMEM((2304, C), BF16),
             pltpu.VMEM((2304, C), BF16),
-            dma((6,)),
+            dma((7,)),
             dma((3,)),
             dma((3,)),
         ],
         outs=(HBM, HBM),
-        name="main",
         vmem=MAIN_LIMIT,
-    )(pos, land, hi, tgt, low, from_w, from_e, from_n, from_s, *[k.reshape(9 * C, C) for k in (kh, kl, kj)])
+    )(pos, land, low, from_w, from_e, from_n, from_s, *saved, *weights)
     recv = lax.ppermute(send, "core", ring(2, 1))
     (parts,) = call(
-        merge,
-        [((32, 3, 72, 128), BF16)],
-        [HBM, VMEM],
-        [pltpu.VMEM((3, 16, 72, C), F32), dma((6,))],
-        name="merge",
-        vmem=MERGE_LIMIT,
+        merge, [((32, 3, 72, 128), BF16)], [HBM, VMEM], [pltpu.VMEM((3, 16, 72, C), F32), dma((6,))], vmem=MERGE_LIMIT
     )(keep, recv)
     parts = lax.all_to_all(parts, FIRST, 0, 0, tiled=True)
-    (parts,) = call(total, [((4, 56, 128), F32)], [VMEM], name="total", vmem=6 * MIB)(parts)
+    (parts,) = call(total, [((4, 56, 128), F32)], [VMEM], vmem=6 * MIB)(parts)
     parts = lax.all_to_all(parts, SECOND, 0, 0, tiled=True)
-    grads = call(finish, [((32, 72), F32)] * 3, [VMEM], name="finish", vmem=2 * MIB)(parts)
+    grads = call(finish, [((32, 72), F32)] * 3, [VMEM], vmem=2 * MIB)(parts)
     return tuple(g.T for g in grads)
 
 
 def solution(mesh):
     fine = Mesh(mesh.devices.reshape((2,) * 8), LAT + LON)
     tile = P(LAT, LON, None)
-    mapped = jax.shard_map(
-        body,
+    return jax.shard_map(
+        step,
         mesh=fine,
         in_specs=(tile, tile, P(), P(), P(), tile, P(LAT, LON)),
         out_specs=(P(LON, LAT),) * 3,
         check_vma=False,
     )
-    return mapped

time: 101 us -> 98.6 us (0.976)
  waiting for transfers between devices: 12.4 us -> 7.4 us
  Pallas kernels: 25.6 us -> 28.2 us
    ppermute x5, waiting for transfers between devices: 12.4 us -> 7.4 us  [the longest x1 3.89 us: step(): recv = lax.ppermute(send, 'core', ring(2, 1))]
    pallas_call x6 -> x7, Pallas kernels: 25.6 us -> 28.2 us  [the longest x1 16.3 us: step(): call(main, [((3, 16, 72, C), F32), ((3, 16, 72, C), BF16)], [SMEM] * 2 +...]
  transfers between devices with their start and end apart: 5 -> 5, of which waited for: 4 -> 2; matrix products, arithmetic and copies ran while one was open for 0% -> 0% of each run, Pallas kernels for 0% -> 5%
where the time goes in v7:
time: 98.6 us; the launch traced here: 97.2 us
  blocking collectives  48.2 us (49%)
  Pallas kernels  28.2 us (29%)
  starting transfers between devices  11 us (11%)
  waiting for transfers between devices  7.4 us (8%)
  between operations  1.44 us (1%)
    all_to_all x1, blocking collectives, step(): parts = lax.all_to_all(parts, FIRST, 0, 0, tiled=True)  31.3 us
    all_to_all x1, blocking collectives, step(): parts = lax.all_to_all(parts, SECOND, 0, 0, tiled=True)  16.9 us
    pallas_call x1, Pallas kernels, step(): call(main, [((3, 16, 72, C), F32), ((3, 16, 72, C), BF16)], [SMEM] * 2 +...  16.3 us
    ppermute x1, starting transfers between devices, step(): from_e = lax.ppermute(west, LON, ring(32, -1))  6.3 us
    pallas_call x1, Pallas kernels, step(): call(inner, [((1536, 768), BF16), ((1472, C), BF16), ((1536, C), BF16)],...  5.01 us
    ppermute x1, waiting for transfers between devices, step(): recv = lax.ppermute(send, 'core', ring(2, 1))  3.89 us
    ppermute x1, waiting for transfers between devices, step(): from_w = lax.ppermute(east, LON, ring(32, 1))  3.47 us
    pallas_call x1, Pallas kernels, step(): call(merge, [((32, 3, 72, 128), BF16)], [HBM, VMEM], [pltpu.VMEM((3, 16,...  3.42 us
  transfers between devices with their start and end apart: 5, of which 2 were waited for; matrix products, arithmetic and copies ran while one was open for 0% of the time, Pallas kernels for 5%

profile of v7, /device:TPU:8, one launch (start us, length us, event | category | flops | bytes accessed | tf_op | source)
XLA Modules:
  0.0 97.2 jit_solution(17443619119829057794)
XLA Ops:
  0.6 0.0 copy-start
  1.3 2.2 %shard_map.94 = (bf16[48,8,256]{2,1,0:T(8,128)(2,1)}, bf16[48,8,256]{2,1,0:T(8,128)(2,1)}, bf16[2,7,24,256]{3,2,1,0:T(8,128)(2,1)}) custom-call(s32[1,1]{1,0:T(1,128)S(6)} %copy.10.land_ref, bf16[48,24,256]{2,1,0:T(8,128)(2,1)} %hi_hbm.1, bf16[48,24,256]{2,1,0:T(8,128)(2,1)} %tgt_hbm.1, bf16[16,8,256]{2,1,0:T(8,128)(2,1)} %low_hbm.1), custom_call_target="tpu_custom_call" | custom-call | tf_op jit(solution)/shard_map/pallas_call | solution.py:460
  3.6 0.0 copy-start.1
  3.6 0.1 collective-permute-start
  3.7 6.3 %collective-permute-start.1 = (bf16[48,8,256]{2,1,0:T(8,128)(2,1)}, bf16[48,8,256]{2,1,0:T(8,128)(2,1)S(1)}, u32[]{:S(2)}, u32[]{:S(2)}) collective-permute-start(bf16[48,8,256]{2,1,0:T(8,128)(2,1)} %get-tuple-element.17), channel_id=1, source_target_pairs={{0,31},{1,0},{2,1},{3,2},{4,3},{5,4},{6,5},{7,6},{8,7},{9,8},{10,9... | collective-permute-start | bytes 589832 | tf_op jit(solution)/shard_map/ppermute | solution.py:467
  10.0 3.5 %collective-permute-done.w_ref = bf16[48,8,256]{2,1,0:T(8,128)(2,1)S(1)} collective-permute-done((bf16[48,8,256]{2,1,0:T(8,128)(2,1)}, bf16[48,8,256]{2,1,0:T(8,128)(2,1)S(1)}, u32[]{:S(2)}, u32[]{:S(2)}) %collective-permute-start) | collective-permute-done | bytes 196640 | tf_op jit(solution)/shard_map/ppermute | solution.py:468
  13.5 0.0 collective-permute-done.1.e_ref
  13.5 0.0 copy-start.2
  13.5 0.9 copy-done.2
  14.4 0.1 shard_map.95
  14.5 2.8 %collective-permute-start.2 = (bf16[304,256]{1,0:T(8,128)(2,1)S(1)}, bf16[304,256]{1,0:T(8,128)(2,1)S(1)}, u32[]{:S(2)}, u32[]{:S(2)}) collective-permute-start(bf16[304,256]{1,0:T(8,128)(2,1)S(1)} %get-tuple-element.19), channel_id=1, source_target_pairs={{0,32},{32,64},{64,96},{96,128},{128,160},{160,192},{192,224},{224... | collective-permute-start | bytes 466952 | tf_op jit(solution)/shard_map/ppermute | solution.py:471
  17.3 1.7 %collective-permute-start.3 = (bf16[304,256]{1,0:T(8,128)(2,1)S(1)}, bf16[304,256]{1,0:T(8,128)(2,1)S(1)}, u32[]{:S(2)}, u32[]{:S(2)}) collective-permute-start(bf16[304,256]{1,0:T(8,128)(2,1)S(1)} %get-tuple-element.20), channel_id=1, source_target_pairs={{0,224},{32,0},{64,32},{96,64},{128,96},{160,128},{192,160},{224,1... | collective-permute-start | bytes 466952 | tf_op jit(solution)/shard_map/ppermute | solution.py:470
  19.0 0.1 pad_add_fusion.pos_ref
  19.1 0.0 copy-done
  19.1 5.0 %shard_map.96 = (bf16[1536,768]{1,0:T(8,128)(2,1)}, bf16[1472,256]{1,0:T(8,128)(2,1)}, bf16[1536,256]{1,0:T(8,128)(2,1)}) custom-call(bf16[48,24,256]{2,1,0:T(8,128)(2,1)S(1)} %copy-done, bf16[48,24,256]{2,1,0:T(8,128)(2,1)} %tgt_hbm.1, bf16[48,8,256]{2,1,0:T(8,128)(2,1)S(1)} %collective-permute-done.w_ref, ...), custom_call_target="tpu_custom_call" | custom-call | tf_op jit(solution)/shard_map/pallas_call | solution.py:474
  24.1 0.0 collective-permute-done.2.n_ref
  24.1 0.0 collective-permute-done.3.s_ref
  24.1 0.0 copy-done.1
  24.1 16.3 %shard_map.97 = (f32[3,16,72,256]{3,2,1,0:T(8,128)}, bf16[3,16,72,256]{3,2,1,0:T(8,128)(2,1)}) custom-call(s32[2]{0:T(128)S(1)} %pad_add_fusion.pos_ref, s32[1,1]{1,0:T(1,128)S(6)} %copy.10.land_ref, bf16[16,8,256]{2,1,0:T(8,128)(2,1)S(1)} %copy-done.1, bf16[48,8,256]{2,1,0:T(8,128)(2,1)S(1)} %collective-permute-done.w_ref, ...), custom_call_target="tpu_custom_call" | custom-call | tf_op jit(solution)/shard_map/pallas_call | solution.py:490
  40.5 0.1 collective-permute-start.4
  40.6 3.9 %collective-permute-done.4.recv_ref = bf16[3,16,72,256]{3,2,1,0:T(8,128)(2,1)S(1)} collective-permute-done((bf16[3,16,72,256]{3,2,1,0:T(8,128)(2,1)}, bf16[3,16,72,256]{3,2,1,0:T(8,128)(2,1)S(1)}, u32[]{:S(2)}, u32[]{:S(2)}) %collective-permute-start.4) | collective-permute-done | bytes 1769504 | tf_op jit(solution)/shard_map/ppermute | solution.py:520
  44.5 3.4 %shard_map.98 = bf16[32,3,72,128]{3,2,1,0:T(8,128)(2,1)S(1)} custom-call(f32[3,16,72,256]{3,2,1,0:T(8,128)} %get-tuple-element.24.keep_hbm, bf16[3,16,72,256]{3,2,1,0:T(8,128)(2,1)S(1)} %collective-permute-done.4.recv_ref), custom_call_target="tpu_custom_call" | custom-call | tf_op jit(solution)/shard_map/pallas_call | solution.py:521
  47.9 31.3 %all_to_all.10.in_ref = bf16[32,3,72,128]{3,2,1,0:T(8,128)(2,1)S(1)} all-to-all(bf16[32,3,72,128]{3,2,1,0:T(8,128)(2,1)S(1)} %shard_map.98), channel_id=1, replica_groups=mesh['yh'=2,'yl'=2,'xh'=2,'zh'=2,'zm'=2,'zl'=2,'xl'=2,'core'=2] {'yh','y..., dimensions={0} | all-to-all | bytes 3538944 | tf_op jit(solution)/shard_map/all_to_all | solution.py:524
  79.2 0.4 shard_map.99
  79.5 16.9 %all_to_all.11.in_ref = f32[4,56,128]{2,1,0:T(8,128)S(1)} all-to-all(f32[4,56,128]{2,1,0:T(8,128)S(1)} %shard_map.99), channel_id=1, replica_groups=mesh['yh'=2,'yl'=2,'xh'=2,'zh'=2,'zm'=2,'zl'=2,'xl'=2,'core'=2] {'zh','zm'}, dimensions={0} | all-to-all | bytes 229376 | tf_op jit(solution)/shard_map/all_to_all | solution.py:526
  96.5 0.8 shard_map.100
Async XLA Ops:
  0.6 18.5 %copy-start = (bf16[48,24,256]{2,1,0:T(8,128)(2,1)S(1)}, bf16[48,24,256]{2,1,0:T(8,128)(2,1)}, u32[]{:S(2)}) copy-start(bf16[48,24,256]{2,1,0:T(8,128)(2,1)} %hi_hbm.1) | copy-start | bytes 1769476
  3.6 20.5 %copy-start.1 = (bf16[16,8,256]{2,1,0:T(8,128)(2,1)S(1)}, bf16[16,8,256]{2,1,0:T(8,128)(2,1)}, u32[]{:S(2)}) copy-start(bf16[16,8,256]{2,1,0:T(8,128)(2,1)} %low_hbm.1) | copy-start | bytes 196612
  3.6 9.9 %collective-permute-start = (bf16[48,8,256]{2,1,0:T(8,128)(2,1)}, bf16[48,8,256]{2,1,0:T(8,128)(2,1)S(1)}, u32[]{:S(2)}, u32[]{:S(2)}) collective-permute-start(bf16[48,8,256]{2,1,0:T(8,128)(2,1)} %get-tuple-element.16), channel_id=1, source_target_pairs={{0,1},{1,2},{2,3},{3,4},{4,5},{5,6},{6,7},{7,8},{8,9},{9,10},{10,1... | collective-permute-start | bytes 589832 | tf_op jit(solution)/shard_map/ppermute | solution.py:468
  3.7 9.8 %collective-permute-start.1 = (bf16[48,8,256]{2,1,0:T(8,128)(2,1)}, bf16[48,8,256]{2,1,0:T(8,128)(2,1)S(1)}, u32[]{:S(2)}, u32[]{:S(2)}) collective-permute-start(bf16[48,8,256]{2,1,0:T(8,128)(2,1)} %get-tuple-element.17), channel_id=1, source_target_pairs={{0,31},{1,0},{2,1},{3,2},{4,3},{5,4},{6,5},{7,6},{8,7},{9,8},{10,9... | collective-permute-start | bytes 589832 | tf_op jit(solution)/shard_map/ppermute | solution.py:467
  13.5 0.9 copy-start.2
  14.5 9.6 %collective-permute-start.2 = (bf16[304,256]{1,0:T(8,128)(2,1)S(1)}, bf16[304,256]{1,0:T(8,128)(2,1)S(1)}, u32[]{:S(2)}, u32[]{:S(2)}) collective-permute-start(bf16[304,256]{1,0:T(8,128)(2,1)S(1)} %get-tuple-element.19), channel_id=1, source_target_pairs={{0,32},{32,64},{64,96},{96,128},{128,160},{160,192},{192,224},{224... | collective-permute-start | bytes 466952 | tf_op jit(solution)/shard_map/ppermute | solution.py:471
  17.3 6.8 %collective-permute-start.3 = (bf16[304,256]{1,0:T(8,128)(2,1)S(1)}, bf16[304,256]{1,0:T(8,128)(2,1)S(1)}, u32[]{:S(2)}, u32[]{:S(2)}) collective-permute-start(bf16[304,256]{1,0:T(8,128)(2,1)S(1)} %get-tuple-element.20), channel_id=1, source_target_pairs={{0,224},{32,0},{64,32},{96,64},{128,96},{160,128},{192,160},{224,1... | collective-permute-start | bytes 466952 | tf_op jit(solution)/shard_map/ppermute | solution.py:470
  40.5 4.0 %collective-permute-start.4 = (bf16[3,16,72,256]{3,2,1,0:T(8,128)(2,1)}, bf16[3,16,72,256]{3,2,1,0:T(8,128)(2,1)S(1)}, u32[]{:S(2)}, u32[]{:S(2)}) collective-permute-start(bf16[3,16,72,256]{3,2,1,0:T(8,128)(2,1)} %get-tuple-element.25), channel_id=1, source_target_pairs={{0,1},{1,0},{2,3},{3,2},{4,5},{5,4},{6,7},{7,6},{8,9},{9,8},{10,11... | collective-permute-start | bytes 5308424 | tf_op jit(solution)/shard_map/ppermute | solution.py:520

commit v8 on v7

--- a/solution.py
+++ b/solution.py
@@ -16,10 +16,10 @@
 LON = ("zh", "zm", "zl", "xl", "core")
 SCALE = 2.0 / (H * W * H * W)
 NINTH = 1.0 / 9.0
-PK = 304
+PK = 240
 MIB = 1024 * 1024
-FULL = 60 * 1024 * 1024
 MAIN_LIMIT = 64 * MIB - 12_000_000
+LON_LIMIT = 64 * MIB - 11_200_000
 MERGE_LIMIT = 64 * MIB - 15_500_000
 VMEM = pl.BlockSpec(memory_space=pltpu.VMEM)
 SMEM = pl.BlockSpec(memory_space=pltpu.SMEM)
@@ -117,24 +117,26 @@
     return jnp.concatenate([left, right], axis=1)
 
 
-def land_row(part, own, wpk, epk):
+def land_columns(left, own, right):
     col = lax.broadcasted_iota(jnp.int32, (WW, C), 0)
-    left = wpk[part, 6:7, :]
-    right = epk[part, 6:7, :]
-    return jnp.where(col < 4, left, jnp.where(col < 4 + W, own, right))
+    weight = jnp.where(col < 4, left, jnp.where(col < 4 + W, own, right))
+    return (weight * SCALE)[None]
 
 
 def pack_lat(land_ref, own_ref, w_ref, e_ref, north_ref, south_ref):
     land = land_ref[0, 0]
     wpk = w_ref[0:2].astype(F32)
     epk = e_ref[0:2].astype(F32)
-    lands = jnp.concatenate(
-        [
-            land_row(0, (land // 32).astype(F32), wpk, epk),
-            land_row(1, (land % 32).astype(F32), wpk, epk),
-        ],
-        axis=0,
-    ).astype(BF16)
+    area = lax.broadcasted_iota(jnp.int32, (3, LWW, C), 0)
+    col = lax.broadcasted_iota(jnp.int32, (3, LWW, C), 1)
+
+    def lands(part, own):
+        left = wpk[part, 6:7, :][None]
+        right = epk[part, 6:7, :][None]
+        return jnp.where(area == 0, left, jnp.where(area == 1, own, right))
+
+    high_part = lands(0, (land // 32).astype(F32))
+    low_part = lands(1, (land % 32).astype(F32))
     for side, out_ref in enumerate((north_ref, south_ref)):
         def edge(ref, depth):
             start = (H - depth) * side
@@ -144,10 +146,10 @@
         hi = widen_hi(own[0:4], edge(w_ref, 4), edge(e_ref, 4))
         tgt = widen_tgt(own[4:6], edge(w_ref, 2), edge(e_ref, 2))
         low = widen_low(own[6].reshape(3, 8, C), edge(w_ref, 9), edge(e_ref, 9))
+        low = jnp.where(col == 14, high_part, jnp.where(col == 15, low_part, low))
         out_ref[0:128] = hi.reshape(128, C).astype(BF16)
         out_ref[128:192] = tgt.reshape(64, C).astype(BF16)
         out_ref[192:240] = low.reshape(48, C).astype(BF16)
-        out_ref[240:304] = lands
 
 
 def put3(dst, start, v):
@@ -281,17 +283,18 @@
     zero_at(first, x3_ref, 0, 128)
     zero_at(last, x3_ref, 1664, 128)
 
-    def weight_of(high_part, low_part):
-        return ((high_part * 32.0 + low_part) * SCALE)[None]
-
-    own = land_ref[0, 0]
-    wland = w_ref[0:2].astype(F32)
-    eland = e_ref[0:2].astype(F32)
-    top = weight_of(n_ref[240:272, :].astype(F32), n_ref[272:304, :].astype(F32))
-    mid = weight_of(
-        land_row(0, (own // 32).astype(F32), wland, eland), land_row(1, (own % 32).astype(F32), wland, eland)
-    )
-    bot = weight_of(s_ref[240:272, :].astype(F32), s_ref[272:304, :].astype(F32))
+    def lands_of(ref):
+        rows = ref[192:240, :].astype(F32)
+        pairs = [rows[16 * n + 14 : 16 * n + 16] for n in range(3)]
+        return land_columns(*[pair[0:1] * 32.0 + pair[1:2] for pair in pairs])
+
+    top = lands_of(n_ref)
+    bot = lands_of(s_ref)
+    mid = land_columns(
+        w_ref[0, 6:7, :].astype(F32) * 32.0 + w_ref[1, 6:7, :].astype(F32),
+        land_ref[0, 0].astype(F32),
+        e_ref[0, 6:7, :].astype(F32) * 32.0 + e_ref[1, 6:7, :].astype(F32),
+    )
     fetch_low.wait()
     put3(
         l3_ref,
@@ -369,17 +372,6 @@
         pltpu.make_async_copy(sent_ref.at[n], send_hbm.at[n], send_sem.at[n]).wait()
 
 
-def regroup_lanes(parts, rows):
-    quarter = lax.broadcasted_iota(jnp.int32, (rows, 128), 1) // 32
-    for q in range(4):
-        out = None
-        for g in range(4):
-            shift = ((g - q) * 32) % 128
-            turned = pltpu.roll(parts[g], shift, 1) if shift else parts[g]
-            out = turned if out is None else jnp.where(quarter == g, turned, out)
-        yield q, out
-
-
 def merge(keep_hbm, recv_ref, out_ref, keep_ref, sem):
     copies = [
         pltpu.make_async_copy(keep_hbm.at[n, pl.ds(8 * xl, 8)], keep_ref.at[n, pl.ds(8 * xl, 8)], sem.at[2 * n + xl])
@@ -388,33 +380,39 @@
     ]
     for copy in copies:
         copy.start()
+    quarter = lax.broadcasted_iota(jnp.int32, (72, 128), 1) // 32
     for n in range(3):
         for xl in range(2):
             copies[2 * n + xl].wait()
 
             def one(p, _):
-                blocks = []
-                for g in range(4):
-                    at = xl * 8 + 2 * g + p
-                    blocks.append(keep_ref[n, at] + recv_ref[n, at].astype(F32))
                 for h in range(2):
-                    parts = [v[:, h * 128 : (h + 1) * 128] for v in blocks]
-                    for q, out in regroup_lanes(parts, 72):
+                    lanes = slice(h * 128, (h + 1) * 128)
+                    parts = []
+                    for g in range(4):
+                        at = xl * 8 + 2 * g + p
+                        v = keep_ref[n, at, :, lanes] + recv_ref[n, at, :, lanes].astype(F32)
+                        parts.append(pltpu.roll(v, 32 * g, 1) if g else v)
+                    for q in range(4):
+                        out = parts[(3 - q) % 4]
+                        for s in range(3):
+                            out = jnp.where(quarter == s, parts[(s - q) % 4], out)
                         out_ref[(h * 4 + q) * 4 + 2 * xl + p, n] = out.astype(BF16)
                 return 0
 
             lax.fori_loop(0, 2, one, 0)
 
 
-def total(in_ref, out_ref):
+def total(pos_ref, in_ref, out_ref):
     quarter = lax.broadcasted_iota(jnp.int32, (56, 128), 1) // 32
+    back = (4 - pos_ref[0] % 4) % 4 * 32
     sums = []
     for n in range(3):
         acc = in_ref[0, n].astype(F32)
         for i in range(1, 32):
             acc = acc + in_ref[i, n].astype(F32)
         sums.append(acc)
-    rows = jnp.concatenate(sums + [jnp.zeros((8, 128), F32)], axis=0)
+    rows = pltpu.roll(jnp.concatenate(sums + [jnp.zeros((8, 128), F32)], axis=0), back, 1)
     for g in range(4):
         out = None
         for s in range(4):
@@ -462,7 +460,7 @@
         [((H, 8, C), BF16)] * 2 + [((2, 7, W, C), BF16)],
         [SMEM] + [HBM] * 3,
         [pltpu.VMEM((2, H, 8, C), BF16), pltpu.VMEM((2, H, 8, C), BF16), pltpu.VMEM((LH, LW, C), BF16), dma((9,))],
-        vmem=FULL,
+        vmem=LON_LIMIT,
     )(land, hi, tgt, low)
     from_e = lax.ppermute(west, LON, ring(32, -1))
     from_w = lax.ppermute(east, LON, ring(32, 1))
@@ -522,7 +520,7 @@
         merge, [((32, 3, 72, 128), BF16)], [HBM, VMEM], [pltpu.VMEM((3, 16, 72, C), F32), dma((6,))], vmem=MERGE_LIMIT
     )(keep, recv)
     parts = lax.all_to_all(parts, FIRST, 0, 0, tiled=True)
-    (parts,) = call(total, [((4, 56, 128), F32)], [VMEM], vmem=6 * MIB)(parts)
+    (parts,) = call(total, [((4, 56, 128), F32)], [SMEM, VMEM], vmem=6 * MIB)(pos, parts)
     parts = lax.all_to_all(parts, SECOND, 0, 0, tiled=True)
     grads = call(finish, [((32, 72), F32)] * 3, [VMEM], vmem=2 * MIB)(parts)
     return tuple(g.T for g in grads)

time: 98.6 us -> 96 us (0.974)
  blocking collectives: 48.2 us -> 46.8 us
    all_to_all x1, blocking collectives: 31.3 us -> 29.8 us  [step(): parts = lax.all_to_all(parts, FIRST, 0, 0, tiled=True)]
where the time goes in v8:
time: 96 us; the launch traced here: 94.6 us
  blocking collectives  46.8 us (49%)
  Pallas kernels  27.3 us (28%)
  starting transfers between devices  11 us (11%)
  waiting for transfers between devices  7.16 us (7%)
  between operations  1.45 us (2%)
    all_to_all x1, blocking collectives, step(): parts = lax.all_to_all(parts, FIRST, 0, 0, tiled=True)  29.8 us
    all_to_all x1, blocking collectives, step(): parts = lax.all_to_all(parts, SECOND, 0, 0, tiled=True)  17 us
    pallas_call x1, Pallas kernels, step(): call(main, [((3, 16, 72, C), F32), ((3, 16, 72, C), BF16)], [SMEM] * 2 +...  16.3 us
    ppermute x1, starting transfers between devices, step(): from_e = lax.ppermute(west, LON, ring(32, -1))  6.3 us
    pallas_call x1, Pallas kernels, step(): call(inner, [((1536, 768), BF16), ((1472, C), BF16), ((1536, C), BF16)],...  5.01 us
    ppermute x1, waiting for transfers between devices, step(): recv = lax.ppermute(send, 'core', ring(2, 1))  3.89 us
    ppermute x1, waiting for transfers between devices, step(): from_w = lax.ppermute(east, LON, ring(32, 1))  3.26 us
    ppermute x1, starting transfers between devices, step(): from_n = lax.ppermute(south, LAT, ring(8, 1))  2.81 us
  transfers between devices with their start and end apart: 5, of which 2 were waited for; matrix products, arithmetic and copies ran while one was open for 0% of the time, Pallas kernels for 5%

profile of v8, /device:TPU:8, one launch (start us, length us, event | category | flops | bytes accessed | tf_op | source)
XLA Modules:
  0.0 94.6 jit_solution(15354860184058706547)
XLA Ops:
  0.6 0.0 copy-start
  1.3 0.0 copy-start.1
  1.4 0.8 copy-done.1
  2.2 1.5 %shard_map.94 = (bf16[48,8,256]{2,1,0:T(8,128)(2,1)S(1)}, bf16[48,8,256]{2,1,0:T(8,128)(2,1)S(1)}, bf16[2,7,24,256]{3,2,1,0:T(8,128)(2,1)S(1)}) custom-call(s32[1,1]{1,0:T(1,128)S(6)} %copy.10.land_ref, bf16[48,24,256]{2,1,0:T(8,128)(2,1)} %hi_hbm.1, bf16[48,24,256]{2,1,0:T(8,128)(2,1)} %tgt_hbm.1, bf16[16,8,256]{2,1,0:T(8,128)(2,1)S(1)} %copy-done.1), custom_call_target="tpu_custom_call" | custom-call | tf_op jit(solution)/shard_map/pallas_call | solution.py:458
  3.7 0.0 copy-start.2
  3.7 0.1 collective-permute-start
  3.8 6.3 %collective-permute-start.1 = (bf16[48,8,256]{2,1,0:T(8,128)(2,1)S(1)}, bf16[48,8,256]{2,1,0:T(8,128)(2,1)S(1)}, u32[]{:S(2)}, u32[]{:S(2)}) collective-permute-start(bf16[48,8,256]{2,1,0:T(8,128)(2,1)S(1)} %get-tuple-element.17), channel_id=1, source_target_pairs={{0,31},{1,0},{2,1},{3,2},{4,3},{5,4},{6,5},{7,6},{8,7},{9,8},{10,9... | collective-permute-start | bytes 589832 | tf_op jit(solution)/shard_map/ppermute | solution.py:465
  10.1 3.3 %collective-permute-done.w_ref = bf16[48,8,256]{2,1,0:T(8,128)(2,1)S(1)} collective-permute-done((bf16[48,8,256]{2,1,0:T(8,128)(2,1)S(1)}, bf16[48,8,256]{2,1,0:T(8,128)(2,1)S(1)}, u32[]{:S(2)}, u32[]{:S(2)}) %collective-permute-start) | collective-permute-done | bytes 196640 | tf_op jit(solution)/shard_map/ppermute | solution.py:466
  13.4 0.0 collective-permute-done.1.e_ref
  13.4 0.1 shard_map.95
  13.5 2.8 %collective-permute-start.2 = (bf16[240,256]{1,0:T(8,128)(2,1)S(1)}, bf16[240,256]{1,0:T(8,128)(2,1)S(1)}, u32[]{:S(2)}, u32[]{:S(2)}) collective-permute-start(bf16[240,256]{1,0:T(8,128)(2,1)S(1)} %get-tuple-element.19), channel_id=1, source_target_pairs={{0,32},{32,64},{64,96},{96,128},{128,160},{160,192},{192,224},{224... | collective-permute-start | bytes 368648 | tf_op jit(solution)/shard_map/ppermute | solution.py:469
  16.3 1.7 %collective-permute-start.3 = (bf16[240,256]{1,0:T(8,128)(2,1)S(1)}, bf16[240,256]{1,0:T(8,128)(2,1)S(1)}, u32[]{:S(2)}, u32[]{:S(2)}) collective-permute-start(bf16[240,256]{1,0:T(8,128)(2,1)S(1)} %get-tuple-element.20), channel_id=1, source_target_pairs={{0,224},{32,0},{64,32},{96,64},{128,96},{160,128},{192,160},{224,1... | collective-permute-start | bytes 368648 | tf_op jit(solution)/shard_map/ppermute | solution.py:468
  18.0 0.1 pad_add_fusion.pos_ref
  18.1 0.0 copy-done
  18.1 5.0 %shard_map.96 = (bf16[1536,768]{1,0:T(8,128)(2,1)}, bf16[1472,256]{1,0:T(8,128)(2,1)}, bf16[1536,256]{1,0:T(8,128)(2,1)}) custom-call(bf16[48,24,256]{2,1,0:T(8,128)(2,1)S(1)} %copy-done, bf16[48,24,256]{2,1,0:T(8,128)(2,1)} %tgt_hbm.1, bf16[48,8,256]{2,1,0:T(8,128)(2,1)S(1)} %collective-permute-done.w_ref, ...), custom_call_target="tpu_custom_call" | custom-call | tf_op jit(solution)/shard_map/pallas_call | solution.py:472
  23.1 0.0 collective-permute-done.2.n_ref
  23.1 0.0 collective-permute-done.3.s_ref
  23.1 0.0 copy-done.2
  23.1 16.3 %shard_map.97 = (f32[3,16,72,256]{3,2,1,0:T(8,128)}, bf16[3,16,72,256]{3,2,1,0:T(8,128)(2,1)}) custom-call(s32[2]{0:T(128)S(1)} %pad_add_fusion.pos_ref, s32[1,1]{1,0:T(1,128)S(6)} %copy.10.land_ref, bf16[16,8,256]{2,1,0:T(8,128)(2,1)S(1)} %copy-done.2, bf16[48,8,256]{2,1,0:T(8,128)(2,1)S(1)} %collective-permute-done.w_ref, ...), custom_call_target="tpu_custom_call" | custom-call | tf_op jit(solution)/shard_map/pallas_call | solution.py:488
  39.4 0.1 collective-permute-start.4
  39.5 3.9 %collective-permute-done.4.recv_ref = bf16[3,16,72,256]{3,2,1,0:T(8,128)(2,1)S(1)} collective-permute-done((bf16[3,16,72,256]{3,2,1,0:T(8,128)(2,1)}, bf16[3,16,72,256]{3,2,1,0:T(8,128)(2,1)S(1)}, u32[]{:S(2)}, u32[]{:S(2)}) %collective-permute-start.4) | collective-permute-done | bytes 1769504 | tf_op jit(solution)/shard_map/ppermute | solution.py:518
  43.4 2.6 %shard_map.98 = bf16[32,3,72,128]{3,2,1,0:T(8,128)(2,1)S(1)} custom-call(f32[3,16,72,256]{3,2,1,0:T(8,128)} %get-tuple-element.24.keep_hbm, bf16[3,16,72,256]{3,2,1,0:T(8,128)(2,1)S(1)} %collective-permute-done.4.recv_ref), custom_call_target="tpu_custom_call" | custom-call | tf_op jit(solution)/shard_map/pallas_call | solution.py:519
  46.0 29.8 %all_to_all.10.in_ref = bf16[32,3,72,128]{3,2,1,0:T(8,128)(2,1)S(1)} all-to-all(bf16[32,3,72,128]{3,2,1,0:T(8,128)(2,1)S(1)} %shard_map.98), channel_id=1, replica_groups=mesh['yh'=2,'yl'=2,'xh'=2,'zh'=2,'zm'=2,'zl'=2,'xl'=2,'core'=2] {'yh','y..., dimensions={0} | all-to-all | bytes 3538944 | tf_op jit(solution)/shard_map/all_to_all | solution.py:522
  75.8 1.0 %shard_map.99 = f32[4,56,128]{2,1,0:T(8,128)S(1)} custom-call(s32[2]{0:T(128)S(1)} %pad_add_fusion.pos_ref, bf16[32,3,72,128]{3,2,1,0:T(8,128)(2,1)S(1)} %all_to_all.10.in_ref), custom_call_target="tpu_custom_call" | custom-call | tf_op jit(solution)/shard_map/pallas_call | solution.py:523
  76.8 17.0 %all_to_all.11.in_ref = f32[4,56,128]{2,1,0:T(8,128)S(1)} all-to-all(f32[4,56,128]{2,1,0:T(8,128)S(1)} %shard_map.99), channel_id=1, replica_groups=mesh['yh'=2,'yl'=2,'xh'=2,'zh'=2,'zm'=2,'zl'=2,'xl'=2,'core'=2] {'zh','zm'}, dimensions={0} | all-to-all | bytes 229376 | tf_op jit(solution)/shard_map/all_to_all | solution.py:524
  93.8 0.8 shard_map.100
Async XLA Ops:
  0.6 17.4 %copy-start = (bf16[48,24,256]{2,1,0:T(8,128)(2,1)S(1)}, bf16[48,24,256]{2,1,0:T(8,128)(2,1)}, u32[]{:S(2)}) copy-start(bf16[48,24,256]{2,1,0:T(8,128)(2,1)} %hi_hbm.1) | copy-start | bytes 1769476
  1.3 0.8 copy-start.1
  3.7 19.4 %copy-start.2 = (bf16[16,8,256]{2,1,0:T(8,128)(2,1)S(1)}, bf16[16,8,256]{2,1,0:T(8,128)(2,1)}, u32[]{:S(2)}) copy-start(bf16[16,8,256]{2,1,0:T(8,128)(2,1)} %low_hbm.1) | copy-start | bytes 196612
  3.7 9.7 %collective-permute-start = (bf16[48,8,256]{2,1,0:T(8,128)(2,1)S(1)}, bf16[48,8,256]{2,1,0:T(8,128)(2,1)S(1)}, u32[]{:S(2)}, u32[]{:S(2)}) collective-permute-start(bf16[48,8,256]{2,1,0:T(8,128)(2,1)S(1)} %get-tuple-element.16), channel_id=1, source_target_pairs={{0,1},{1,2},{2,3},{3,4},{4,5},{5,6},{6,7},{7,8},{8,9},{9,10},{10,1... | collective-permute-start | bytes 589832 | tf_op jit(solution)/shard_map/ppermute | solution.py:466
  3.8 9.6 %collective-permute-start.1 = (bf16[48,8,256]{2,1,0:T(8,128)(2,1)S(1)}, bf16[48,8,256]{2,1,0:T(8,128)(2,1)S(1)}, u32[]{:S(2)}, u32[]{:S(2)}) collective-permute-start(bf16[48,8,256]{2,1,0:T(8,128)(2,1)S(1)} %get-tuple-element.17), channel_id=1, source_target_pairs={{0,31},{1,0},{2,1},{3,2},{4,3},{5,4},{6,5},{7,6},{8,7},{9,8},{10,9... | collective-permute-start | bytes 589832 | tf_op jit(solution)/shard_map/ppermute | solution.py:465
  13.5 9.6 %collective-permute-start.2 = (bf16[240,256]{1,0:T(8,128)(2,1)S(1)}, bf16[240,256]{1,0:T(8,128)(2,1)S(1)}, u32[]{:S(2)}, u32[]{:S(2)}) collective-permute-start(bf16[240,256]{1,0:T(8,128)(2,1)S(1)} %get-tuple-element.19), channel_id=1, source_target_pairs={{0,32},{32,64},{64,96},{96,128},{128,160},{160,192},{192,224},{224... | collective-permute-start | bytes 368648 | tf_op jit(solution)/shard_map/ppermute | solution.py:469
  16.3 6.8 %collective-permute-start.3 = (bf16[240,256]{1,0:T(8,128)(2,1)S(1)}, bf16[240,256]{1,0:T(8,128)(2,1)S(1)}, u32[]{:S(2)}, u32[]{:S(2)}) collective-permute-start(bf16[240,256]{1,0:T(8,128)(2,1)S(1)} %get-tuple-element.20), channel_id=1, source_target_pairs={{0,224},{32,0},{64,32},{96,64},{128,96},{160,128},{192,160},{224,1... | collective-permute-start | bytes 368648 | tf_op jit(solution)/shard_map/ppermute | solution.py:468
  39.4 4.0 %collective-permute-start.4 = (bf16[3,16,72,256]{3,2,1,0:T(8,128)(2,1)}, bf16[3,16,72,256]{3,2,1,0:T(8,128)(2,1)S(1)}, u32[]{:S(2)}, u32[]{:S(2)}) collective-permute-start(bf16[3,16,72,256]{3,2,1,0:T(8,128)(2,1)} %get-tuple-element.25), channel_id=1, source_target_pairs={{0,1},{1,0},{2,3},{3,2},{4,5},{5,4},{6,7},{7,6},{8,9},{9,8},{10,11... | collective-permute-start | bytes 5308424 | tf_op jit(solution)/shard_map/ppermute | solution.py:518

commit v9 on v8

--- a/solution.py
+++ b/solution.py
@@ -177,13 +177,11 @@
 
 
 def contract(x_ref, g_val, base, stride, rows, out):
+    turned = g_val.T
     for d in range(3):
-        out[d * 768 : (d + 1) * 768, :] = lax.dot_general(
-            x_ref[base + d * stride : base + d * stride + rows, :],
-            g_val,
-            (((0,), (0,)), ((), ())),
-            preferred_element_type=F32,
-        )
+        out[d * 768 : (d + 1) * 768, :] = jnp.dot(
+            turned, x_ref[base + d * stride : base + d * stride + rows, :], preferred_element_type=F32
+        ).T
 
 
 def block_start(t, half):
@@ -405,22 +403,22 @@
 
 def total(pos_ref, in_ref, out_ref):
     quarter = lax.broadcasted_iota(jnp.int32, (56, 128), 1) // 32
-    back = (4 - pos_ref[0] % 4) % 4 * 32
+    mine = pos_ref[0] % 4
     sums = []
     for n in range(3):
         acc = in_ref[0, n].astype(F32)
         for i in range(1, 32):
             acc = acc + in_ref[i, n].astype(F32)
         sums.append(acc)
-    rows = pltpu.roll(jnp.concatenate(sums + [jnp.zeros((8, 128), F32)], axis=0), back, 1)
-    for g in range(4):
+    rows = jnp.concatenate(sums + [jnp.zeros((8, 128), F32)], axis=0)
+    for at in range(4):
         out = None
         for s in range(4):
-            shift = ((s - g) * 32) % 128
+            shift = ((s - at) * 32) % 128
             part = rows[s * 56 : (s + 1) * 56]
             turned = pltpu.roll(part, shift, 1) if shift else part
             out = turned if out is None else jnp.where(quarter == s, turned, out)
-        out_ref[g] = out
+        out_ref[(at + 4 - mine) % 4] = out
 
 
 def finish(in_ref, a_ref, b_ref, c_ref):

time: 96 us -> 95.5 us (level)
  no operation moved by 1% of the time
where the time goes in v9:
time: 95.5 us; the launch traced here: 94.1 us
  blocking collectives  46.8 us (49%)
  Pallas kernels  26.8 us (28%)
  starting transfers between devices  11 us (12%)
  waiting for transfers between devices  7.16 us (7%)
  between operations  1.45 us (2%)
    all_to_all x1, blocking collectives, step(): parts = lax.all_to_all(parts, FIRST, 0, 0, tiled=True)  29.8 us
    all_to_all x1, blocking collectives, step(): parts = lax.all_to_all(parts, SECOND, 0, 0, tiled=True)  17.1 us
    pallas_call x1, Pallas kernels, step(): call(main, [((3, 16, 72, C), F32), ((3, 16, 72, C), BF16)], [SMEM] * 2 +...  15.9 us
    ppermute x1, starting transfers between devices, step(): from_e = lax.ppermute(west, LON, ring(32, -1))  6.3 us
    pallas_call x1, Pallas kernels, step(): call(inner, [((1536, 768), BF16), ((1472, C), BF16), ((1536, C), BF16)],...  5.01 us
    ppermute x1, waiting for transfers between devices, step(): recv = lax.ppermute(send, 'core', ring(2, 1))  3.89 us
    ppermute x1, waiting for transfers between devices, step(): from_w = lax.ppermute(east, LON, ring(32, 1))  3.26 us
    ppermute x1, starting transfers between devices, step(): from_n = lax.ppermute(south, LAT, ring(8, 1))  2.81 us
  transfers between devices with their start and end apart: 5, of which 2 were waited for; matrix products, arithmetic and copies ran while one was open for 0% of the time, Pallas kernels for 5%

profile of v9, /device:TPU:8, one launch (start us, length us, event | category | flops | bytes accessed | tf_op | source)
XLA Modules:
  0.0 94.1 jit_solution(16576772772585976149)
XLA Ops:
  0.6 0.0 copy-start
  1.3 0.0 copy-start.1
  1.4 0.8 copy-done.1
  2.2 1.5 %shard_map.94 = (bf16[48,8,256]{2,1,0:T(8,128)(2,1)S(1)}, bf16[48,8,256]{2,1,0:T(8,128)(2,1)S(1)}, bf16[2,7,24,256]{3,2,1,0:T(8,128)(2,1)S(1)}) custom-call(s32[1,1]{1,0:T(1,128)S(6)} %copy.10.land_ref, bf16[48,24,256]{2,1,0:T(8,128)(2,1)} %hi_hbm.1, bf16[48,24,256]{2,1,0:T(8,128)(2,1)} %tgt_hbm.1, bf16[16,8,256]{2,1,0:T(8,128)(2,1)S(1)} %copy-done.1), custom_call_target="tpu_custom_call" | custom-call | tf_op jit(solution)/shard_map/pallas_call | solution.py:456
  3.7 0.0 copy-start.2
  3.7 0.1 collective-permute-start
  3.8 6.3 %collective-permute-start.1 = (bf16[48,8,256]{2,1,0:T(8,128)(2,1)S(1)}, bf16[48,8,256]{2,1,0:T(8,128)(2,1)S(1)}, u32[]{:S(2)}, u32[]{:S(2)}) collective-permute-start(bf16[48,8,256]{2,1,0:T(8,128)(2,1)S(1)} %get-tuple-element.17), channel_id=1, source_target_pairs={{0,31},{1,0},{2,1},{3,2},{4,3},{5,4},{6,5},{7,6},{8,7},{9,8},{10,9... | collective-permute-start | bytes 589832 | tf_op jit(solution)/shard_map/ppermute | solution.py:463
  10.1 3.3 %collective-permute-done.w_ref = bf16[48,8,256]{2,1,0:T(8,128)(2,1)S(1)} collective-permute-done((bf16[48,8,256]{2,1,0:T(8,128)(2,1)S(1)}, bf16[48,8,256]{2,1,0:T(8,128)(2,1)S(1)}, u32[]{:S(2)}, u32[]{:S(2)}) %collective-permute-start) | collective-permute-done | bytes 196640 | tf_op jit(solution)/shard_map/ppermute | solution.py:464
  13.4 0.0 collective-permute-done.1.e_ref
  13.4 0.1 shard_map.95
  13.5 2.8 %collective-permute-start.2 = (bf16[240,256]{1,0:T(8,128)(2,1)S(1)}, bf16[240,256]{1,0:T(8,128)(2,1)S(1)}, u32[]{:S(2)}, u32[]{:S(2)}) collective-permute-start(bf16[240,256]{1,0:T(8,128)(2,1)S(1)} %get-tuple-element.19), channel_id=1, source_target_pairs={{0,32},{32,64},{64,96},{96,128},{128,160},{160,192},{192,224},{224... | collective-permute-start | bytes 368648 | tf_op jit(solution)/shard_map/ppermute | solution.py:467
  16.3 1.7 %collective-permute-start.3 = (bf16[240,256]{1,0:T(8,128)(2,1)S(1)}, bf16[240,256]{1,0:T(8,128)(2,1)S(1)}, u32[]{:S(2)}, u32[]{:S(2)}) collective-permute-start(bf16[240,256]{1,0:T(8,128)(2,1)S(1)} %get-tuple-element.20), channel_id=1, source_target_pairs={{0,224},{32,0},{64,32},{96,64},{128,96},{160,128},{192,160},{224,1... | collective-permute-start | bytes 368648 | tf_op jit(solution)/shard_map/ppermute | solution.py:466
  18.0 0.1 pad_add_fusion.pos_ref
  18.1 0.0 copy-done
  18.1 5.0 %shard_map.96 = (bf16[1536,768]{1,0:T(8,128)(2,1)}, bf16[1472,256]{1,0:T(8,128)(2,1)}, bf16[1536,256]{1,0:T(8,128)(2,1)}) custom-call(bf16[48,24,256]{2,1,0:T(8,128)(2,1)S(1)} %copy-done, bf16[48,24,256]{2,1,0:T(8,128)(2,1)} %tgt_hbm.1, bf16[48,8,256]{2,1,0:T(8,128)(2,1)S(1)} %collective-permute-done.w_ref, ...), custom_call_target="tpu_custom_call" | custom-call | tf_op jit(solution)/shard_map/pallas_call | solution.py:470
  23.1 0.0 collective-permute-done.2.n_ref
  23.1 0.0 collective-permute-done.3.s_ref
  23.1 0.0 copy-done.2
  23.1 15.9 %shard_map.97 = (f32[3,16,72,256]{3,2,1,0:T(8,128)}, bf16[3,16,72,256]{3,2,1,0:T(8,128)(2,1)}) custom-call(s32[2]{0:T(128)S(1)} %pad_add_fusion.pos_ref, s32[1,1]{1,0:T(1,128)S(6)} %copy.10.land_ref, bf16[16,8,256]{2,1,0:T(8,128)(2,1)S(1)} %copy-done.2, bf16[48,8,256]{2,1,0:T(8,128)(2,1)S(1)} %collective-permute-done.w_ref, ...), custom_call_target="tpu_custom_call" | custom-call | tf_op jit(solution)/shard_map/pallas_call | solution.py:486
  39.0 0.1 collective-permute-start.4
  39.1 3.9 %collective-permute-done.4.recv_ref = bf16[3,16,72,256]{3,2,1,0:T(8,128)(2,1)S(1)} collective-permute-done((bf16[3,16,72,256]{3,2,1,0:T(8,128)(2,1)}, bf16[3,16,72,256]{3,2,1,0:T(8,128)(2,1)S(1)}, u32[]{:S(2)}, u32[]{:S(2)}) %collective-permute-start.4) | collective-permute-done | bytes 1769504 | tf_op jit(solution)/shard_map/ppermute | solution.py:516
  43.0 2.6 %shard_map.98 = bf16[32,3,72,128]{3,2,1,0:T(8,128)(2,1)S(1)} custom-call(f32[3,16,72,256]{3,2,1,0:T(8,128)} %get-tuple-element.24.keep_hbm, bf16[3,16,72,256]{3,2,1,0:T(8,128)(2,1)S(1)} %collective-permute-done.4.recv_ref), custom_call_target="tpu_custom_call" | custom-call | tf_op jit(solution)/shard_map/pallas_call | solution.py:517
  45.6 29.8 %all_to_all.10.in_ref = bf16[32,3,72,128]{3,2,1,0:T(8,128)(2,1)S(1)} all-to-all(bf16[32,3,72,128]{3,2,1,0:T(8,128)(2,1)S(1)} %shard_map.98), channel_id=1, replica_groups=mesh['yh'=2,'yl'=2,'xh'=2,'zh'=2,'zm'=2,'zl'=2,'xl'=2,'core'=2] {'yh','y..., dimensions={0} | all-to-all | bytes 3538944 | tf_op jit(solution)/shard_map/all_to_all | solution.py:520
  75.4 0.9 shard_map.99
  76.3 17.1 %all_to_all.11.in_ref = f32[4,56,128]{2,1,0:T(8,128)S(1)} all-to-all(f32[4,56,128]{2,1,0:T(8,128)S(1)} %shard_map.99), channel_id=1, replica_groups=mesh['yh'=2,'yl'=2,'xh'=2,'zh'=2,'zm'=2,'zl'=2,'xl'=2,'core'=2] {'zh','zm'}, dimensions={0} | all-to-all | bytes 229376 | tf_op jit(solution)/shard_map/all_to_all | solution.py:522
  93.4 0.8 shard_map.100
Async XLA Ops:
  0.6 17.4 %copy-start = (bf16[48,24,256]{2,1,0:T(8,128)(2,1)S(1)}, bf16[48,24,256]{2,1,0:T(8,128)(2,1)}, u32[]{:S(2)}) copy-start(bf16[48,24,256]{2,1,0:T(8,128)(2,1)} %hi_hbm.1) | copy-start | bytes 1769476
  1.3 0.8 copy-start.1
  3.7 19.4 %copy-start.2 = (bf16[16,8,256]{2,1,0:T(8,128)(2,1)S(1)}, bf16[16,8,256]{2,1,0:T(8,128)(2,1)}, u32[]{:S(2)}) copy-start(bf16[16,8,256]{2,1,0:T(8,128)(2,1)} %low_hbm.1) | copy-start | bytes 196612
  3.7 9.7 %collective-permute-start = (bf16[48,8,256]{2,1,0:T(8,128)(2,1)S(1)}, bf16[48,8,256]{2,1,0:T(8,128)(2,1)S(1)}, u32[]{:S(2)}, u32[]{:S(2)}) collective-permute-start(bf16[48,8,256]{2,1,0:T(8,128)(2,1)S(1)} %get-tuple-element.16), channel_id=1, source_target_pairs={{0,1},{1,2},{2,3},{3,4},{4,5},{5,6},{6,7},{7,8},{8,9},{9,10},{10,1... | collective-permute-start | bytes 589832 | tf_op jit(solution)/shard_map/ppermute | solution.py:464
  3.8 9.6 %collective-permute-start.1 = (bf16[48,8,256]{2,1,0:T(8,128)(2,1)S(1)}, bf16[48,8,256]{2,1,0:T(8,128)(2,1)S(1)}, u32[]{:S(2)}, u32[]{:S(2)}) collective-permute-start(bf16[48,8,256]{2,1,0:T(8,128)(2,1)S(1)} %get-tuple-element.17), channel_id=1, source_target_pairs={{0,31},{1,0},{2,1},{3,2},{4,3},{5,4},{6,5},{7,6},{8,7},{9,8},{10,9... | collective-permute-start | bytes 589832 | tf_op jit(solution)/shard_map/ppermute | solution.py:463
  13.5 9.6 %collective-permute-start.2 = (bf16[240,256]{1,0:T(8,128)(2,1)S(1)}, bf16[240,256]{1,0:T(8,128)(2,1)S(1)}, u32[]{:S(2)}, u32[]{:S(2)}) collective-permute-start(bf16[240,256]{1,0:T(8,128)(2,1)S(1)} %get-tuple-element.19), channel_id=1, source_target_pairs={{0,32},{32,64},{64,96},{96,128},{128,160},{160,192},{192,224},{224... | collective-permute-start | bytes 368648 | tf_op jit(solution)/shard_map/ppermute | solution.py:467
  16.3 6.8 %collective-permute-start.3 = (bf16[240,256]{1,0:T(8,128)(2,1)S(1)}, bf16[240,256]{1,0:T(8,128)(2,1)S(1)}, u32[]{:S(2)}, u32[]{:S(2)}) collective-permute-start(bf16[240,256]{1,0:T(8,128)(2,1)S(1)} %get-tuple-element.20), channel_id=1, source_target_pairs={{0,224},{32,0},{64,32},{96,64},{128,96},{160,128},{192,160},{224,1... | collective-permute-start | bytes 368648 | tf_op jit(solution)/shard_map/ppermute | solution.py:466
  39.0 4.0 %collective-permute-start.4 = (bf16[3,16,72,256]{3,2,1,0:T(8,128)(2,1)}, bf16[3,16,72,256]{3,2,1,0:T(8,128)(2,1)S(1)}, u32[]{:S(2)}, u32[]{:S(2)}) collective-permute-start(bf16[3,16,72,256]{3,2,1,0:T(8,128)(2,1)} %get-tuple-element.25), channel_id=1, source_target_pairs={{0,1},{1,0},{2,3},{3,2},{4,5},{5,4},{6,7},{7,6},{8,9},{9,8},{10,11... | collective-permute-start | bytes 5308424 | tf_op jit(solution)/shard_map/ppermute | solution.py:516

commit v10 on v9

--- a/solution.py
+++ b/solution.py
@@ -216,7 +216,7 @@
         put3(x3_ref, pl.multiple_of(t * 256, 128), wide.reshape(256, C))
         return 0
 
-    lax.fori_loop(0, 6, widen_rows, 0)
+    lax.fori_loop(0, 6, widen_rows, 0, unroll=True)
     leave[0].start()
     fetch[1].wait()
     fetch[2].wait()
@@ -243,7 +243,7 @@
 
 
 def main(
-    pos_ref, land_ref, low_hbm, w_ref, e_ref, n_ref, s_ref, x3_hbm, ha_hbm, tgw_hbm, kh_hbm, kl_hbm, kj_hbm,
+    land_ref, low_hbm, w_ref, e_ref, n_ref, s_ref, x3_hbm, ha_hbm, tgw_hbm, kh_hbm, kl_hbm, kj_hbm,
     keep_hbm, send_hbm,
     x3_ref, j3_ref, o3_ref, l3_ref, ha_ref, la_ref, og_ref, tg_ref, jg_ref, lg_ref, g_ref, sent_ref, up_ref,
     low_v, kh_ref, kl_ref, kj_ref, kt_ref, sem, keep_sem, send_sem,
@@ -265,9 +265,10 @@
     for copy in fetch:
         copy.start()
     fetch_low, fetch_kl, fetch_kh, fetch_x3, fetch_ha, fetch_kj, fetch_tgt = fetch
-    first = pos_ref[0] == 0
-    last = pos_ref[0] == 7
-    core = pos_ref[1]
+    lat = lax.axis_index(LAT)
+    core = lax.axis_index("core")
+    first = lat == 0
+    last = lat == 7
     up_ref[...] = up_matrix()
 
     put3(l3_ref, 0, n_ref[192:240, :].astype(F32))
@@ -398,12 +399,12 @@
                         out_ref[(h * 4 + q) * 4 + 2 * xl + p, n] = out.astype(BF16)
                 return 0
 
-            lax.fori_loop(0, 2, one, 0)
-
-
-def total(pos_ref, in_ref, out_ref):
+            lax.fori_loop(0, 2, one, 0, unroll=True)
+
+
+def total(in_ref, out_ref):
     quarter = lax.broadcasted_iota(jnp.int32, (56, 128), 1) // 32
-    mine = pos_ref[0] % 4
+    mine = lax.axis_index(LAT) % 4
     sums = []
     for n in range(3):
         acc = in_ref[0, n].astype(F32)
@@ -465,7 +466,6 @@
     north, south = call(pack_lat, [((PK, C), BF16)] * 2, [SMEM] + [VMEM] * 3, vmem=6 * MIB)(land, edges, from_w, from_e)
     from_s = lax.ppermute(north, LAT, ring(8, -1))
     from_n = lax.ppermute(south, LAT, ring(8, 1))
-    pos = jnp.stack([lax.axis_index(LAT), lax.axis_index("core")]).astype(jnp.int32)
     weights = [k.reshape(9 * C, C) for k in (kh, kl, kj)]
     saved = call(
         inner,
@@ -486,7 +486,7 @@
     keep, send = call(
         main,
         [((3, 16, 72, C), F32), ((3, 16, 72, C), BF16)],
-        [SMEM] * 2 + [HBM] + [VMEM] * 4 + [HBM] * 6,
+        [SMEM] + [HBM] + [VMEM] * 4 + [HBM] * 6,
         [
             pltpu.VMEM((1792, 768), BF16),
             pltpu.VMEM((1728, 768), BF16),
@@ -512,13 +512,13 @@
         ],
         outs=(HBM, HBM),
         vmem=MAIN_LIMIT,
-    )(pos, land, low, from_w, from_e, from_n, from_s, *saved, *weights)
+    )(land, low, from_w, from_e, from_n, from_s, *saved, *weights)
     recv = lax.ppermute(send, "core", ring(2, 1))
     (parts,) = call(
         merge, [((32, 3, 72, 128), BF16)], [HBM, VMEM], [pltpu.VMEM((3, 16, 72, C), F32), dma((6,))], vmem=MERGE_LIMIT
     )(keep, recv)
     parts = lax.all_to_all(parts, FIRST, 0, 0, tiled=True)
-    (parts,) = call(total, [((4, 56, 128), F32)], [SMEM, VMEM], vmem=6 * MIB)(pos, parts)
+    (parts,) = call(total, [((4, 56, 128), F32)], [VMEM], vmem=6 * MIB)(parts)
     parts = lax.all_to_all(parts, SECOND, 0, 0, tiled=True)
     grads = call(finish, [((32, 72), F32)] * 3, [VMEM], vmem=2 * MIB)(parts)
     return tuple(g.T for g in grads)

time: 95.5 us -> 94.4 us (0.988)
  Pallas kernels: 26.8 us -> 25.8 us
where the time goes in v10:
time: 94.4 us; the launch traced here: 93 us
  blocking collectives  46.8 us (50%)
  Pallas kernels  25.8 us (27%)
  starting transfers between devices  11 us (12%)
  waiting for transfers between devices  7.16 us (8%)
  between operations  1.44 us (2%)
    all_to_all x1, blocking collectives, step(): parts = lax.all_to_all(parts, FIRST, 0, 0, tiled=True)  29.8 us
    all_to_all x1, blocking collectives, step(): parts = lax.all_to_all(parts, SECOND, 0, 0, tiled=True)  17.1 us
    pallas_call x1, Pallas kernels, step(): call(main, [((3, 16, 72, C), F32), ((3, 16, 72, C), BF16)], [SMEM] + [HBM...  15.8 us
    ppermute x1, starting transfers between devices, step(): from_e = lax.ppermute(west, LON, ring(32, -1))  6.3 us
    pallas_call x1, Pallas kernels, step(): call(inner, [((1536, 768), BF16), ((1472, C), BF16), ((1536, C), BF16)],...  5.07 us
    ppermute x1, waiting for transfers between devices, step(): recv = lax.ppermute(send, 'core', ring(2, 1))  3.89 us
    ppermute x1, waiting for transfers between devices, step(): from_w = lax.ppermute(east, LON, ring(32, 1))  3.26 us
    ppermute x1, starting transfers between devices, step(): from_n = lax.ppermute(south, LAT, ring(8, 1))  2.81 us
  transfers between devices with their start and end apart: 5, of which 2 were waited for; matrix products, arithmetic and copies ran while one was open for 0% of the time, Pallas kernels for 5%

profile of v10, /device:TPU:8, one launch (start us, length us, event | category | flops | bytes accessed | tf_op | source)
XLA Modules:
  0.0 93.0 jit_solution(2256101171355595215)
XLA Ops:
  0.6 0.0 copy-start
  1.3 0.0 copy-start.1
  1.4 0.8 copy-done.1
  2.2 1.5 %shard_map.94 = (bf16[48,8,256]{2,1,0:T(8,128)(2,1)S(1)}, bf16[48,8,256]{2,1,0:T(8,128)(2,1)S(1)}, bf16[2,7,24,256]{3,2,1,0:T(8,128)(2,1)S(1)}) custom-call(s32[1,1]{1,0:T(1,128)S(6)} %copy.10.land_ref, bf16[48,24,256]{2,1,0:T(8,128)(2,1)} %hi_hbm.1, bf16[48,24,256]{2,1,0:T(8,128)(2,1)} %tgt_hbm.1, bf16[16,8,256]{2,1,0:T(8,128)(2,1)S(1)} %copy-done.1), custom_call_target="tpu_custom_call" | custom-call | tf_op jit(solution)/shard_map/pallas_call | solution.py:457
  3.7 0.1 collective-permute-start
  3.8 6.3 %collective-permute-start.1 = (bf16[48,8,256]{2,1,0:T(8,128)(2,1)S(1)}, bf16[48,8,256]{2,1,0:T(8,128)(2,1)S(1)}, u32[]{:S(2)}, u32[]{:S(2)}) collective-permute-start(bf16[48,8,256]{2,1,0:T(8,128)(2,1)S(1)} %get-tuple-element.17), channel_id=1, source_target_pairs={{0,31},{1,0},{2,1},{3,2},{4,3},{5,4},{6,5},{7,6},{8,7},{9,8},{10,9... | collective-permute-start | bytes 589832 | tf_op jit(solution)/shard_map/ppermute | solution.py:464
  10.1 3.3 %collective-permute-done.w_ref = bf16[48,8,256]{2,1,0:T(8,128)(2,1)S(1)} collective-permute-done((bf16[48,8,256]{2,1,0:T(8,128)(2,1)S(1)}, bf16[48,8,256]{2,1,0:T(8,128)(2,1)S(1)}, u32[]{:S(2)}, u32[]{:S(2)}) %collective-permute-start) | collective-permute-done | bytes 196640 | tf_op jit(solution)/shard_map/ppermute | solution.py:465
  13.4 0.0 collective-permute-done.1.e_ref
  13.4 0.1 shard_map.95
  13.5 2.8 %collective-permute-start.2 = (bf16[240,256]{1,0:T(8,128)(2,1)S(1)}, bf16[240,256]{1,0:T(8,128)(2,1)S(1)}, u32[]{:S(2)}, u32[]{:S(2)}) collective-permute-start(bf16[240,256]{1,0:T(8,128)(2,1)S(1)} %get-tuple-element.19), channel_id=1, source_target_pairs={{0,32},{32,64},{64,96},{96,128},{128,160},{160,192},{192,224},{224... | collective-permute-start | bytes 368648 | tf_op jit(solution)/shard_map/ppermute | solution.py:468
  16.3 1.7 %collective-permute-start.3 = (bf16[240,256]{1,0:T(8,128)(2,1)S(1)}, bf16[240,256]{1,0:T(8,128)(2,1)S(1)}, u32[]{:S(2)}, u32[]{:S(2)}) collective-permute-start(bf16[240,256]{1,0:T(8,128)(2,1)S(1)} %get-tuple-element.20), channel_id=1, source_target_pairs={{0,224},{32,0},{64,32},{96,64},{128,96},{160,128},{192,160},{224,1... | collective-permute-start | bytes 368648 | tf_op jit(solution)/shard_map/ppermute | solution.py:467
  18.0 0.0 copy-done
  18.0 5.1 %shard_map.96 = (bf16[1536,768]{1,0:T(8,128)(2,1)}, bf16[1472,256]{1,0:T(8,128)(2,1)}, bf16[1536,256]{1,0:T(8,128)(2,1)}) custom-call(bf16[48,24,256]{2,1,0:T(8,128)(2,1)S(1)} %copy-done, bf16[48,24,256]{2,1,0:T(8,128)(2,1)} %tgt_hbm.1, bf16[48,8,256]{2,1,0:T(8,128)(2,1)S(1)} %collective-permute-done.w_ref, ...), custom_call_target="tpu_custom_call" | custom-call | tf_op jit(solution)/shard_map/pallas_call | solution.py:470
  23.1 0.0 collective-permute-done.2.n_ref
  23.1 0.0 collective-permute-done.3.s_ref
  23.1 15.8 %shard_map.97 = (f32[3,16,72,256]{3,2,1,0:T(8,128)}, bf16[3,16,72,256]{3,2,1,0:T(8,128)(2,1)}) custom-call(s32[1,1]{1,0:T(1,128)S(6)} %copy.10.land_ref, bf16[16,8,256]{2,1,0:T(8,128)(2,1)S(1)} %copy-done.1, bf16[48,8,256]{2,1,0:T(8,128)(2,1)S(1)} %collective-permute-done.w_ref, bf16[48,8,256]{2,1,0:T(8,128)(2,1)S(1)} %collective-permute-done.1.e_ref, ...), custom_call_target="tpu_custom_call" | custom-call | tf_op jit(solution)/shard_map/pallas_call | solution.py:486
  38.9 0.1 collective-permute-start.4
  39.0 3.9 %collective-permute-done.4.recv_ref = bf16[3,16,72,256]{3,2,1,0:T(8,128)(2,1)S(1)} collective-permute-done((bf16[3,16,72,256]{3,2,1,0:T(8,128)(2,1)}, bf16[3,16,72,256]{3,2,1,0:T(8,128)(2,1)S(1)}, u32[]{:S(2)}, u32[]{:S(2)}) %collective-permute-start.4) | collective-permute-done | bytes 1769504 | tf_op jit(solution)/shard_map/ppermute | solution.py:516
  42.9 2.2 %shard_map.98 = bf16[32,3,72,128]{3,2,1,0:T(8,128)(2,1)S(1)} custom-call(f32[3,16,72,256]{3,2,1,0:T(8,128)} %get-tuple-element.24.keep_hbm, bf16[3,16,72,256]{3,2,1,0:T(8,128)(2,1)S(1)} %collective-permute-done.4.recv_ref), custom_call_target="tpu_custom_call" | custom-call | tf_op jit(solution)/shard_map/pallas_call | solution.py:517
  45.1 29.8 %all_to_all.10.in_ref = bf16[32,3,72,128]{3,2,1,0:T(8,128)(2,1)S(1)} all-to-all(bf16[32,3,72,128]{3,2,1,0:T(8,128)(2,1)S(1)} %shard_map.98), channel_id=1, replica_groups=mesh['yh'=2,'yl'=2,'xh'=2,'zh'=2,'zm'=2,'zl'=2,'xl'=2,'core'=2] {'yh','y..., dimensions={0} | all-to-all | bytes 3538944 | tf_op jit(solution)/shard_map/all_to_all | solution.py:520
  74.8 0.4 shard_map.99
  75.2 17.1 %all_to_all.11.in_ref = f32[4,56,128]{2,1,0:T(8,128)S(1)} all-to-all(f32[4,56,128]{2,1,0:T(8,128)S(1)} %shard_map.99), channel_id=1, replica_groups=mesh['yh'=2,'yl'=2,'xh'=2,'zh'=2,'zm'=2,'zl'=2,'xl'=2,'core'=2] {'zh','zm'}, dimensions={0} | all-to-all | bytes 229376 | tf_op jit(solution)/shard_map/all_to_all | solution.py:522
  92.3 0.8 shard_map.100
Async XLA Ops:
  0.6 17.3 %copy-start = (bf16[48,24,256]{2,1,0:T(8,128)(2,1)S(1)}, bf16[48,24,256]{2,1,0:T(8,128)(2,1)}, u32[]{:S(2)}) copy-start(bf16[48,24,256]{2,1,0:T(8,128)(2,1)} %hi_hbm.1) | copy-start | bytes 1769476
  1.3 0.8 copy-start.1
  3.7 9.7 %collective-permute-start = (bf16[48,8,256]{2,1,0:T(8,128)(2,1)S(1)}, bf16[48,8,256]{2,1,0:T(8,128)(2,1)S(1)}, u32[]{:S(2)}, u32[]{:S(2)}) collective-permute-start(bf16[48,8,256]{2,1,0:T(8,128)(2,1)S(1)} %get-tuple-element.16), channel_id=1, source_target_pairs={{0,1},{1,2},{2,3},{3,4},{4,5},{5,6},{6,7},{7,8},{8,9},{9,10},{10,1... | collective-permute-start | bytes 589832 | tf_op jit(solution)/shard_map/ppermute | solution.py:465
  3.8 9.6 %collective-permute-start.1 = (bf16[48,8,256]{2,1,0:T(8,128)(2,1)S(1)}, bf16[48,8,256]{2,1,0:T(8,128)(2,1)S(1)}, u32[]{:S(2)}, u32[]{:S(2)}) collective-permute-start(bf16[48,8,256]{2,1,0:T(8,128)(2,1)S(1)} %get-tuple-element.17), channel_id=1, source_target_pairs={{0,31},{1,0},{2,1},{3,2},{4,3},{5,4},{6,5},{7,6},{8,7},{9,8},{10,9... | collective-permute-start | bytes 589832 | tf_op jit(solution)/shard_map/ppermute | solution.py:464
  13.5 9.6 %collective-permute-start.2 = (bf16[240,256]{1,0:T(8,128)(2,1)S(1)}, bf16[240,256]{1,0:T(8,128)(2,1)S(1)}, u32[]{:S(2)}, u32[]{:S(2)}) collective-permute-start(bf16[240,256]{1,0:T(8,128)(2,1)S(1)} %get-tuple-element.19), channel_id=1, source_target_pairs={{0,32},{32,64},{64,96},{96,128},{128,160},{160,192},{192,224},{224... | collective-permute-start | bytes 368648 | tf_op jit(solution)/shard_map/ppermute | solution.py:468
  16.3 6.8 %collective-permute-start.3 = (bf16[240,256]{1,0:T(8,128)(2,1)S(1)}, bf16[240,256]{1,0:T(8,128)(2,1)S(1)}, u32[]{:S(2)}, u32[]{:S(2)}) collective-permute-start(bf16[240,256]{1,0:T(8,128)(2,1)S(1)} %get-tuple-element.20), channel_id=1, source_target_pairs={{0,224},{32,0},{64,32},{96,64},{128,96},{160,128},{192,160},{224,1... | collective-permute-start | bytes 368648 | tf_op jit(solution)/shard_map/ppermute | solution.py:467
  38.9 4.0 %collective-permute-start.4 = (bf16[3,16,72,256]{3,2,1,0:T(8,128)(2,1)}, bf16[3,16,72,256]{3,2,1,0:T(8,128)(2,1)S(1)}, u32[]{:S(2)}, u32[]{:S(2)}) collective-permute-start(bf16[3,16,72,256]{3,2,1,0:T(8,128)(2,1)} %get-tuple-element.25), channel_id=1, source_target_pairs={{0,1},{1,0},{2,3},{3,2},{4,5},{5,4},{6,7},{7,6},{8,9},{9,8},{10,11... | collective-permute-start | bytes 5308424 | tf_op jit(solution)/shard_map/ppermute | solution.py:516
